TPU v7x, 32 devices: a whole 2x2x4 slice. The times are simulated.
32 devices in a mesh: batch: 2 (over x), blk: 16 (over z, y, core).
Axes of the slice: x: 2, y: 2, z: 4, core: 2. Of those that a mesh axis runs over, the one named last changes fastest.
Arguments:
- stream: bfloat16 [32768, 1024], P(('batch', 'blk')), parts along dimension 0, may hold values from -6 to 6
- norm_gain: float32 [4, 1024], replicated, may hold values from 0.1 to 1.9
- norm_bias: float32 [4, 1024], replicated, may hold values from -3 to 3
- proj_in: bfloat16 [4, 1024, 512], replicated, may hold values from -0.1875 to 0.1875
- convolution_taps: bfloat16 [4, 3, 512, 512], replicated, may hold values from -0.15625 to 0.15625
- output_projection: bfloat16 [4, 512, 1024], replicated, may hold values from -0.25 to 0.25
Outputs:
- result: bfloat16 [32768, 1024], P(('batch', 'blk')), parts along dimension 0
There are 2 independent parts, one for each index of `batch`. A program takes and returns all parts, laid end to end along the dimension named above; an argument that names none is the same for every part. Nothing has to cross between parts.
All inputs are finite; a program needn't handle non-finite values.
Results may differ from a plain program's by a relative error of at most 0.017.
Values may be sent and summed in bfloat16 or wider, within the bound.
No kernel may reach another device: no remote copies, remote signals or barrier semaphores. Data moves between devices by JAX's collectives and lax.ppermute only.
A program may use at most 64 MiB of HBM per device.

v0:
```python
import jax
import jax.numpy as jnp
from jax import lax
from jax.sharding import PartitionSpec as P

LAYERS = 4
DILATION_START = 512


EPSILON = 1e-05


def passed_along(array, axis, by):
    peers = lax.axis_size(axis)
    return lax.ppermute(array, axis, [(i, (i + by) % peers) for i in range(peers)])


def extended(array, sides, width):
    for axis, dim in sides:
        peers, length = (lax.axis_size(axis), array.shape[dim])
        up = [(i, (i + 1) % peers) for i in range(peers)]
        down = [(j, i) for i, j in up]
        last = lax.slice_in_dim(array, length - width, length, axis=dim)
        leading = lax.slice_in_dim(array, 0, width, axis=dim)
        before = lax.ppermute(last, axis, up)
        after = lax.ppermute(leading, axis, down)
        array = jnp.concatenate([before, array, after], axis=dim)
    return array


def normalize(stream, scales, offsets):
    values = stream.astype(jnp.float32)
    average = jnp.mean(values, axis=1, keepdims=True)
    centred_values = values - average
    variance = jnp.mean(centred_values * centred_values, axis=1, keepdims=True)
    return (centred_values * lax.rsqrt(variance + EPSILON) * scales + offsets).astype(jnp.bfloat16)


def direct_move(block, offset):
    return passed_along(block, "blk", offset)


def gather_distant(narrow, distance):
    earlier = direct_move(narrow, distance)
    after = direct_move(narrow, -distance)
    return (earlier, after)


def body(stream, norm_gain, norm_bias, proj_in, convolution_taps, output_projection):
    shard_rows = stream.shape[0]
    for block_depth in range(LAYERS):
        dilation_factor = DILATION_START * 2**block_depth
        normed = normalize(stream, norm_gain[block_depth], norm_bias[block_depth])
        narrow = jnp.dot(normed, proj_in[block_depth], preferred_element_type=jnp.float32).astype(
            jnp.bfloat16
        )
        kernel = convolution_taps[block_depth]
        middle = jnp.dot(narrow, kernel[1], preferred_element_type=jnp.float32)
        if dilation_factor < shard_rows:
            padded = extended(narrow, (("blk", 0),), dilation_factor)
            convolved = middle + jnp.dot(
                padded[:shard_rows], kernel[0], preferred_element_type=jnp.float32
            )
            convolved = convolved + jnp.dot(
                padded[2 * dilation_factor :], kernel[2], preferred_element_type=jnp.float32
            )
        else:
            earlier, after = gather_distant(narrow, dilation_factor // shard_rows)
            convolved = middle + jnp.dot(earlier, kernel[0], preferred_element_type=jnp.float32)
            convolved = convolved + jnp.dot(after, kernel[2], preferred_element_type=jnp.float32)
        activated = jax.nn.gelu(convolved, approximate=False).astype(jnp.bfloat16)
        update = jnp.dot(
            activated, output_projection[block_depth], preferred_element_type=jnp.float32
        )
        stream = (stream.astype(jnp.float32) + update).astype(jnp.bfloat16)
    return stream


def solution(mesh):
    return jax.shard_map(
        body,
        mesh=mesh,
        in_specs=(P(("batch", "blk"), None), P(), P(), P(), P(), P()),
        out_specs=P(("batch", "blk"), None),
        check_vma=False,
    )
```

profile of v0, /device:TPU:16, one launch (start us, length us, event | category | flops | bytes accessed | tf_op | source)
XLA Modules:
  0.0 210.9 jit_solution(3940178037873406018)
XLA Ops:
  0.0 0.9 fusion.286
  0.9 0.9 fusion.287
  1.8 2.9 %copy.7 = bf16[1024,1024]{0,1:T(8,128)(2,1)S(1)} copy(bf16[1024,1024]{1,0:T(8,128)(2,1)} %param.6) | data formatting | bytes 4194304 | tf_op args[0]
  4.6 0.4 convert_reduce_fusion.3
  5.0 0.6 fusion.20
  5.6 2.7 %fusion.101 = bf16[1024,512]{1,0:T(8,128)(2,1)S(1)} fusion(bf16[1024,1024]{0,1:T(8,128)(2,1)S(1)} %copy.7, f32[1024]{0:T(1024)S(1)} %bitcast.101, f32[1024]{0:T(1024)S(1)} %bitcast.100, f32[1024]{0:T(1024)S(1)} %add_rsqrt_fusion.3, f32[1024]{0:T(1024)S(1)} %broadcast_multiply_fusion.3, bf16[4,1024,512]{2,1,0:T(8,128)(2,1)} %param.9), kind=kOutput, calls=%fused_computation.143 | convolution fusion | flops 1080557568 | bytes 4210688 | tf_op jit(solution)/shard_map/dot_general | solution.py:54
  8.3 0.1 fusion.285
  8.4 0.1 collective-permute-start
  8.5 2.6 %collective-permute-start.1 = (bf16[512,512]{1,0:T(8,128)(2,1)S(1)}, bf16[512,512]{1,0:T(8,128)(2,1)}, u32[]{:S(2)}, u32[]{:S(2)}) collective-permute-start(bf16[512,512]{1,0:T(8,128)(2,1)S(1)} %get-tuple-element.5), channel_id=1, source_target_pairs={{1,0},{2,1},{3,2},{4,3},{5,4},{6,5},{7,6},{8,7},{9,8},{10,9},{11,1... | collective-permute-start | bytes 1572872 | tf_op jit(solution)/shard_map/ppermute | solution.py:26
  11.1 3.1 %fusion.144 = f32[1024,512]{1,0:T(8,128)} fusion(bf16[1024,512]{1,0:T(8,128)(2,1)S(1)} %fusion.101, bf16[4,3,512,512]{3,2,1,0:T(8,128)(2,1)} %param.10), kind=kOutput, calls=%fused_computation.182 | convolution fusion | flops 536870912 | bytes 3670016 | tf_op jit(solution)/shard_map/dot_general | solution.py:58
  14.2 3.9 %collective-permute-done = bf16[512,512]{1,0:T(8,128)(2,1)S(1)} collective-permute-done((bf16[512,512]{1,0:T(8,128)(2,1)S(1)}, bf16[512,512]{1,0:T(8,128)(2,1)S(1)}, u32[]{:S(2)}, u32[]{:S(2)}) %collective-permute-start) | collective-permute-done | bytes 524320 | tf_op jit(solution)/shard_map/ppermute | solution.py:25
  18.1 3.0 %fusion.105 = f32[1024,512]{1,0:T(8,128)} fusion(bf16[1024,512]{1,0:T(8,128)(2,1)S(1)} %fusion.101, bf16[512,512]{1,0:T(8,128)(2,1)S(1)} %collective-permute-done, bf16[4,3,512,512]{3,2,1,0:T(8,128)(2,1)} %param.10), kind=kOutput, calls=%fused_computation.147 | convolution fusion | flops 538968064 | bytes 4194304 | tf_op jit(solution)/shard_map/dot_general | solution.py:61
  21.1 0.0 collective-permute-done.1
  21.1 10.1 %convert_reduce_fusion.2 = (f32[1024]{0:T(1024)S(1)}, bf16[1024,1024]{0,1:T(8,128)(2,1)}) fusion(bf16[4,512,1024]{2,1,0:T(8,128)(2,1)} %param.11, f32[1024,512]{1,0:T(8,128)} %fusion.144, f32[1024,512]{1,0:T(8,128)} %fusion.105, bf16[512,512]{1,0:T(8,128)(2,1)} %collective-permute-done.1, bf16[1024,512]{1,0:T(8,128)(2,1)S(1)} %fusion.101, ...), kind=kOutput, calls=%fused_computation.8 | convolution fusion | flops 1653079040 | bytes 11538432 | tf_op jit(solution)/shard_map/dot_general | solution.py:72
  31.3 0.0 copy-start
  31.3 2.3 %fusion.16 = f32[1024]{0:T(1024)S(1)} fusion(bf16[1024,1024]{0,1:T(8,128)(2,1)} %get-tuple-element.16, f32[1024]{0:T(1024)S(1)} %broadcast_multiply_fusion.2), kind=kLoop, calls=%fused_computation.28 | loop fusion | flops 4193280 | bytes 2105344 | tf_op jit(solution)/shard_map/reduce_sum | solution.py:35
  33.6 0.0 copy-done
  33.6 2.8 %fusion.98 = bf16[1024,512]{1,0:T(8,128)(2,1)S(1)} fusion(bf16[1024,1024]{0,1:T(8,128)(2,1)S(1)} %copy-done, f32[1024]{0:T(1024)S(1)} %bitcast.99, f32[1024]{0:T(1024)S(1)} %bitcast.98, f32[1024]{0:T(1024)S(1)} %add_rsqrt_fusion.2, f32[1024]{0:T(1024)S(1)} %broadcast_multiply_fusion.2, bf16[4,1024,512]{2,1,0:T(8,128)(2,1)} %param.9), kind=kOutput, calls=%fused_computation.142 | convolution fusion | flops 1080557568 | bytes 4210688 | tf_op jit(solution)/shard_map/dot_general | solution.py:54
  36.5 3.8 %collective-permute-start.2 = (bf16[1024,512]{1,0:T(8,128)(2,1)S(1)}, bf16[1024,512]{1,0:T(8,128)(2,1)S(1)}, u32[]{:S(2)}, u32[]{:S(2)}) collective-permute-start(bf16[1024,512]{1,0:T(8,128)(2,1)S(1)} %fusion.98), channel_id=1, source_target_pairs={{0,1},{1,2},{2,3},{3,4},{4,5},{5,6},{6,7},{7,8},{8,9},{9,10},{10,1... | collective-permute-start | bytes 3145736 | tf_op jit(solution)/shard_map/ppermute | solution.py:15
  40.3 0.0 collective-permute-start.3
  40.3 1.7 fusion.139
  42.0 9.7 %collective-permute-done.2 = bf16[1024,512]{1,0:T(8,128)(2,1)S(1)} collective-permute-done((bf16[1024,512]{1,0:T(8,128)(2,1)S(1)}, bf16[1024,512]{1,0:T(8,128)(2,1)S(1)}, u32[]{:S(2)}, u32[]{:S(2)}) %collective-permute-start.2) | collective-permute-done | bytes 1048608 | tf_op jit(solution)/shard_map/ppermute | solution.py:15
  51.7 3.1 %fusion.137 = f32[1024,512]{1,0:T(8,128)} fusion(bf16[1024,512]{1,0:T(8,128)(2,1)S(1)} %collective-permute-done.2, bf16[4,3,512,512]{3,2,1,0:T(8,128)(2,1)} %param.10), kind=kOutput, calls=%fused_computation.176 | convolution fusion | flops 536870912 | bytes 3670016 | tf_op jit(solution)/shard_map/dot_general | solution.py:69
  54.8 0.0 collective-permute-done.3
  54.8 9.8 %convert_reduce_fusion.1 = (f32[1024]{0:T(1024)S(1)}, bf16[1024,1024]{0,1:T(8,128)(2,1)}) fusion(bf16[4,512,1024]{2,1,0:T(8,128)(2,1)} %param.11, f32[1024,512]{1,0:T(8,128)S(1)} %fusion.139, f32[1024,512]{1,0:T(8,128)} %fusion.137, bf16[1024,512]{1,0:T(8,128)(2,1)S(1)} %collective-permute-done.3, bf16[4,3,512,512]{3,2,1,0:T(8,128)(2,1)} %param.10, ...), kind=kOutput, calls=%fused_computation.5 | convolution fusion | flops 1650981888 | bytes 11014144 | tf_op jit(solution)/shard_map/dot_general | solution.py:72
  64.6 0.0 copy-start.1
  64.6 2.3 %fusion.12 = f32[1024]{0:T(1024)S(1)} fusion(bf16[1024,1024]{0,1:T(8,128)(2,1)} %get-tuple-element.18, f32[1024]{0:T(1024)S(1)} %broadcast_multiply_fusion.1), kind=kLoop, calls=%fused_computation.24 | loop fusion | flops 4193280 | bytes 2105344 | tf_op jit(solution)/shard_map/reduce_sum | solution.py:35
  67.0 0.0 copy-done.1
  67.0 2.8 %fusion.95 = bf16[1024,512]{1,0:T(8,128)(2,1)S(1)} fusion(bf16[1024,1024]{0,1:T(8,128)(2,1)S(1)} %copy-done.1, f32[1024]{0:T(1024)S(1)} %bitcast.97, f32[1024]{0:T(1024)S(1)} %bitcast.96, f32[1024]{0:T(1024)S(1)} %add_rsqrt_fusion.1, f32[1024]{0:T(1024)S(1)} %broadcast_multiply_fusion.1, bf16[4,1024,512]{2,1,0:T(8,128)(2,1)} %param.9), kind=kOutput, calls=%fused_computation.141 | convolution fusion | flops 1080557568 | bytes 4210688 | tf_op jit(solution)/shard_map/dot_general | solution.py:54
  69.8 15.6 %collective-permute-start.4 = (bf16[1024,512]{1,0:T(8,128)(2,1)S(1)}, bf16[1024,512]{1,0:T(8,128)(2,1)S(1)}, u32[]{:S(2)}, u32[]{:S(2)}) collective-permute-start(bf16[1024,512]{1,0:T(8,128)(2,1)S(1)} %fusion.95), channel_id=1, source_target_pairs={{0,2},{1,3},{2,4},{3,5},{4,6},{5,7},{6,8},{7,9},{8,10},{9,11},{10,... | collective-permute-start | bytes 3145736 | tf_op jit(solution)/shard_map/ppermute | solution.py:15
  85.5 0.2 collective-permute-start.5
  85.6 1.7 fusion.133
  87.4 41.1 %collective-permute-done.4 = bf16[1024,512]{1,0:T(8,128)(2,1)S(1)} collective-permute-done((bf16[1024,512]{1,0:T(8,128)(2,1)S(1)}, bf16[1024,512]{1,0:T(8,128)(2,1)S(1)}, u32[]{:S(2)}, u32[]{:S(2)}) %collective-permute-start.4) | collective-permute-done | bytes 1048608 | tf_op jit(solution)/shard_map/ppermute | solution.py:15
  128.4 3.1 %fusion.131 = f32[1024,512]{1,0:T(8,128)} fusion(bf16[1024,512]{1,0:T(8,128)(2,1)S(1)} %collective-permute-done.4, bf16[4,3,512,512]{3,2,1,0:T(8,128)(2,1)} %param.10), kind=kOutput, calls=%fused_computation.171 | convolution fusion | flops 536870912 | bytes 3670016 | tf_op jit(solution)/shard_map/dot_general | solution.py:69
  131.5 0.0 collective-permute-done.5
  131.5 9.8 %convert_reduce_fusion = (f32[1024]{0:T(1024)S(1)}, bf16[1024,1024]{0,1:T(8,128)(2,1)}) fusion(bf16[4,512,1024]{2,1,0:T(8,128)(2,1)} %param.11, f32[1024,512]{1,0:T(8,128)S(1)} %fusion.133, f32[1024,512]{1,0:T(8,128)} %fusion.131, bf16[1024,512]{1,0:T(8,128)(2,1)S(1)} %collective-permute-done.5, bf16[4,3,512,512]{3,2,1,0:T(8,128)(2,1)} %param.10, ...), kind=kOutput, calls=%fused_computation.2 | convolution fusion | flops 1650981888 | bytes 11014144 | tf_op jit(solution)/shard_map/dot_general | solution.py:72
  141.4 0.0 copy-start.2
  141.4 2.3 %fusion.8 = f32[1024]{0:T(1024)S(1)} fusion(bf16[1024,1024]{0,1:T(8,128)(2,1)} %get-tuple-element.20, f32[1024]{0:T(1024)S(1)} %broadcast_multiply_fusion), kind=kLoop, calls=%fused_computation.20 | loop fusion | flops 4193280 | bytes 2105344 | tf_op jit(solution)/shard_map/reduce_sum | solution.py:35
  143.7 0.0 copy-done.2
  143.7 2.8 %fusion.92 = bf16[1024,512]{1,0:T(8,128)(2,1)S(1)} fusion(bf16[1024,1024]{0,1:T(8,128)(2,1)S(1)} %copy-done.2, f32[1024]{0:T(1024)S(1)} %bitcast.95, f32[1024]{0:T(1024)S(1)} %bitcast.94, f32[1024]{0:T(1024)S(1)} %add_rsqrt_fusion, f32[1024]{0:T(1024)S(1)} %broadcast_multiply_fusion, bf16[4,1024,512]{2,1,0:T(8,128)(2,1)} %param.9), kind=kOutput, calls=%fused_computation.140 | convolution fusion | flops 1080557568 | bytes 4210688 | tf_op jit(solution)/shard_map/dot_general | solution.py:54
  146.6 2.3 %collective-permute-start.6 = (bf16[1024,512]{1,0:T(8,128)(2,1)S(1)}, bf16[1024,512]{1,0:T(8,128)(2,1)S(1)}, u32[]{:S(2)}, u32[]{:S(2)}) collective-permute-start(bf16[1024,512]{1,0:T(8,128)(2,1)S(1)} %fusion.92), channel_id=1, source_target_pairs={{0,4},{1,5},{2,6},{3,7},{4,8},{5,9},{6,10},{7,11},{8,12},{9,13},{1... | collective-permute-start | bytes 3145736 | tf_op jit(solution)/shard_map/ppermute | solution.py:15
  148.8 0.0 collective-permute-start.7
  148.8 1.7 fusion.127
  150.6 43.6 %collective-permute-done.6 = bf16[1024,512]{1,0:T(8,128)(2,1)S(1)} collective-permute-done((bf16[1024,512]{1,0:T(8,128)(2,1)S(1)}, bf16[1024,512]{1,0:T(8,128)(2,1)S(1)}, u32[]{:S(2)}, u32[]{:S(2)}) %collective-permute-start.6) | collective-permute-done | bytes 1048608 | tf_op jit(solution)/shard_map/ppermute | solution.py:15
  194.2 3.1 %fusion.125 = f32[1024,512]{1,0:T(8,128)} fusion(bf16[1024,512]{1,0:T(8,128)(2,1)S(1)} %collective-permute-done.6, bf16[4,3,512,512]{3,2,1,0:T(8,128)(2,1)} %param.10), kind=kOutput, calls=%fused_computation.166 | convolution fusion | flops 536870912 | bytes 3670016 | tf_op jit(solution)/shard_map/dot_general | solution.py:69
  197.2 0.0 collective-permute-done.7
  197.2 9.8 %fusion.27 = bf16[1024,1024]{0,1:T(8,128)(2,1)} fusion(bf16[1024,1024]{0,1:T(8,128)(2,1)} %get-tuple-element.20, bf16[4,512,1024]{2,1,0:T(8,128)(2,1)} %param.11, f32[1024,512]{1,0:T(8,128)S(1)} %fusion.127, f32[1024,512]{1,0:T(8,128)} %fusion.125, bf16[1024,512]{1,0:T(8,128)(2,1)S(1)} %collective-permute-done.7, bf16[4,3,512,512]{3,2,1,0:T(8,128)(2,1)} %param.10), kind=kOutput, calls=%fused_computation.39 | convolution fusion | flops 1648885760 | bytes 11010048 | tf_op jit(solution)/shard_map/dot_general | solution.py:72
  207.0 3.9 %copy.9 = bf16[1024,1024]{1,0:T(8,128)(2,1)} copy(bf16[1024,1024]{0,1:T(8,128)(2,1)} %fusion.27) | data formatting | bytes 4194304 | tf_op jit(solution)/shard_map/convert_element_type | solution.py:75
  (8 shorter events, 0.0 us)
Async XLA Ops:
  8.4 9.7 %collective-permute-start = (bf16[512,512]{1,0:T(8,128)(2,1)S(1)}, bf16[512,512]{1,0:T(8,128)(2,1)S(1)}, u32[]{:S(2)}, u32[]{:S(2)}) collective-permute-start(bf16[512,512]{1,0:T(8,128)(2,1)S(1)} %get-tuple-element.6), channel_id=1, source_target_pairs={{0,1},{1,2},{2,3},{3,4},{4,5},{5,6},{6,7},{7,8},{8,9},{9,10},{10,1... | collective-permute-start | bytes 1572872 | tf_op jit(solution)/shard_map/ppermute | solution.py:25
  8.5 12.6 %collective-permute-start.1 = (bf16[512,512]{1,0:T(8,128)(2,1)S(1)}, bf16[512,512]{1,0:T(8,128)(2,1)}, u32[]{:S(2)}, u32[]{:S(2)}) collective-permute-start(bf16[512,512]{1,0:T(8,128)(2,1)S(1)} %get-tuple-element.5), channel_id=1, source_target_pairs={{1,0},{2,1},{3,2},{4,3},{5,4},{6,5},{7,6},{8,7},{9,8},{10,9},{11,1... | collective-permute-start | bytes 1572872 | tf_op jit(solution)/shard_map/ppermute | solution.py:26
  31.3 2.4 %copy-start = (bf16[1024,1024]{0,1:T(8,128)(2,1)S(1)}, bf16[1024,1024]{0,1:T(8,128)(2,1)}, u32[]{:S(2)}) copy-start(bf16[1024,1024]{0,1:T(8,128)(2,1)} %get-tuple-element.16) | copy-start | bytes 6291460
  36.5 15.3 %collective-permute-start.2 = (bf16[1024,512]{1,0:T(8,128)(2,1)S(1)}, bf16[1024,512]{1,0:T(8,128)(2,1)S(1)}, u32[]{:S(2)}, u32[]{:S(2)}) collective-permute-start(bf16[1024,512]{1,0:T(8,128)(2,1)S(1)} %fusion.98), channel_id=1, source_target_pairs={{0,1},{1,2},{2,3},{3,4},{4,5},{5,6},{6,7},{7,8},{8,9},{9,10},{10,1... | collective-permute-start | bytes 3145736 | tf_op jit(solution)/shard_map/ppermute | solution.py:15
  40.3 14.5 %collective-permute-start.3 = (bf16[1024,512]{1,0:T(8,128)(2,1)S(1)}, bf16[1024,512]{1,0:T(8,128)(2,1)S(1)}, u32[]{:S(2)}, u32[]{:S(2)}) collective-permute-start(bf16[1024,512]{1,0:T(8,128)(2,1)S(1)} %fusion.98), channel_id=1, source_target_pairs={{0,15},{1,0},{2,1},{3,2},{4,3},{5,4},{6,5},{7,6},{8,7},{9,8},{10,9... | collective-permute-start | bytes 3145736 | tf_op jit(solution)/shard_map/ppermute | solution.py:15
  64.6 2.4 %copy-start.1 = (bf16[1024,1024]{0,1:T(8,128)(2,1)S(1)}, bf16[1024,1024]{0,1:T(8,128)(2,1)}, u32[]{:S(2)}) copy-start(bf16[1024,1024]{0,1:T(8,128)(2,1)} %get-tuple-element.18) | copy-start | bytes 6291460
  69.8 58.6 %collective-permute-start.4 = (bf16[1024,512]{1,0:T(8,128)(2,1)S(1)}, bf16[1024,512]{1,0:T(8,128)(2,1)S(1)}, u32[]{:S(2)}, u32[]{:S(2)}) collective-permute-start(bf16[1024,512]{1,0:T(8,128)(2,1)S(1)} %fusion.95), channel_id=1, source_target_pairs={{0,2},{1,3},{2,4},{3,5},{4,6},{5,7},{6,8},{7,9},{8,10},{9,11},{10,... | collective-permute-start | bytes 3145736 | tf_op jit(solution)/shard_map/ppermute | solution.py:15
  85.5 46.1 %collective-permute-start.5 = (bf16[1024,512]{1,0:T(8,128)(2,1)S(1)}, bf16[1024,512]{1,0:T(8,128)(2,1)S(1)}, u32[]{:S(2)}, u32[]{:S(2)}) collective-permute-start(bf16[1024,512]{1,0:T(8,128)(2,1)S(1)} %fusion.95), channel_id=1, source_target_pairs={{0,14},{1,15},{2,0},{3,1},{4,2},{5,3},{6,4},{7,5},{8,6},{9,7},{10,... | collective-permute-start | bytes 3145736 | tf_op jit(solution)/shard_map/ppermute | solution.py:15
  141.4 2.4 %copy-start.2 = (bf16[1024,1024]{0,1:T(8,128)(2,1)S(1)}, bf16[1024,1024]{0,1:T(8,128)(2,1)}, u32[]{:S(2)}) copy-start(bf16[1024,1024]{0,1:T(8,128)(2,1)} %get-tuple-element.20) | copy-start | bytes 6291460
  146.6 47.6 %collective-permute-start.6 = (bf16[1024,512]{1,0:T(8,128)(2,1)S(1)}, bf16[1024,512]{1,0:T(8,128)(2,1)S(1)}, u32[]{:S(2)}, u32[]{:S(2)}) collective-permute-start(bf16[1024,512]{1,0:T(8,128)(2,1)S(1)} %fusion.92), channel_id=1, source_target_pairs={{0,4},{1,5},{2,6},{3,7},{4,8},{5,9},{6,10},{7,11},{8,12},{9,13},{1... | collective-permute-start | bytes 3145736 | tf_op jit(solution)/shard_map/ppermute | solution.py:15
  148.8 48.4 %collective-permute-start.7 = (bf16[1024,512]{1,0:T(8,128)(2,1)S(1)}, bf16[1024,512]{1,0:T(8,128)(2,1)S(1)}, u32[]{:S(2)}, u32[]{:S(2)}) collective-permute-start(bf16[1024,512]{1,0:T(8,128)(2,1)S(1)} %fusion.92), channel_id=1, source_target_pairs={{0,12},{1,13},{2,14},{3,15},{4,0},{5,1},{6,2},{7,3},{8,4},{9,5},{1... | collective-permute-start | bytes 3145736 | tf_op jit(solution)/shard_map/ppermute | solution.py:15
where the time goes:
time: 212 us; the launch traced here: 211 us
  waiting for transfers between devices  98.3 us (46%)
  matrix products  71.2 us (34%)
  starting transfers between devices  24.6 us (12%)
  local copies, waits for them, and re-layouts  8.64 us (4%)
  other arithmetic  8.05 us (4%)
    ppermute x6, waiting for transfers between devices, passed_along(): lax.ppermute(array, axis, [(i, (i + by) % peers) for i in range(peers)])  94.4 us
    dot_general x4, matrix products, body(): jnp.dot(activated, output_projection[block_depth], preferred_element_type...  39.5 us
    ppermute x6, starting transfers between devices, passed_along(): lax.ppermute(array, axis, [(i, (i + by) % peers) for i in range(peers)])  21.9 us
    dot_general x4, matrix products, body(): jnp.dot(normed, proj_in[block_depth], preferred_element_type=jnp.float32)  11.2 us
    dot_general x3, matrix products, body(): jnp.dot(earlier, kernel[0], preferred_element_type=jnp.float32)  9.19 us
    dot_general x4, matrix products, body(): middle = jnp.dot(narrow, kernel[1], preferred_element_type=jnp.float32)  8.28 us
    reduce_sum x4, other arithmetic, normalize(): variance = jnp.mean(centred_values * centred_values, axis=1, keepdims=True)  7.64 us
  transfers between devices with their start and end apart: 8, of which 4 were waited for; matrix products, arithmetic and copies ran while one was open for 10% of the time, Pallas kernels for 0%

commit v1 on v0

v1 whole, which is shorter than its diff:
```python
import functools

import jax
import jax.numpy as jnp
from jax import lax
from jax.experimental import pallas as pl
from jax.experimental.pallas import tpu as pltpu
from jax.sharding import PartitionSpec as P


DILATION_START = 512
EPSILON = 1e-05
CORES = 2
CHUNKS = 2
TILE = 256


VMEM = pl.BlockSpec(memory_space=pltpu.VMEM)
HBM = pl.BlockSpec(memory_space=pl.ANY)


def gelu(x):
    return 0.5 * x * (1.0 + lax.erf(x * (0.5**0.5)))


def project(x, gain, bias, proj):
    values = x.astype(jnp.float32)
    average = jnp.mean(values, axis=1, keepdims=True)
    centred = values - average
    variance = jnp.mean(centred * centred, axis=1, keepdims=True)
    normed = (centred * lax.rsqrt(variance + EPSILON) * gain + bias).astype(jnp.bfloat16)
    return jnp.dot(normed, proj, preferred_element_type=jnp.float32).astype(jnp.bfloat16)


def advance(x, earlier, middle, after, taps, output):
    convolved = jnp.dot(middle, taps[1], preferred_element_type=jnp.float32)
    convolved = convolved + jnp.dot(earlier, taps[0], preferred_element_type=jnp.float32)
    convolved = convolved + jnp.dot(after, taps[2], preferred_element_type=jnp.float32)
    activated = gelu(convolved).astype(jnp.bfloat16)
    update = jnp.dot(activated, output, preferred_element_type=jnp.float32)
    return (x.astype(jnp.float32) + update).astype(jnp.bfloat16)


def tiles(rows):
    size = min(TILE, rows)
    return [slice(r, r + size) for r in range(0, rows, size)]


def position():
    index = lax.axis_index("blk")
    return index // CORES, index % CORES


def start_all(copies):
    for copy in copies:
        copy.start()


def enter_kernel(chips, width, *refs):
    pieces, (gain, bias, proj_hbm, x_ref, narrow_ref, proj, sem) = refs[:chips], refs[chips:]
    copy = pltpu.make_async_copy(proj_hbm.at[0], proj, sem)
    copy.start()
    chip, _ = position()
    for k in range(chips):
        x_ref[pl.ds(pl.multiple_of((chip ^ k) * width, width), width), :] = pieces[k][...]
    copy.wait()
    for t in tiles(chips * width):
        narrow_ref[t, :] = project(x_ref[t, :], gain[0:1, :], bias[0:1, :], proj[...])


def load_partner(partner, padded, chips, width):
    rows = chips * width
    padded[pl.ds(width, rows), :] = partner[...]
    padded[pl.ds(0, width), :] = partner[pl.ds(rows - width, width), :]
    padded[pl.ds(width + rows, width), :] = partner[pl.ds(0, width), :]


def slot_kernel(chips, width, slots, block, x_in, narrow, partner, gain, bias, taps_hbm, output_hbm, proj_hbm,
                x_ref, narrow_ref, taps, output, proj, padded, earlier, after, sems):
    copies = [
        pltpu.make_async_copy(taps_hbm.at[block], taps, sems.at[0]),
        pltpu.make_async_copy(output_hbm.at[block], output, sems.at[1]),
        pltpu.make_async_copy(proj_hbm.at[block + 1], proj, sems.at[2]),
    ]
    start_all(copies)
    _, core = position()
    load_partner(partner, padded, chips, width)
    part = width // slots
    shift = 2**block
    for c in range(chips):
        for slot in range(slots):
            to = pl.ds(c * width + slot * part, part)
            if slot >= shift:
                earlier[to, :] = narrow[pl.ds(c * width + (slot - shift) * part, part), :]
            else:
                at = (c + core) * width + (slot - shift + slots) * part
                earlier[to, :] = padded[pl.ds(pl.multiple_of(at, part), part), :]
            if slot + shift < slots:
                after[to, :] = narrow[pl.ds(c * width + (slot + shift) * part, part), :]
            else:
                at = (c + core + 1) * width + (slot + shift - slots) * part
                after[to, :] = padded[pl.ds(pl.multiple_of(at, part), part), :]
    for copy in copies:
        copy.wait()
    for t in tiles(chips * width):
        x = advance(x_in[t, :], earlier[t, :], narrow[t, :], after[t, :], taps, output[...])
        x_ref[t, :] = x
        narrow_ref[t, :] = project(
            x, gain[block + 1 : block + 2, :], bias[block + 1 : block + 2, :], proj[...]
        )


def rest_kernel(chips, width, first, layers, x_in, narrow, partner, gain, bias, taps_hbm, output_hbm, proj_hbm, *refs):
    pieces, (taps, output, proj, padded, own, x_ref, sems) = refs[:chips], refs[chips:]
    blocks = range(first, layers)
    rows = chips * width
    copies = {}
    for n, block in enumerate(blocks):
        copies[block] = [
            pltpu.make_async_copy(taps_hbm.at[block], taps.at[n], sems.at[n, 0]),
            pltpu.make_async_copy(output_hbm.at[block], output.at[n], sems.at[n, 1]),
        ]
        if block + 1 < layers:
            copies[block].append(pltpu.make_async_copy(proj_hbm.at[block + 1], proj.at[n], sems.at[n, 2]))
        start_all(copies[block])
    chip, core = position()
    load_partner(partner, padded, chips, width)
    pad = (own.shape[1] - rows) // 2
    for n, block in enumerate(blocks):
        for copy in copies[block]:
            copy.wait()
        for t in tiles(rows):
            size = t.stop - t.start
            if n == 0:
                x = x_in[t, :]
                middle = narrow[t, :]
                earlier = padded[pl.ds(pl.multiple_of(core * width + t.start, width), size), :]
                after = padded[pl.ds(pl.multiple_of((core + 1) * width + t.start, width), size), :]
            else:
                x = x_ref[t, :]
                shift = 2 ** (n - 1) * width
                held = own.at[n - 1]
                middle = held[pl.ds(pad + t.start, size), :]
                earlier = held[pl.ds(pad + t.start - shift, size), :]
                after = held[pl.ds(pad + t.start + shift, size), :]
            x = advance(x, earlier, middle, after, taps.at[n], output[n])
            x_ref[t, :] = x
            if block + 1 < layers:
                own[n, pl.ds(pad + t.start, size), :] = project(
                    x, gain[block + 1 : block + 2, :], bias[block + 1 : block + 2, :], proj[n]
                )
        if block + 1 < layers:
            own[n, pl.ds(0, pad), :] = own[n, pl.ds(rows, pad), :]
            own[n, pl.ds(pad + rows, pad), :] = own[n, pl.ds(pad, pad), :]
    for k in range(chips):
        pieces[k][...] = x_ref[pl.ds(pl.multiple_of((chip ^ k) * width, width), width), :]


def estimate(rows, model, neck, blocks):
    return pl.CostEstimate(
        flops=2 * rows * blocks * (2 * model * neck + 3 * neck * neck),
        bytes_accessed=blocks * 2 * (2 * model * neck + 3 * neck * neck) + 8 * rows * model,
        transcendentals=0,
    )


def chunk_count(chips):
    return max(1, min(CHUNKS, DILATION_START // chips // 16))


def body(stream, norm_gain, norm_bias, proj_in, convolution_taps, output_projection):
    rows, model = stream.shape
    layers, neck = norm_gain.shape[0], proj_in.shape[2]
    peers = lax.axis_size("blk")
    chips = peers // CORES
    slots = rows // DILATION_START
    span = DILATION_START // chips
    chunks = chunk_count(chips)
    part = span // chunks
    width = slots * part
    count = chips * width
    bf16 = jnp.bfloat16
    chip = lax.axis_index("blk") // CORES

    def to_chip(piece, k):
        return lax.ppermute(piece, "blk", [(i, i ^ (k * CORES)) for i in range(peers)])

    def other_core(narrow):
        return lax.ppermute(narrow, "blk", [(i, i ^ 1) for i in range(peers)])

    shape = jax.ShapeDtypeStruct
    enter = pl.pallas_call(
        functools.partial(enter_kernel, chips, width),
        out_shape=(shape((count, model), bf16), shape((count, neck), bf16)),
        in_specs=[VMEM] * chips + [VMEM, VMEM, HBM],
        out_specs=(VMEM, VMEM),
        scratch_shapes=[pltpu.VMEM((model, neck), bf16), pltpu.SemaphoreType.DMA],
        cost_estimate=estimate(count, model, neck, 1),
        name="enter",
    )
    slot_block = pl.pallas_call(
        functools.partial(slot_kernel, chips, width, slots, 0),
        out_shape=(shape((count, model), bf16), shape((count, neck), bf16)),
        in_specs=[VMEM] * 5 + [HBM] * 3,
        out_specs=(VMEM, VMEM),
        scratch_shapes=[
            pltpu.VMEM((3, neck, neck), bf16),
            pltpu.VMEM((neck, model), bf16),
            pltpu.VMEM((model, neck), bf16),
            pltpu.VMEM((count + 2 * width, neck), bf16),
            pltpu.VMEM((count, neck), bf16),
            pltpu.VMEM((count, neck), bf16),
            pltpu.SemaphoreType.DMA((3,)),
        ],
        cost_estimate=estimate(count, model, neck, 1),
        name="slot_block",
    )
    held = layers - 1
    pad = 2 ** (held - 2) * width
    rest = pl.pallas_call(
        functools.partial(rest_kernel, chips, width, 1, layers),
        out_shape=tuple(shape((width, model), bf16) for _ in range(chips)),
        in_specs=[VMEM] * 5 + [HBM] * 3,
        out_specs=tuple(VMEM for _ in range(chips)),
        scratch_shapes=[
            pltpu.VMEM((held, 3, neck, neck), bf16),
            pltpu.VMEM((held, neck, model), bf16),
            pltpu.VMEM((held - 1, model, neck), bf16),
            pltpu.VMEM((count + 2 * width, neck), bf16),
            pltpu.VMEM((held - 1, count + 2 * pad, neck), bf16),
            pltpu.VMEM((count, model), bf16),
            pltpu.SemaphoreType.DMA((held, 3)),
        ],
        cost_estimate=estimate(count, model, neck, held),
        name="rest",
    )

    grid = stream.reshape(slots, chips * chunks, part, model)
    arrived = []
    for j in range(chunks):
        pieces = []
        for k in range(chips):
            piece = lax.dynamic_slice_in_dim(grid, (chip ^ k) * chunks + j, 1, axis=1).reshape(width, model)
            pieces.append(to_chip(piece, k) if k else piece)
        arrived.append(pieces)

    left = []
    for j in range(chunks):
        x, narrow = enter(*arrived[j], norm_gain, norm_bias, proj_in)
        weights = (norm_gain, norm_bias, convolution_taps, output_projection, proj_in)
        x, narrow = slot_block(x, narrow, other_core(narrow), *weights)
        partner = other_core(narrow)
        pieces = rest(x, narrow, partner, *weights)
        left.append([to_chip(piece, k) if k else piece for k, piece in enumerate(pieces)])

    result = jnp.zeros(grid.shape, bf16)
    for j in range(chunks):
        for k in range(chips):
            piece = left[j][k].reshape(slots, 1, part, model)
            result = lax.dynamic_update_slice_in_dim(result, piece, (chip ^ k) * chunks + j, axis=1)
    return result.reshape(rows, model)


def solution(mesh):
    return jax.shard_map(
        body,
        mesh=mesh,
        in_specs=(P(("batch", "blk"), None), P(), P(), P(), P(), P()),
        out_specs=P(("batch", "blk"), None),
        check_vma=False,
    )
```

time: 212 us -> 159 us (0.75)
  matrix products: 71.2 us -> 0 us
  Pallas kernels: 0 us -> 48.8 us
  waiting for transfers between devices: 98.3 us -> 70.5 us
  other arithmetic: 8.05 us -> 0 us
  starting transfers between devices: 24.6 us -> 30.3 us
    dot_general x16 -> x0, matrix products: 71.2 us -> none  [the longest x4 39.5 us: body(): jnp.dot(activated, output_projection[block_depth], preferred_element_type...]
    pallas_call x0 -> x6, Pallas kernels: none -> 48.8 us  [the longest x2 25.1 us: body(): pieces = rest(x, narrow, partner, *weights)]
    ppermute x8 -> x32, waiting for transfers between devices: 98.3 us -> 70.5 us  [the longest x28 70.5 us: to_chip(): lax.ppermute(piece, 'blk', [(i, i ^ k * CORES) for i in range(peers)])]
    reduce_sum x5 -> x0, other arithmetic: 8.01 us -> none  [the longest x4 7.64 us: normalize(): variance = jnp.mean(centred_values * centred_values, axis=1, keepdims=True)]
    ppermute x8 -> x32, starting transfers between devices: 24.6 us -> 30.3 us  [the longest x28 29.6 us: to_chip(): lax.ppermute(piece, 'blk', [(i, i ^ k * CORES) for i in range(peers)])]
    convert_element_type x1 -> x0, local copies, waits for them, and re-layouts: 3.93 us -> none  [body(): stream = (stream.astype(jnp.float32) + update).astype(jnp.bfloat16)]
    unnamed x7 -> x60, local copies, waits for them, and re-layouts: 2.87 us -> 5.6 us
    dynamic_slice x0 -> x1, local copies, waits for them, and re-layouts: none -> 2.53 us  [body(): lax.dynamic_slice_in_dim(grid, (chip ^ k) * chunks + j, 1, axis=1)]
  transfers between devices with their start and end apart: 8 -> 32, of which waited for: 4 -> 18; matrix products, arithmetic and copies ran while one was open for 10% -> 0% of each run, Pallas kernels for 0% -> 28%
where the time goes in v1:
time: 159 us
  waiting for transfers between devices  70.5 us (44%)
  Pallas kernels  48.8 us (31%)
  starting transfers between devices  30.3 us (19%)
  local copies, waits for them, and re-layouts  8.58 us (5%)
    ppermute x28, waiting for transfers between devices, to_chip(): lax.ppermute(piece, 'blk', [(i, i ^ k * CORES) for i in range(peers)])  70.5 us
    ppermute x28, starting transfers between devices, to_chip(): lax.ppermute(piece, 'blk', [(i, i ^ k * CORES) for i in range(peers)])  29.6 us
    pallas_call x2, Pallas kernels, body(): pieces = rest(x, narrow, partner, *weights)  25.1 us
    pallas_call x2, Pallas kernels, body(): x, narrow = slot_block(x, narrow, other_core(narrow), *weights)  14.8 us
    pallas_call x2, Pallas kernels, body(): x, narrow = enter(*arrived[j], norm_gain, norm_bias, proj_in)  8.89 us
    unnamed x60, local copies, waits for them, and re-layouts  5.6 us
  transfers between devices with their start and end apart: 32, of which 18 were waited for; matrix products, arithmetic and copies ran while one was open for 0% of the time, Pallas kernels for 28%

profile of v1, /device:TPU:16, one launch (start us, length us, event | category | flops | bytes accessed | tf_op | source)
XLA Modules:
  0.0 158.6 jit_solution(9939353760204674819)
XLA Ops:
  0.0 2.5 %constant_dynamic-slice_fusion = (bf16[2,1,32,1024]{3,2,1,0:T(8,128)(2,1)S(1)}, bf16[2,1,32,1024]{3,2,1,0:T(8,128)(2,1)S(1)}, bf16[2,1,32,1024]{3,2,1,0:T(8,128)...) fusion(bf16[2,16,32,1024]{3,2,1,0:T(8,128)(2,1)} %bitcast.98, ...), kind=kLoop, calls=%fused_computation.8 | loop fusion | bytes 4194368 | tf_op jit(solution)/shard_map/dynamic_slice | solution.py:243
  2.5 1.5 collective-permute-start
  4.0 1.6 collective-permute-start.1
  6.0 3.9 %collective-permute-start.4 = (bf16[64,1024]{1,0:T(8,128)(2,1)S(1)}, bf16[64,1024]{1,0:T(8,128)(2,1)S(1)}, u32[]{:S(2)}, u32[]{:S(2)}) collective-permute-start(bf16[64,1024]{1,0:T(8,128)(2,1)S(1)} %bitcast.110), channel_id=1, source_target_pairs={{0,10},{1,11},{2,8},{3,9},{4,14},{5,15},{6,12},{7,13},{8,2},{9,3},... | collective-permute-start | bytes 393224 | tf_op jit(solution)/shard_map/ppermute | solution.py:186
  10.4 2.3 %collective-permute-done.1.refs_2_ = bf16[64,1024]{1,0:T(8,128)(2,1)S(1)} collective-permute-done((bf16[64,1024]{1,0:T(8,128)(2,1)S(1)}, bf16[64,1024]{1,0:T(8,128)(2,1)S(1)}, u32[]{:S(2)}, u32[]{:S(2)}) %collective-permute-start.1) | collective-permute-done | bytes 131104 | tf_op jit(solution)/shard_map/ppermute | solution.py:186
  12.7 1.4 collective-permute-done.2.refs_3_
  14.1 2.0 %collective-permute-done.3.refs_4_ = bf16[64,1024]{1,0:T(8,128)(2,1)S(1)} collective-permute-done((bf16[64,1024]{1,0:T(8,128)(2,1)S(1)}, bf16[64,1024]{1,0:T(8,128)(2,1)S(1)}, u32[]{:S(2)}, u32[]{:S(2)}) %collective-permute-start.3) | collective-permute-done | bytes 131104 | tf_op jit(solution)/shard_map/ppermute | solution.py:186
  16.0 8.2 %collective-permute-done.4.refs_5_ = bf16[64,1024]{1,0:T(8,128)(2,1)S(1)} collective-permute-done((bf16[64,1024]{1,0:T(8,128)(2,1)S(1)}, bf16[64,1024]{1,0:T(8,128)(2,1)S(1)}, u32[]{:S(2)}, u32[]{:S(2)}) %collective-permute-start.4) | collective-permute-done | bytes 131104 | tf_op jit(solution)/shard_map/ppermute | solution.py:186
  24.2 5.5 %collective-permute-done.5.refs_6_ = bf16[64,1024]{1,0:T(8,128)(2,1)S(1)} collective-permute-done((bf16[64,1024]{1,0:T(8,128)(2,1)S(1)}, bf16[64,1024]{1,0:T(8,128)(2,1)S(1)}, u32[]{:S(2)}, u32[]{:S(2)}) %collective-permute-start.5) | collective-permute-done | bytes 131104 | tf_op jit(solution)/shard_map/ppermute | solution.py:186
  29.7 2.3 %collective-permute-done.6.refs_7_ = bf16[64,1024]{1,0:T(8,128)(2,1)S(1)} collective-permute-done((bf16[64,1024]{1,0:T(8,128)(2,1)S(1)}, bf16[64,1024]{1,0:T(8,128)(2,1)S(1)}, u32[]{:S(2)}, u32[]{:S(2)}) %collective-permute-start.6) | collective-permute-done | bytes 131104 | tf_op jit(solution)/shard_map/ppermute | solution.py:186
  32.1 0.6 copy-done.28
  32.7 4.4 %enter.2 = (bf16[512,1024]{1,0:T(8,128)(2,1)}, bf16[512,512]{1,0:T(8,128)(2,1)}) custom-call(bf16[64,1024]{1,0:T(8,128)(2,1)} %bitcast.107, bf16[64,1024]{1,0:T(8,128)(2,1)} %copy-done.17, bf16[64,1024]{1,0:T(8,128)(2,1)} %copy-done.19, bf16[64,1024]{1,0:T(8,128)(2,1)} %copy-done.21, bf16[64,1024]{1,0:T(8,128)(2,1)} %copy-done.23, ...), custom_call_target="tpu_custom_call" | custom-call | flops 1879048192 | bytes 7864320 | tf_op jit(solution)/shard_map/enter/pallas_call | solution.py:249
  37.2 0.6 collective-permute-start.16
  37.8 2.9 %collective-permute-start.18 = (bf16[64,1024]{1,0:T(8,128)(2,1)S(1)}, bf16[64,1024]{1,0:T(8,128)(2,1)S(1)}, u32[]{:S(2)}, u32[]{:S(2)}) collective-permute-start(bf16[64,1024]{1,0:T(8,128)(2,1)S(1)} %bitcast.104), channel_id=1, source_target_pairs={{0,6},{1,7},{2,4},{3,5},{4,2},{5,3},{6,0},{7,1},{8,14},{9,15},{10,... | collective-permute-start | bytes 393224 | tf_op jit(solution)/shard_map/ppermute | solution.py:186
  40.8 2.3 %collective-permute-done.16.refs_1_ = bf16[64,1024]{1,0:T(8,128)(2,1)S(1)} collective-permute-done((bf16[64,1024]{1,0:T(8,128)(2,1)S(1)}, bf16[64,1024]{1,0:T(8,128)(2,1)S(1)}, u32[]{:S(2)}, u32[]{:S(2)}) %collective-permute-start.16) | collective-permute-done | bytes 131104 | tf_op jit(solution)/shard_map/ppermute | solution.py:186
  43.1 0.6 collective-permute-start.20
  44.2 3.7 %collective-permute-done.18.refs_3_ = bf16[64,1024]{1,0:T(8,128)(2,1)S(1)} collective-permute-done((bf16[64,1024]{1,0:T(8,128)(2,1)S(1)}, bf16[64,1024]{1,0:T(8,128)(2,1)S(1)}, u32[]{:S(2)}, u32[]{:S(2)}) %collective-permute-start.18) | collective-permute-done | bytes 131104 | tf_op jit(solution)/shard_map/ppermute | solution.py:186
  47.9 1.5 collective-permute-start.22
  49.4 9.2 %collective-permute-done.20.refs_5_ = bf16[64,1024]{1,0:T(8,128)(2,1)S(1)} collective-permute-done((bf16[64,1024]{1,0:T(8,128)(2,1)S(1)}, bf16[64,1024]{1,0:T(8,128)(2,1)S(1)}, u32[]{:S(2)}, u32[]{:S(2)}) %collective-permute-start.20) | collective-permute-done | bytes 131104 | tf_op jit(solution)/shard_map/ppermute | solution.py:186
  58.6 4.8 %collective-permute-done.21.refs_6_ = bf16[64,1024]{1,0:T(8,128)(2,1)S(1)} collective-permute-done((bf16[64,1024]{1,0:T(8,128)(2,1)S(1)}, bf16[64,1024]{1,0:T(8,128)(2,1)S(1)}, u32[]{:S(2)}, u32[]{:S(2)}) %collective-permute-start.21) | collective-permute-done | bytes 131104 | tf_op jit(solution)/shard_map/ppermute | solution.py:186
  63.4 1.8 %collective-permute-done.22.refs_7_ = bf16[64,1024]{1,0:T(8,128)(2,1)S(1)} collective-permute-done((bf16[64,1024]{1,0:T(8,128)(2,1)S(1)}, bf16[64,1024]{1,0:T(8,128)(2,1)S(1)}, u32[]{:S(2)}, u32[]{:S(2)}) %collective-permute-start.22) | collective-permute-done | bytes 131104 | tf_op jit(solution)/shard_map/ppermute | solution.py:186
  65.2 0.6 copy-done.29
  65.8 4.5 %enter.3 = (bf16[512,1024]{1,0:T(8,128)(2,1)}, bf16[512,512]{1,0:T(8,128)(2,1)}) custom-call(bf16[64,1024]{1,0:T(8,128)(2,1)} %bitcast.99, bf16[64,1024]{1,0:T(8,128)(2,1)} %copy-done.16, bf16[64,1024]{1,0:T(8,128)(2,1)} %copy-done.18, bf16[64,1024]{1,0:T(8,128)(2,1)} %copy-done.20, bf16[64,1024]{1,0:T(8,128)(2,1)} %copy-done.22, ...), custom_call_target="tpu_custom_call" | custom-call | flops 1879048192 | bytes 7864320 | tf_op jit(solution)/shard_map/enter/pallas_call | solution.py:249
  70.4 0.8 copy-done.1
  71.2 7.4 %slot_block.2 = (bf16[512,1024]{1,0:T(8,128)(2,1)}, bf16[512,512]{1,0:T(8,128)(2,1)}) custom-call(bf16[512,1024]{1,0:T(8,128)(2,1)} %get-tuple-element.29.x_in, bf16[512,512]{1,0:T(8,128)(2,1)} %get-tuple-element.30.narrow, bf16[512,512]{1,0:T(8,128)(2,1)} %copy-done.1, f32[4,1024]{1,0:T(4,128)} %gain.7, f32[4,1024]{1,0:T(4,128)} %bias.7, ...), custom_call_target="tpu_custom_call" | custom-call | flops 1879048192 | bytes 7864320 | tf_op jit(solution)/shard_map/slot_block/pallas_call | solution.py:251
  78.6 0.6 collective-permute-start.8
  79.2 0.8 copy-done.2
  80.0 7.4 %slot_block.3 = (bf16[512,1024]{1,0:T(8,128)(2,1)}, bf16[512,512]{1,0:T(8,128)(2,1)}) custom-call(bf16[512,1024]{1,0:T(8,128)(2,1)} %get-tuple-element.41.x_in, bf16[512,512]{1,0:T(8,128)(2,1)} %get-tuple-element.42.narrow, bf16[512,512]{1,0:T(8,128)(2,1)} %copy-done.2, f32[4,1024]{1,0:T(4,128)} %gain.7, f32[4,1024]{1,0:T(4,128)} %bias.7, ...), custom_call_target="tpu_custom_call" | custom-call | flops 1879048192 | bytes 7864320 | tf_op jit(solution)/shard_map/slot_block/pallas_call | solution.py:251
  87.5 0.8 copy-done.6
  88.3 12.6 %rest.2 = (bf16[64,1024]{1,0:T(8,128)(2,1)}, bf16[64,1024]{1,0:T(8,128)(2,1)}, bf16[64,1024]{1,0:T(8,128)(2,1)}, bf16[64,1024]{1,0:T(8,128)(2,1)}, bf16[64,1024]...) custom-call(bf16[512,1024]{1,0:T(8,128)(2,1)} %get-tuple-element.31.x_in, ...), custom_call_target="tpu_custom_call" | custom-call | flops 5637144576 | bytes 15204352 | tf_op jit(solution)/shard_map/rest/pallas_call | solution.py:253
  100.9 1.5 collective-permute-start.9
  102.4 2.0 %collective-permute-start.11 = (bf16[64,1024]{1,0:T(8,128)(2,1)}, bf16[64,1024]{1,0:T(8,128)(2,1)S(1)}, u32[]{:S(2)}, u32[]{:S(2)}) collective-permute-start(bf16[64,1024]{1,0:T(8,128)(2,1)} %get-tuple-element.36), channel_id=1, source_target_pairs={{0,6},{1,7},{2,4},{3,5},{4,2},{5,3},{6,0},{7,1},{8,14},{9,15},{10,... | collective-permute-start | bytes 393224 | tf_op jit(solution)/shard_map/ppermute | solution.py:186
  104.9 3.4 %collective-permute-start.13 = (bf16[64,1024]{1,0:T(8,128)(2,1)}, bf16[64,1024]{1,0:T(8,128)(2,1)S(1)}, u32[]{:S(2)}, u32[]{:S(2)}) collective-permute-start(bf16[64,1024]{1,0:T(8,128)(2,1)} %get-tuple-element.38), channel_id=1, source_target_pairs={{0,10},{1,11},{2,8},{3,9},{4,14},{5,15},{6,12},{7,13},{8,2},{9,3},... | collective-permute-start | bytes 393224 | tf_op jit(solution)/shard_map/ppermute | solution.py:186
  108.3 12.4 %rest.3 = (bf16[64,1024]{1,0:T(8,128)(2,1)}, bf16[64,1024]{1,0:T(8,128)(2,1)}, bf16[64,1024]{1,0:T(8,128)(2,1)}, bf16[64,1024]{1,0:T(8,128)(2,1)}, bf16[64,1024]...) custom-call(bf16[512,1024]{1,0:T(8,128)(2,1)} %get-tuple-element.43.x_in, ...), custom_call_target="tpu_custom_call" | custom-call | flops 5637144576 | bytes 15204352 | tf_op jit(solution)/shard_map/rest/pallas_call | solution.py:253
  121.1 0.5 copy-done.4
  121.7 0.6 collective-permute-start.14
  122.4 1.5 collective-permute-start.15
  123.9 1.5 collective-permute-start.25
  125.5 1.9 %collective-permute-start.26 = (bf16[64,1024]{1,0:T(8,128)(2,1)S(1)}, bf16[64,1024]{1,0:T(8,128)(2,1)S(1)}, u32[]{:S(2)}, u32[]{:S(2)}) collective-permute-start(bf16[64,1024]{1,0:T(8,128)(2,1)S(1)} %copy-done.13), channel_id=1, source_target_pairs={{0,4},{1,5},{2,6},{3,7},{4,0},{5,1},{6,2},{7,3},{8,12},{9,13},{10,... | collective-permute-start | bytes 393224 | tf_op jit(solution)/shard_map/ppermute | solution.py:186
  127.7 4.9 %collective-permute-done.14 = bf16[64,1024]{1,0:T(8,128)(2,1)S(1)} collective-permute-done((bf16[64,1024]{1,0:T(8,128)(2,1)S(1)}, bf16[64,1024]{1,0:T(8,128)(2,1)S(1)}, u32[]{:S(2)}, u32[]{:S(2)}) %collective-permute-start.14) | collective-permute-done | bytes 131104 | tf_op jit(solution)/shard_map/ppermute | solution.py:186
  132.6 4.1 %collective-permute-done.15 = bf16[64,1024]{1,0:T(8,128)(2,1)S(1)} collective-permute-done((bf16[64,1024]{1,0:T(8,128)(2,1)S(1)}, bf16[64,1024]{1,0:T(8,128)(2,1)S(1)}, u32[]{:S(2)}, u32[]{:S(2)}) %collective-permute-start.15) | collective-permute-done | bytes 131104 | tf_op jit(solution)/shard_map/ppermute | solution.py:186
  136.8 1.1 collective-permute-start.30
  138.0 1.8 %collective-permute-start.31 = (bf16[64,1024]{1,0:T(8,128)(2,1)S(1)}, bf16[64,1024]{1,0:T(8,128)(2,1)S(1)}, u32[]{:S(2)}, u32[]{:S(2)}) collective-permute-start(bf16[64,1024]{1,0:T(8,128)(2,1)S(1)} %copy-done.7), channel_id=1, source_target_pairs={{0,14},{1,15},{2,12},{3,13},{4,10},{5,11},{6,8},{7,9},{8,6},{9,7},... | collective-permute-start | bytes 393224 | tf_op jit(solution)/shard_map/ppermute | solution.py:186
  139.8 7.8 %collective-permute-done.28 = bf16[64,1024]{1,0:T(8,128)(2,1)S(1)} collective-permute-done((bf16[64,1024]{1,0:T(8,128)(2,1)S(1)}, bf16[64,1024]{1,0:T(8,128)(2,1)S(1)}, u32[]{:S(2)}, u32[]{:S(2)}) %collective-permute-start.28) | collective-permute-done | bytes 131104 | tf_op jit(solution)/shard_map/ppermute | solution.py:186
  147.7 2.8 %collective-permute-done.29 = bf16[64,1024]{1,0:T(8,128)(2,1)S(1)} collective-permute-done((bf16[64,1024]{1,0:T(8,128)(2,1)S(1)}, bf16[64,1024]{1,0:T(8,128)(2,1)S(1)}, u32[]{:S(2)}, u32[]{:S(2)}) %collective-permute-start.29) | collective-permute-done | bytes 131104 | tf_op jit(solution)/shard_map/ppermute | solution.py:186
  150.5 4.8 %collective-permute-done.30 = bf16[64,1024]{1,0:T(8,128)(2,1)S(1)} collective-permute-done((bf16[64,1024]{1,0:T(8,128)(2,1)S(1)}, bf16[64,1024]{1,0:T(8,128)(2,1)S(1)}, u32[]{:S(2)}, u32[]{:S(2)}) %collective-permute-start.30) | collective-permute-done | bytes 131104 | tf_op jit(solution)/shard_map/ppermute | solution.py:186
  155.3 2.0 %collective-permute-done.31 = bf16[64,1024]{1,0:T(8,128)(2,1)S(1)} collective-permute-done((bf16[64,1024]{1,0:T(8,128)(2,1)S(1)}, bf16[64,1024]{1,0:T(8,128)(2,1)S(1)}, u32[]{:S(2)}, u32[]{:S(2)}) %collective-permute-start.31) | collective-permute-done | bytes 131104 | tf_op jit(solution)/shard_map/ppermute | solution.py:186
  157.3 1.3 copy-done
  (100 shorter events, 2.9 us)
Async XLA Ops:
  2.5 7.4 %collective-permute-start = (bf16[64,1024]{1,0:T(8,128)(2,1)S(1)}, bf16[64,1024]{1,0:T(8,128)(2,1)S(1)}, u32[]{:S(2)}, u32[]{:S(2)}) collective-permute-start(bf16[64,1024]{1,0:T(8,128)(2,1)S(1)} %bitcast.114), channel_id=1, source_target_pairs={{0,2},{1,3},{2,0},{3,1},{4,6},{5,7},{6,4},{7,5},{8,10},{9,11},{10,... | collective-permute-start | bytes 393224 | tf_op jit(solution)/shard_map/ppermute | solution.py:186
  4.0 8.6 %collective-permute-start.1 = (bf16[64,1024]{1,0:T(8,128)(2,1)S(1)}, bf16[64,1024]{1,0:T(8,128)(2,1)S(1)}, u32[]{:S(2)}, u32[]{:S(2)}) collective-permute-start(bf16[64,1024]{1,0:T(8,128)(2,1)S(1)} %bitcast.113), channel_id=1, source_target_pairs={{0,4},{1,5},{2,6},{3,7},{4,0},{5,1},{6,2},{7,3},{8,12},{9,13},{10,... | collective-permute-start | bytes 393224 | tf_op jit(solution)/shard_map/ppermute | solution.py:186
  5.6 8.4 %collective-permute-start.2 = (bf16[64,1024]{1,0:T(8,128)(2,1)S(1)}, bf16[64,1024]{1,0:T(8,128)(2,1)S(1)}, u32[]{:S(2)}, u32[]{:S(2)}) collective-permute-start(bf16[64,1024]{1,0:T(8,128)(2,1)S(1)} %bitcast.112), channel_id=1, source_target_pairs={{0,6},{1,7},{2,4},{3,5},{4,2},{5,3},{6,0},{7,1},{8,14},{9,15},{10,... | collective-permute-start | bytes 393224 | tf_op jit(solution)/shard_map/ppermute | solution.py:186
  6.0 10.0 %collective-permute-start.3 = (bf16[64,1024]{1,0:T(8,128)(2,1)S(1)}, bf16[64,1024]{1,0:T(8,128)(2,1)S(1)}, u32[]{:S(2)}, u32[]{:S(2)}) collective-permute-start(bf16[64,1024]{1,0:T(8,128)(2,1)S(1)} %bitcast.111), channel_id=1, source_target_pairs={{0,8},{1,9},{2,10},{3,11},{4,12},{5,13},{6,14},{7,15},{8,0},{9,1},... | collective-permute-start | bytes 393224 | tf_op jit(solution)/shard_map/ppermute | solution.py:186
  6.0 18.2 %collective-permute-start.4 = (bf16[64,1024]{1,0:T(8,128)(2,1)S(1)}, bf16[64,1024]{1,0:T(8,128)(2,1)S(1)}, u32[]{:S(2)}, u32[]{:S(2)}) collective-permute-start(bf16[64,1024]{1,0:T(8,128)(2,1)S(1)} %bitcast.110), channel_id=1, source_target_pairs={{0,10},{1,11},{2,8},{3,9},{4,14},{5,15},{6,12},{7,13},{8,2},{9,3},... | collective-permute-start | bytes 393224 | tf_op jit(solution)/shard_map/ppermute | solution.py:186
  9.9 22.1 %copy-start.17 = (bf16[64,1024]{1,0:T(8,128)(2,1)}, bf16[64,1024]{1,0:T(8,128)(2,1)S(1)}, u32[]{:S(2)}) copy-start(bf16[64,1024]{1,0:T(8,128)(2,1)S(1)} %collective-permute-done.refs_1_) | copy-start | bytes 393220
  9.9 19.8 %collective-permute-start.5 = (bf16[64,1024]{1,0:T(8,128)(2,1)S(1)}, bf16[64,1024]{1,0:T(8,128)(2,1)S(1)}, u32[]{:S(2)}, u32[]{:S(2)}) collective-permute-start(bf16[64,1024]{1,0:T(8,128)(2,1)S(1)} %bitcast.109), channel_id=1, source_target_pairs={{0,12},{1,13},{2,14},{3,15},{4,8},{5,9},{6,10},{7,11},{8,4},{9,5},... | collective-permute-start | bytes 393224 | tf_op jit(solution)/shard_map/ppermute | solution.py:186
  12.7 19.4 %copy-start.19 = (bf16[64,1024]{1,0:T(8,128)(2,1)}, bf16[64,1024]{1,0:T(8,128)(2,1)S(1)}, u32[]{:S(2)}) copy-start(bf16[64,1024]{1,0:T(8,128)(2,1)S(1)} %collective-permute-done.1.refs_2_) | copy-start | bytes 393220
  12.7 19.4 %collective-permute-start.6 = (bf16[64,1024]{1,0:T(8,128)(2,1)S(1)}, bf16[64,1024]{1,0:T(8,128)(2,1)S(1)}, u32[]{:S(2)}, u32[]{:S(2)}) collective-permute-start(bf16[64,1024]{1,0:T(8,128)(2,1)S(1)} %bitcast.108), channel_id=1, source_target_pairs={{0,14},{1,15},{2,12},{3,13},{4,10},{5,11},{6,8},{7,9},{8,6},{9,7},... | collective-permute-start | bytes 393224 | tf_op jit(solution)/shard_map/ppermute | solution.py:186
  14.0 18.0 %copy-start.21 = (bf16[64,1024]{1,0:T(8,128)(2,1)}, bf16[64,1024]{1,0:T(8,128)(2,1)S(1)}, u32[]{:S(2)}) copy-start(bf16[64,1024]{1,0:T(8,128)(2,1)S(1)} %collective-permute-done.2.refs_3_) | copy-start | bytes 393220
  16.0 16.0 %copy-start.23 = (bf16[64,1024]{1,0:T(8,128)(2,1)}, bf16[64,1024]{1,0:T(8,128)(2,1)S(1)}, u32[]{:S(2)}) copy-start(bf16[64,1024]{1,0:T(8,128)(2,1)S(1)} %collective-permute-done.3.refs_4_) | copy-start | bytes 393220
  24.2 7.8 %copy-start.24 = (bf16[64,1024]{1,0:T(8,128)(2,1)}, bf16[64,1024]{1,0:T(8,128)(2,1)S(1)}, u32[]{:S(2)}) copy-start(bf16[64,1024]{1,0:T(8,128)(2,1)S(1)} %collective-permute-done.4.refs_5_) | copy-start | bytes 393220
  37.1 33.3 %collective-permute-start.7 = (bf16[512,512]{1,0:T(8,128)(2,1)}, bf16[512,512]{1,0:T(8,128)(2,1)S(1)}, u32[]{:S(2)}, u32[]{:S(2)}) collective-permute-start(bf16[512,512]{1,0:T(8,128)(2,1)} %get-tuple-element.30.narrow), channel_id=1, source_target_pairs={{0,1},{1,0},{2,3},{3,2},{4,5},{5,4},{6,7},{7,6},{8,9},{9,8},{10,11... | collective-permute-start | bytes 1572872 | tf_op jit(solution)/shard_map/ppermute | solution.py:189
  37.2 5.9 %collective-permute-start.16 = (bf16[64,1024]{1,0:T(8,128)(2,1)S(1)}, bf16[64,1024]{1,0:T(8,128)(2,1)S(1)}, u32[]{:S(2)}, u32[]{:S(2)}) collective-permute-start(bf16[64,1024]{1,0:T(8,128)(2,1)S(1)} %bitcast.106), channel_id=1, source_target_pairs={{0,2},{1,3},{2,0},{3,1},{4,6},{5,7},{6,4},{7,5},{8,10},{9,11},{10,... | collective-permute-start | bytes 393224 | tf_op jit(solution)/shard_map/ppermute | solution.py:186
  37.8 6.4 %collective-permute-start.17 = (bf16[64,1024]{1,0:T(8,128)(2,1)S(1)}, bf16[64,1024]{1,0:T(8,128)(2,1)S(1)}, u32[]{:S(2)}, u32[]{:S(2)}) collective-permute-start(bf16[64,1024]{1,0:T(8,128)(2,1)S(1)} %bitcast.105), channel_id=1, source_target_pairs={{0,4},{1,5},{2,6},{3,7},{4,0},{5,1},{6,2},{7,3},{8,12},{9,13},{10,... | collective-permute-start | bytes 393224 | tf_op jit(solution)/shard_map/ppermute | solution.py:186
  37.8 10.1 %collective-permute-start.18 = (bf16[64,1024]{1,0:T(8,128)(2,1)S(1)}, bf16[64,1024]{1,0:T(8,128)(2,1)S(1)}, u32[]{:S(2)}, u32[]{:S(2)}) collective-permute-start(bf16[64,1024]{1,0:T(8,128)(2,1)S(1)} %bitcast.104), channel_id=1, source_target_pairs={{0,6},{1,7},{2,4},{3,5},{4,2},{5,3},{6,0},{7,1},{8,14},{9,15},{10,... | collective-permute-start | bytes 393224 | tf_op jit(solution)/shard_map/ppermute | solution.py:186
  40.8 8.7 %collective-permute-start.19 = (bf16[64,1024]{1,0:T(8,128)(2,1)S(1)}, bf16[64,1024]{1,0:T(8,128)(2,1)S(1)}, u32[]{:S(2)}, u32[]{:S(2)}) collective-permute-start(bf16[64,1024]{1,0:T(8,128)(2,1)S(1)} %bitcast.103), channel_id=1, source_target_pairs={{0,8},{1,9},{2,10},{3,11},{4,12},{5,13},{6,14},{7,15},{8,0},{9,1},... | collective-permute-start | bytes 393224 | tf_op jit(solution)/shard_map/ppermute | solution.py:186
  43.1 22.1 %copy-start.16 = (bf16[64,1024]{1,0:T(8,128)(2,1)}, bf16[64,1024]{1,0:T(8,128)(2,1)S(1)}, u32[]{:S(2)}) copy-start(bf16[64,1024]{1,0:T(8,128)(2,1)S(1)} %collective-permute-done.16.refs_1_) | copy-start | bytes 393220
  43.1 15.5 %collective-permute-start.20 = (bf16[64,1024]{1,0:T(8,128)(2,1)S(1)}, bf16[64,1024]{1,0:T(8,128)(2,1)S(1)}, u32[]{:S(2)}, u32[]{:S(2)}) collective-permute-start(bf16[64,1024]{1,0:T(8,128)(2,1)S(1)} %bitcast.102), channel_id=1, source_target_pairs={{0,10},{1,11},{2,8},{3,9},{4,14},{5,15},{6,12},{7,13},{8,2},{9,3},... | collective-permute-start | bytes 393224 | tf_op jit(solution)/shard_map/ppermute | solution.py:186
  44.2 21.0 %copy-start.18 = (bf16[64,1024]{1,0:T(8,128)(2,1)}, bf16[64,1024]{1,0:T(8,128)(2,1)S(1)}, u32[]{:S(2)}) copy-start(bf16[64,1024]{1,0:T(8,128)(2,1)S(1)} %collective-permute-done.17.refs_2_) | copy-start | bytes 393220
  44.2 19.2 %collective-permute-start.21 = (bf16[64,1024]{1,0:T(8,128)(2,1)S(1)}, bf16[64,1024]{1,0:T(8,128)(2,1)S(1)}, u32[]{:S(2)}, u32[]{:S(2)}) collective-permute-start(bf16[64,1024]{1,0:T(8,128)(2,1)S(1)} %bitcast.101), channel_id=1, source_target_pairs={{0,12},{1,13},{2,14},{3,15},{4,8},{5,9},{6,10},{7,11},{8,4},{9,5},... | collective-permute-start | bytes 393224 | tf_op jit(solution)/shard_map/ppermute | solution.py:186
  47.9 17.3 %copy-start.20 = (bf16[64,1024]{1,0:T(8,128)(2,1)}, bf16[64,1024]{1,0:T(8,128)(2,1)S(1)}, u32[]{:S(2)}) copy-start(bf16[64,1024]{1,0:T(8,128)(2,1)S(1)} %collective-permute-done.18.refs_3_) | copy-start | bytes 393220
  47.9 17.3 %collective-permute-start.22 = (bf16[64,1024]{1,0:T(8,128)(2,1)S(1)}, bf16[64,1024]{1,0:T(8,128)(2,1)S(1)}, u32[]{:S(2)}, u32[]{:S(2)}) collective-permute-start(bf16[64,1024]{1,0:T(8,128)(2,1)S(1)} %bitcast.100), channel_id=1, source_target_pairs={{0,14},{1,15},{2,12},{3,13},{4,10},{5,11},{6,8},{7,9},{8,6},{9,7},... | collective-permute-start | bytes 393224 | tf_op jit(solution)/shard_map/ppermute | solution.py:186
  49.4 15.8 %copy-start.22 = (bf16[64,1024]{1,0:T(8,128)(2,1)}, bf16[64,1024]{1,0:T(8,128)(2,1)S(1)}, u32[]{:S(2)}) copy-start(bf16[64,1024]{1,0:T(8,128)(2,1)S(1)} %collective-permute-done.19.refs_4_) | copy-start | bytes 393220
  58.6 6.6 %copy-start.25 = (bf16[64,1024]{1,0:T(8,128)(2,1)}, bf16[64,1024]{1,0:T(8,128)(2,1)S(1)}, u32[]{:S(2)}) copy-start(bf16[64,1024]{1,0:T(8,128)(2,1)S(1)} %collective-permute-done.20.refs_5_) | copy-start | bytes 393220
  70.3 8.9 %collective-permute-start.23 = (bf16[512,512]{1,0:T(8,128)(2,1)}, bf16[512,512]{1,0:T(8,128)(2,1)S(1)}, u32[]{:S(2)}, u32[]{:S(2)}) collective-permute-start(bf16[512,512]{1,0:T(8,128)(2,1)} %get-tuple-element.42.narrow), channel_id=1, source_target_pairs={{0,1},{1,0},{2,3},{3,2},{4,5},{5,4},{6,7},{7,6},{8,9},{9,8},{10,11... | collective-permute-start | bytes 1572872 | tf_op jit(solution)/shard_map/ppermute | solution.py:189
  78.6 8.9 %collective-permute-start.8 = (bf16[512,512]{1,0:T(8,128)(2,1)}, bf16[512,512]{1,0:T(8,128)(2,1)S(1)}, u32[]{:S(2)}, u32[]{:S(2)}) collective-permute-start(bf16[512,512]{1,0:T(8,128)(2,1)} %get-tuple-element.32.narrow), channel_id=1, source_target_pairs={{0,1},{1,0},{2,3},{3,2},{4,5},{5,4},{6,7},{7,6},{8,9},{9,8},{10,11... | collective-permute-start | bytes 1572872 | tf_op jit(solution)/shard_map/ppermute | solution.py:189
  87.4 17.5 %collective-permute-start.24 = (bf16[512,512]{1,0:T(8,128)(2,1)}, bf16[512,512]{1,0:T(8,128)(2,1)S(1)}, u32[]{:S(2)}, u32[]{:S(2)}) collective-permute-start(bf16[512,512]{1,0:T(8,128)(2,1)} %get-tuple-element.44.narrow), channel_id=1, source_target_pairs={{0,1},{1,0},{2,3},{3,2},{4,5},{5,4},{6,7},{7,6},{8,9},{9,8},{10,11... | collective-permute-start | bytes 1572872 | tf_op jit(solution)/shard_map/ppermute | solution.py:189
  100.9 20.8 %collective-permute-start.9 = (bf16[64,1024]{1,0:T(8,128)(2,1)}, bf16[64,1024]{1,0:T(8,128)(2,1)S(1)}, u32[]{:S(2)}, u32[]{:S(2)}) collective-permute-start(bf16[64,1024]{1,0:T(8,128)(2,1)} %get-tuple-element.34), channel_id=1, source_target_pairs={{0,2},{1,3},{2,0},{3,1},{4,6},{5,7},{6,4},{7,5},{8,10},{9,11},{10,... | collective-permute-start | bytes 393224 | tf_op jit(solution)/shard_map/ppermute | solution.py:186
  102.4 19.9 %collective-permute-start.10 = (bf16[64,1024]{1,0:T(8,128)(2,1)}, bf16[64,1024]{1,0:T(8,128)(2,1)S(1)}, u32[]{:S(2)}, u32[]{:S(2)}) collective-permute-start(bf16[64,1024]{1,0:T(8,128)(2,1)} %get-tuple-element.35), channel_id=1, source_target_pairs={{0,4},{1,5},{2,6},{3,7},{4,0},{5,1},{6,2},{7,3},{8,12},{9,13},{10,... | collective-permute-start | bytes 393224 | tf_op jit(solution)/shard_map/ppermute | solution.py:186
  102.4 21.5 %collective-permute-start.11 = (bf16[64,1024]{1,0:T(8,128)(2,1)}, bf16[64,1024]{1,0:T(8,128)(2,1)S(1)}, u32[]{:S(2)}, u32[]{:S(2)}) collective-permute-start(bf16[64,1024]{1,0:T(8,128)(2,1)} %get-tuple-element.36), channel_id=1, source_target_pairs={{0,6},{1,7},{2,4},{3,5},{4,2},{5,3},{6,0},{7,1},{8,14},{9,15},{10,... | collective-permute-start | bytes 393224 | tf_op jit(solution)/shard_map/ppermute | solution.py:186
  104.5 21.0 %collective-permute-start.12 = (bf16[64,1024]{1,0:T(8,128)(2,1)}, bf16[64,1024]{1,0:T(8,128)(2,1)S(1)}, u32[]{:S(2)}, u32[]{:S(2)}) collective-permute-start(bf16[64,1024]{1,0:T(8,128)(2,1)} %get-tuple-element.37), channel_id=1, source_target_pairs={{0,8},{1,9},{2,10},{3,11},{4,12},{5,13},{6,14},{7,15},{8,0},{9,1},... | collective-permute-start | bytes 393224 | tf_op jit(solution)/shard_map/ppermute | solution.py:186
  104.9 22.5 %collective-permute-start.13 = (bf16[64,1024]{1,0:T(8,128)(2,1)}, bf16[64,1024]{1,0:T(8,128)(2,1)S(1)}, u32[]{:S(2)}, u32[]{:S(2)}) collective-permute-start(bf16[64,1024]{1,0:T(8,128)(2,1)} %get-tuple-element.38), channel_id=1, source_target_pairs={{0,10},{1,11},{2,8},{3,9},{4,14},{5,15},{6,12},{7,13},{8,2},{9,3},... | collective-permute-start | bytes 393224 | tf_op jit(solution)/shard_map/ppermute | solution.py:186
  120.8 6.6 %copy-start.11 = (bf16[64,1024]{1,0:T(8,128)(2,1)S(1)}, bf16[64,1024]{1,0:T(8,128)(2,1)}, u32[]{:S(2)}) copy-start(bf16[64,1024]{1,0:T(8,128)(2,1)} %get-tuple-element.48) | copy-start | bytes 393220
  120.8 11.8 %copy-start.10 = (bf16[64,1024]{1,0:T(8,128)(2,1)S(1)}, bf16[64,1024]{1,0:T(8,128)(2,1)}, u32[]{:S(2)}) copy-start(bf16[64,1024]{1,0:T(8,128)(2,1)} %get-tuple-element.49) | copy-start | bytes 393220
  120.8 15.9 %copy-start.9 = (bf16[64,1024]{1,0:T(8,128)(2,1)S(1)}, bf16[64,1024]{1,0:T(8,128)(2,1)}, u32[]{:S(2)}) copy-start(bf16[64,1024]{1,0:T(8,128)(2,1)} %get-tuple-element.50) | copy-start | bytes 393220
  120.8 15.9 %copy-start.3 = (bf16[64,1024]{1,0:T(8,128)(2,1)S(1)}, bf16[64,1024]{1,0:T(8,128)(2,1)}, u32[]{:S(2)}) copy-start(bf16[64,1024]{1,0:T(8,128)(2,1)} %get-tuple-element.45) | copy-start | bytes 393220
  120.8 16.0 %copy-start.8 = (bf16[64,1024]{1,0:T(8,128)(2,1)S(1)}, bf16[64,1024]{1,0:T(8,128)(2,1)}, u32[]{:S(2)}) copy-start(bf16[64,1024]{1,0:T(8,128)(2,1)} %get-tuple-element.51) | copy-start | bytes 393220
  120.9 17.1 %copy-start.7 = (bf16[64,1024]{1,0:T(8,128)(2,1)S(1)}, bf16[64,1024]{1,0:T(8,128)(2,1)}, u32[]{:S(2)}) copy-start(bf16[64,1024]{1,0:T(8,128)(2,1)} %get-tuple-element.52) | copy-start | bytes 393220
  121.7 10.9 %collective-permute-start.14 = (bf16[64,1024]{1,0:T(8,128)(2,1)S(1)}, bf16[64,1024]{1,0:T(8,128)(2,1)S(1)}, u32[]{:S(2)}, u32[]{:S(2)}) collective-permute-start(bf16[64,1024]{1,0:T(8,128)(2,1)S(1)} %copy-done.14), channel_id=1, source_target_pairs={{0,12},{1,13},{2,14},{3,15},{4,8},{5,9},{6,10},{7,11},{8,4},{9,5},... | collective-permute-start | bytes 393224 | tf_op jit(solution)/shard_map/ppermute | solution.py:186
  122.4 14.4 %collective-permute-start.15 = (bf16[64,1024]{1,0:T(8,128)(2,1)S(1)}, bf16[64,1024]{1,0:T(8,128)(2,1)S(1)}, u32[]{:S(2)}, u32[]{:S(2)}) collective-permute-start(bf16[64,1024]{1,0:T(8,128)(2,1)S(1)} %copy-done.12), channel_id=1, source_target_pairs={{0,14},{1,15},{2,12},{3,13},{4,10},{5,11},{6,8},{7,9},{8,6},{9,7},... | collective-permute-start | bytes 393224 | tf_op jit(solution)/shard_map/ppermute | solution.py:186
  123.9 12.9 %collective-permute-start.25 = (bf16[64,1024]{1,0:T(8,128)(2,1)S(1)}, bf16[64,1024]{1,0:T(8,128)(2,1)S(1)}, u32[]{:S(2)}, u32[]{:S(2)}) collective-permute-start(bf16[64,1024]{1,0:T(8,128)(2,1)S(1)} %copy-done.15), channel_id=1, source_target_pairs={{0,2},{1,3},{2,0},{3,1},{4,6},{5,7},{6,4},{7,5},{8,10},{9,11},{10,... | collective-permute-start | bytes 393224 | tf_op jit(solution)/shard_map/ppermute | solution.py:186
  125.5 12.5 %collective-permute-start.26 = (bf16[64,1024]{1,0:T(8,128)(2,1)S(1)}, bf16[64,1024]{1,0:T(8,128)(2,1)S(1)}, u32[]{:S(2)}, u32[]{:S(2)}) collective-permute-start(bf16[64,1024]{1,0:T(8,128)(2,1)S(1)} %copy-done.13), channel_id=1, source_target_pairs={{0,4},{1,5},{2,6},{3,7},{4,0},{5,1},{6,2},{7,3},{8,12},{9,13},{10,... | collective-permute-start | bytes 393224 | tf_op jit(solution)/shard_map/ppermute | solution.py:186
  127.4 12.4 %collective-permute-start.27 = (bf16[64,1024]{1,0:T(8,128)(2,1)S(1)}, bf16[64,1024]{1,0:T(8,128)(2,1)S(1)}, u32[]{:S(2)}, u32[]{:S(2)}) collective-permute-start(bf16[64,1024]{1,0:T(8,128)(2,1)S(1)} %copy-done.11), channel_id=1, source_target_pairs={{0,6},{1,7},{2,4},{3,5},{4,2},{5,3},{6,0},{7,1},{8,14},{9,15},{10,... | collective-permute-start | bytes 393224 | tf_op jit(solution)/shard_map/ppermute | solution.py:186
  132.6 15.1 %collective-permute-start.28 = (bf16[64,1024]{1,0:T(8,128)(2,1)S(1)}, bf16[64,1024]{1,0:T(8,128)(2,1)S(1)}, u32[]{:S(2)}, u32[]{:S(2)}) collective-permute-start(bf16[64,1024]{1,0:T(8,128)(2,1)S(1)} %copy-done.10), channel_id=1, source_target_pairs={{0,8},{1,9},{2,10},{3,11},{4,12},{5,13},{6,14},{7,15},{8,0},{9,1},... | collective-permute-start | bytes 393224 | tf_op jit(solution)/shard_map/ppermute | solution.py:186
  136.8 13.7 %collective-permute-start.29 = (bf16[64,1024]{1,0:T(8,128)(2,1)S(1)}, bf16[64,1024]{1,0:T(8,128)(2,1)S(1)}, u32[]{:S(2)}, u32[]{:S(2)}) collective-permute-start(bf16[64,1024]{1,0:T(8,128)(2,1)S(1)} %copy-done.9), channel_id=1, source_target_pairs={{0,10},{1,11},{2,8},{3,9},{4,14},{5,15},{6,12},{7,13},{8,2},{9,3},... | collective-permute-start | bytes 393224 | tf_op jit(solution)/shard_map/ppermute | solution.py:186
  136.8 18.5 %collective-permute-start.30 = (bf16[64,1024]{1,0:T(8,128)(2,1)S(1)}, bf16[64,1024]{1,0:T(8,128)(2,1)S(1)}, u32[]{:S(2)}, u32[]{:S(2)}) collective-permute-start(bf16[64,1024]{1,0:T(8,128)(2,1)S(1)} %copy-done.8), channel_id=1, source_target_pairs={{0,12},{1,13},{2,14},{3,15},{4,8},{5,9},{6,10},{7,11},{8,4},{9,5},... | collective-permute-start | bytes 393224 | tf_op jit(solution)/shard_map/ppermute | solution.py:186
  138.0 19.3 %collective-permute-start.31 = (bf16[64,1024]{1,0:T(8,128)(2,1)S(1)}, bf16[64,1024]{1,0:T(8,128)(2,1)S(1)}, u32[]{:S(2)}, u32[]{:S(2)}) collective-permute-start(bf16[64,1024]{1,0:T(8,128)(2,1)S(1)} %copy-done.7), channel_id=1, source_target_pairs={{0,14},{1,15},{2,12},{3,13},{4,10},{5,11},{6,8},{7,9},{8,6},{9,7},... | collective-permute-start | bytes 393224 | tf_op jit(solution)/shard_map/ppermute | solution.py:186
  (14 other events, 23.9 us)

commit v2 on v1

--- a/solution.py
+++ b/solution.py
@@ -12,11 +12,11 @@
 EPSILON = 1e-05
 CORES = 2
 CHUNKS = 2
-TILE = 256
+TILE = 512
 
 
 VMEM = pl.BlockSpec(memory_space=pltpu.VMEM)
-HBM = pl.BlockSpec(memory_space=pl.ANY)
+LIMIT = pltpu.CompilerParams(vmem_limit_bytes=12 << 20)
 
 
 def gelu(x):
@@ -51,21 +51,13 @@
     return index // CORES, index % CORES
 
 
-def start_all(copies):
-    for copy in copies:
-        copy.start()
-
-
 def enter_kernel(chips, width, *refs):
-    pieces, (gain, bias, proj_hbm, x_ref, narrow_ref, proj, sem) = refs[:chips], refs[chips:]
-    copy = pltpu.make_async_copy(proj_hbm.at[0], proj, sem)
-    copy.start()
+    pieces, (gain, bias, proj, x_ref, narrow_ref) = refs[:chips], refs[chips:]
     chip, _ = position()
     for k in range(chips):
         x_ref[pl.ds(pl.multiple_of((chip ^ k) * width, width), width), :] = pieces[k][...]
-    copy.wait()
     for t in tiles(chips * width):
-        narrow_ref[t, :] = project(x_ref[t, :], gain[0:1, :], bias[0:1, :], proj[...])
+        narrow_ref[t, :] = project(x_ref[t, :], gain[0:1, :], bias[0:1, :], proj[0])
 
 
 def load_partner(partner, padded, chips, width):
@@ -75,14 +67,8 @@
     padded[pl.ds(width + rows, width), :] = partner[pl.ds(0, width), :]
 
 
-def slot_kernel(chips, width, slots, block, x_in, narrow, partner, gain, bias, taps_hbm, output_hbm, proj_hbm,
-                x_ref, narrow_ref, taps, output, proj, padded, earlier, after, sems):
-    copies = [
-        pltpu.make_async_copy(taps_hbm.at[block], taps, sems.at[0]),
-        pltpu.make_async_copy(output_hbm.at[block], output, sems.at[1]),
-        pltpu.make_async_copy(proj_hbm.at[block + 1], proj, sems.at[2]),
-    ]
-    start_all(copies)
+def slot_kernel(chips, width, slots, block, x_in, narrow, partner, gain, bias, taps, output, proj,
+                x_ref, narrow_ref, padded, earlier, after):
     _, core = position()
     load_partner(partner, padded, chips, width)
     part = width // slots
@@ -100,35 +86,22 @@
             else:
                 at = (c + core + 1) * width + (slot + shift - slots) * part
                 after[to, :] = padded[pl.ds(pl.multiple_of(at, part), part), :]
-    for copy in copies:
-        copy.wait()
     for t in tiles(chips * width):
-        x = advance(x_in[t, :], earlier[t, :], narrow[t, :], after[t, :], taps, output[...])
+        x = advance(x_in[t, :], earlier[t, :], narrow[t, :], after[t, :], taps.at[block], output[block])
         x_ref[t, :] = x
         narrow_ref[t, :] = project(
-            x, gain[block + 1 : block + 2, :], bias[block + 1 : block + 2, :], proj[...]
+            x, gain[block + 1 : block + 2, :], bias[block + 1 : block + 2, :], proj[block + 1]
         )
 
 
-def rest_kernel(chips, width, first, layers, x_in, narrow, partner, gain, bias, taps_hbm, output_hbm, proj_hbm, *refs):
-    pieces, (taps, output, proj, padded, own, x_ref, sems) = refs[:chips], refs[chips:]
+def rest_kernel(chips, width, first, layers, x_in, narrow, partner, gain, bias, taps, output, proj, *refs):
+    pieces, (padded, own, x_ref) = refs[:chips], refs[chips:]
     blocks = range(first, layers)
     rows = chips * width
-    copies = {}
-    for n, block in enumerate(blocks):
-        copies[block] = [
-            pltpu.make_async_copy(taps_hbm.at[block], taps.at[n], sems.at[n, 0]),
-            pltpu.make_async_copy(output_hbm.at[block], output.at[n], sems.at[n, 1]),
-        ]
-        if block + 1 < layers:
-            copies[block].append(pltpu.make_async_copy(proj_hbm.at[block + 1], proj.at[n], sems.at[n, 2]))
-        start_all(copies[block])
     chip, core = position()
     load_partner(partner, padded, chips, width)
     pad = (own.shape[1] - rows) // 2
     for n, block in enumerate(blocks):
-        for copy in copies[block]:
-            copy.wait()
         for t in tiles(rows):
             size = t.stop - t.start
             if n == 0:
@@ -143,11 +116,11 @@
                 middle = held[pl.ds(pad + t.start, size), :]
                 earlier = held[pl.ds(pad + t.start - shift, size), :]
                 after = held[pl.ds(pad + t.start + shift, size), :]
-            x = advance(x, earlier, middle, after, taps.at[n], output[n])
+            x = advance(x, earlier, middle, after, taps.at[block], output[block])
             x_ref[t, :] = x
             if block + 1 < layers:
                 own[n, pl.ds(pad + t.start, size), :] = project(
-                    x, gain[block + 1 : block + 2, :], bias[block + 1 : block + 2, :], proj[n]
+                    x, gain[block + 1 : block + 2, :], bias[block + 1 : block + 2, :], proj[block + 1]
                 )
         if block + 1 < layers:
             own[n, pl.ds(0, pad), :] = own[n, pl.ds(rows, pad), :]
@@ -162,6 +135,12 @@
         bytes_accessed=blocks * 2 * (2 * model * neck + 3 * neck * neck) + 8 * rows * model,
         transcendentals=0,
     )
+
+
+def travel_order(chips):
+    half = chips // 2
+    far = sorted(range(max(2, half), chips), key=lambda k: (-(k >> 1), k))
+    return [*range(2, half), *far, *range(1, min(2, chips))]
 
 
 def chunk_count(chips):
@@ -192,27 +171,24 @@
     enter = pl.pallas_call(
         functools.partial(enter_kernel, chips, width),
         out_shape=(shape((count, model), bf16), shape((count, neck), bf16)),
-        in_specs=[VMEM] * chips + [VMEM, VMEM, HBM],
+        in_specs=[VMEM] * (chips + 3),
         out_specs=(VMEM, VMEM),
-        scratch_shapes=[pltpu.VMEM((model, neck), bf16), pltpu.SemaphoreType.DMA],
         cost_estimate=estimate(count, model, neck, 1),
+        compiler_params=LIMIT,
         name="enter",
     )
     slot_block = pl.pallas_call(
         functools.partial(slot_kernel, chips, width, slots, 0),
         out_shape=(shape((count, model), bf16), shape((count, neck), bf16)),
-        in_specs=[VMEM] * 5 + [HBM] * 3,
+        in_specs=[VMEM] * 8,
         out_specs=(VMEM, VMEM),
         scratch_shapes=[
-            pltpu.VMEM((3, neck, neck), bf16),
-            pltpu.VMEM((neck, model), bf16),
-            pltpu.VMEM((model, neck), bf16),
             pltpu.VMEM((count + 2 * width, neck), bf16),
             pltpu.VMEM((count, neck), bf16),
             pltpu.VMEM((count, neck), bf16),
-            pltpu.SemaphoreType.DMA((3,)),
         ],
         cost_estimate=estimate(count, model, neck, 1),
+        compiler_params=LIMIT,
         name="slot_block",
     )
     held = layers - 1
@@ -220,29 +196,26 @@
     rest = pl.pallas_call(
         functools.partial(rest_kernel, chips, width, 1, layers),
         out_shape=tuple(shape((width, model), bf16) for _ in range(chips)),
-        in_specs=[VMEM] * 5 + [HBM] * 3,
+        in_specs=[VMEM] * 8,
         out_specs=tuple(VMEM for _ in range(chips)),
         scratch_shapes=[
-            pltpu.VMEM((held, 3, neck, neck), bf16),
-            pltpu.VMEM((held, neck, model), bf16),
-            pltpu.VMEM((held - 1, model, neck), bf16),
             pltpu.VMEM((count + 2 * width, neck), bf16),
             pltpu.VMEM((held - 1, count + 2 * pad, neck), bf16),
             pltpu.VMEM((count, model), bf16),
-            pltpu.SemaphoreType.DMA((held, 3)),
         ],
         cost_estimate=estimate(count, model, neck, held),
+        compiler_params=LIMIT,
         name="rest",
     )
 
     grid = stream.reshape(slots, chips * chunks, part, model)
     arrived = []
     for j in range(chunks):
-        pieces = []
-        for k in range(chips):
+        pieces = {}
+        for k in [0, *travel_order(chips)]:
             piece = lax.dynamic_slice_in_dim(grid, (chip ^ k) * chunks + j, 1, axis=1).reshape(width, model)
-            pieces.append(to_chip(piece, k) if k else piece)
-        arrived.append(pieces)
+            pieces[k] = to_chip(piece, k) if k else piece
+        arrived.append([pieces[k] for k in range(chips)])
 
     left = []
     for j in range(chunks):
@@ -251,11 +224,14 @@
         x, narrow = slot_block(x, narrow, other_core(narrow), *weights)
         partner = other_core(narrow)
         pieces = rest(x, narrow, partner, *weights)
-        left.append([to_chip(piece, k) if k else piece for k, piece in enumerate(pieces)])
+        gone = {0: pieces[0]}
+        for k in travel_order(chips):
+            gone[k] = to_chip(pieces[k], k)
+        left.append(gone)
 
     result = jnp.zeros(grid.shape, bf16)
     for j in range(chunks):
-        for k in range(chips):
+        for k in [0, *travel_order(chips)]:
             piece = left[j][k].reshape(slots, 1, part, model)
             result = lax.dynamic_update_slice_in_dim(result, piece, (chip ^ k) * chunks + j, axis=1)
     return result.reshape(rows, model)

time: 159 us -> 133 us (0.84)
  the two profiles are of different devices: /device:TPU:16 before, /device:TPU:0 now
where the time goes in v2:
time: 133 us
  starting transfers between devices  60.3 us (45%)
  waiting for transfers between devices  43.9 us (33%)
  Pallas kernels  21.7 us (16%)
  local copies, waits for them, and re-layouts  6.81 us (5%)
    ppermute x28, starting transfers between devices, to_chip(): lax.ppermute(piece, 'blk', [(i, i ^ k * CORES) for i in range(peers)])  59.5 us
    ppermute x28, waiting for transfers between devices, to_chip(): lax.ppermute(piece, 'blk', [(i, i ^ k * CORES) for i in range(peers)])  43.9 us
    pallas_call x2, Pallas kernels, body(): pieces = rest(x, narrow, partner, *weights)  13.9 us
    pallas_call x2, Pallas kernels, body(): x, narrow = slot_block(x, narrow, other_core(narrow), *weights)  5.3 us
    unnamed x16, local copies, waits for them, and re-layouts  4.34 us
  transfers between devices with their start and end apart: 32, of which 9 were waited for; matrix products, arithmetic and copies ran while one was open for 0% of the time, Pallas kernels for 15%

profile of v2, /device:TPU:0, one launch (start us, length us, event | category | flops | bytes accessed | tf_op | source)
XLA Modules:
  0.0 133.0 jit_solution(3411021984737330361)
XLA Ops:
  0.0 2.0 %constant_dynamic-slice_fusion = (bf16[2,1,32,1024]{3,2,1,0:T(8,128)(2,1)S(1)}, bf16[2,1,32,1024]{3,2,1,0:T(8,128)(2,1)S(1)}, bf16[2,1,32,1024]{3,2,1,0:T(8,128)...) fusion(bf16[2,16,32,1024]{3,2,1,0:T(8,128)(2,1)} %bitcast.104, ...), kind=kLoop, calls=%fused_computation.8 | loop fusion | bytes 4194368 | tf_op jit(solution)/shard_map/dynamic_slice | solution.py:216
  2.0 3.1 %collective-permute-start = (bf16[64,1024]{1,0:T(8,128)(2,1)S(1)}, bf16[64,1024]{1,0:T(8,128)(2,1)S(1)}, u32[]{:S(2)}, u32[]{:S(2)}) collective-permute-start(bf16[64,1024]{1,0:T(8,128)(2,1)S(1)} %bitcast.118), channel_id=1, source_target_pairs={{0,2},{1,3},{2,0},{3,1},{4,6},{5,7},{6,4},{7,5},{8,10},{9,11},{10,... | collective-permute-start | bytes 393224 | tf_op jit(solution)/shard_map/ppermute | solution.py:165
  5.2 1.6 %collective-permute-start.1 = (bf16[64,1024]{1,0:T(8,128)(2,1)S(1)}, bf16[64,1024]{1,0:T(8,128)(2,1)S(1)}, u32[]{:S(2)}, u32[]{:S(2)}) collective-permute-start(bf16[64,1024]{1,0:T(8,128)(2,1)S(1)} %bitcast.117), channel_id=1, source_target_pairs={{0,4},{1,5},{2,6},{3,7},{4,0},{5,1},{6,2},{7,3},{8,12},{9,13},{10,... | collective-permute-start | bytes 393224 | tf_op jit(solution)/shard_map/ppermute | solution.py:165
  6.7 3.0 %collective-permute-start.3 = (bf16[64,1024]{1,0:T(8,128)(2,1)S(1)}, bf16[64,1024]{1,0:T(8,128)(2,1)S(1)}, u32[]{:S(2)}, u32[]{:S(2)}) collective-permute-start(bf16[64,1024]{1,0:T(8,128)(2,1)S(1)} %bitcast.115), channel_id=1, source_target_pairs={{0,8},{1,9},{2,10},{3,11},{4,12},{5,13},{6,14},{7,15},{8,0},{9,1},... | collective-permute-start | bytes 393224 | tf_op jit(solution)/shard_map/ppermute | solution.py:165
  9.7 1.3 collective-permute-start.4
  11.0 3.6 %collective-permute-start.5 = (bf16[64,1024]{1,0:T(8,128)(2,1)S(1)}, bf16[64,1024]{1,0:T(8,128)(2,1)S(1)}, u32[]{:S(2)}, u32[]{:S(2)}) collective-permute-start(bf16[64,1024]{1,0:T(8,128)(2,1)S(1)} %bitcast.113), channel_id=1, source_target_pairs={{0,12},{1,13},{2,14},{3,15},{4,8},{5,9},{6,10},{7,11},{8,4},{9,5},... | collective-permute-start | bytes 393224 | tf_op jit(solution)/shard_map/ppermute | solution.py:165
  14.6 1.3 collective-permute-done.1.refs_2_
  15.9 0.7 collective-permute-start.6
  16.6 12.6 %collective-permute-done.4.refs_5_ = bf16[64,1024]{1,0:T(8,128)(2,1)S(1)} collective-permute-done((bf16[64,1024]{1,0:T(8,128)(2,1)S(1)}, bf16[64,1024]{1,0:T(8,128)(2,1)S(1)}, u32[]{:S(2)}, u32[]{:S(2)}) %collective-permute-start.4) | collective-permute-done | bytes 131104 | tf_op jit(solution)/shard_map/ppermute | solution.py:165
  29.2 2.2 %copy-done = bf16[4,1024,512]{2,1,0:T(8,128)(2,1)S(1)} copy-done((bf16[4,1024,512]{2,1,0:T(8,128)(2,1)S(1)}, bf16[4,1024,512]{2,1,0:T(8,128)(2,1)}, u32[]{:S(2)}) %copy-start) | copy-done | bytes 4194328
  31.4 1.2 enter.2
  32.7 0.7 collective-permute-start.16
  33.5 4.7 %collective-permute-start.17 = (bf16[64,1024]{1,0:T(8,128)(2,1)S(1)}, bf16[64,1024]{1,0:T(8,128)(2,1)S(1)}, u32[]{:S(2)}, u32[]{:S(2)}) collective-permute-start(bf16[64,1024]{1,0:T(8,128)(2,1)S(1)} %bitcast.110), channel_id=1, source_target_pairs={{0,4},{1,5},{2,6},{3,7},{4,0},{5,1},{6,2},{7,3},{8,12},{9,13},{10,... | collective-permute-start | bytes 393224 | tf_op jit(solution)/shard_map/ppermute | solution.py:165
  38.2 1.1 collective-permute-start.18
  39.3 3.5 %collective-permute-start.19 = (bf16[64,1024]{1,0:T(8,128)(2,1)S(1)}, bf16[64,1024]{1,0:T(8,128)(2,1)S(1)}, u32[]{:S(2)}, u32[]{:S(2)}) collective-permute-start(bf16[64,1024]{1,0:T(8,128)(2,1)S(1)} %bitcast.108), channel_id=1, source_target_pairs={{0,8},{1,9},{2,10},{3,11},{4,12},{5,13},{6,14},{7,15},{8,0},{9,1},... | collective-permute-start | bytes 393224 | tf_op jit(solution)/shard_map/ppermute | solution.py:165
  42.8 2.3 %collective-permute-start.20 = (bf16[64,1024]{1,0:T(8,128)(2,1)S(1)}, bf16[64,1024]{1,0:T(8,128)(2,1)S(1)}, u32[]{:S(2)}, u32[]{:S(2)}) collective-permute-start(bf16[64,1024]{1,0:T(8,128)(2,1)S(1)} %bitcast.107), channel_id=1, source_target_pairs={{0,10},{1,11},{2,8},{3,9},{4,14},{5,15},{6,12},{7,13},{8,2},{9,3},... | collective-permute-start | bytes 393224 | tf_op jit(solution)/shard_map/ppermute | solution.py:165
  45.2 0.6 collective-permute-start.21
  45.8 4.7 %collective-permute-done.18.refs_3_ = bf16[64,1024]{1,0:T(8,128)(2,1)S(1)} collective-permute-done((bf16[64,1024]{1,0:T(8,128)(2,1)S(1)}, bf16[64,1024]{1,0:T(8,128)(2,1)S(1)}, u32[]{:S(2)}, u32[]{:S(2)}) %collective-permute-start.18) | collective-permute-done | bytes 131104 | tf_op jit(solution)/shard_map/ppermute | solution.py:165
  50.5 1.1 collective-permute-start.22
  51.6 10.4 %collective-permute-done.20.refs_5_ = bf16[64,1024]{1,0:T(8,128)(2,1)S(1)} collective-permute-done((bf16[64,1024]{1,0:T(8,128)(2,1)S(1)}, bf16[64,1024]{1,0:T(8,128)(2,1)S(1)}, u32[]{:S(2)}, u32[]{:S(2)}) %collective-permute-start.20) | collective-permute-done | bytes 131104 | tf_op jit(solution)/shard_map/ppermute | solution.py:165
  62.1 1.2 enter.3
  63.3 0.1 collective-permute-start.23
  63.4 0.8 copy-done.2
  64.2 2.6 %slot_block.2 = (bf16[512,1024]{1,0:T(8,128)(2,1)S(1)}, bf16[512,512]{1,0:T(8,128)(2,1)S(1)}) custom-call(bf16[512,1024]{1,0:T(8,128)(2,1)S(1)} %get-tuple-element.29.x_in, bf16[512,512]{1,0:T(8,128)(2,1)S(1)} %get-tuple-element.30.narrow, bf16[512,512]{1,0:T(8,128)(2,1)S(1)} %collective-permute-done.7.partner, f32[4,1024]{1,0:T(4,128)S(1)} %copy-done.3, ...), custom_call_target="tpu_custom_call" | custom-call | flops 1879048192 | bytes 7864320 | tf_op jit(solution)/shard_map/slot_block/pallas_call | solution.py:224
  67.0 2.7 %slot_block.3 = (bf16[512,1024]{1,0:T(8,128)(2,1)S(1)}, bf16[512,512]{1,0:T(8,128)(2,1)S(1)}) custom-call(bf16[512,1024]{1,0:T(8,128)(2,1)S(1)} %get-tuple-element.41.x_in, bf16[512,512]{1,0:T(8,128)(2,1)S(1)} %get-tuple-element.42.narrow, bf16[512,512]{1,0:T(8,128)(2,1)S(1)} %collective-permute-done.23.partner, f32[4,1024]{1,0:T(4,128)S(1)} %copy-done.3, ...), custom_call_target="tpu_custom_call" | custom-call | flops 1879048192 | bytes 7864320 | tf_op jit(solution)/shard_map/slot_block/pallas_call | solution.py:224
  69.6 0.6 collective-permute-start.24
  70.2 7.0 %rest.2 = (bf16[64,1024]{1,0:T(8,128)(2,1)S(1)}, bf16[64,1024]{1,0:T(8,128)(2,1)S(1)}, bf16[64,1024]{1,0:T(8,128)(2,1)S(1)}, bf16[64,1024]{1,0:T(8,128)(2,1)S(1)...) custom-call(bf16[512,1024]{1,0:T(8,128)(2,1)S(1)} %get-tuple-element, ...), custom_call_target="tpu_custom_call" | custom-call | flops 5637144576 | bytes 15204352 | tf_op jit(solution)/shard_map/rest/pallas_call | solution.py:226
  77.2 4.8 %collective-permute-start.9 = (bf16[64,1024]{1,0:T(8,128)(2,1)S(1)}, bf16[64,1024]{1,0:T(8,128)(2,1)S(1)}, u32[]{:S(2)}, u32[]{:S(2)}) collective-permute-start(bf16[64,1024]{1,0:T(8,128)(2,1)S(1)} %get-tuple-element.34), channel_id=1, source_target_pairs={{0,4},{1,5},{2,6},{3,7},{4,0},{5,1},{6,2},{7,3},{8,12},{9,13},{10,... | collective-permute-start | bytes 393224 | tf_op jit(solution)/shard_map/ppermute | solution.py:165
  82.0 0.6 collective-permute-start.10
  82.6 2.4 %collective-permute-start.11 = (bf16[64,1024]{1,0:T(8,128)(2,1)S(1)}, bf16[64,1024]{1,0:T(8,128)(2,1)S(1)}, u32[]{:S(2)}, u32[]{:S(2)}) collective-permute-start(bf16[64,1024]{1,0:T(8,128)(2,1)S(1)} %get-tuple-element.36), channel_id=1, source_target_pairs={{0,12},{1,13},{2,14},{3,15},{4,8},{5,9},{6,10},{7,11},{8,4},{9,5},... | collective-permute-start | bytes 393224 | tf_op jit(solution)/shard_map/ppermute | solution.py:165
  85.0 1.9 %collective-permute-start.12 = (bf16[64,1024]{1,0:T(8,128)(2,1)S(1)}, bf16[64,1024]{1,0:T(8,128)(2,1)S(1)}, u32[]{:S(2)}, u32[]{:S(2)}) collective-permute-start(bf16[64,1024]{1,0:T(8,128)(2,1)S(1)} %get-tuple-element.37), channel_id=1, source_target_pairs={{0,14},{1,15},{2,12},{3,13},{4,10},{5,11},{6,8},{7,9},{8,6},{9,7},... | collective-permute-start | bytes 393224 | tf_op jit(solution)/shard_map/ppermute | solution.py:165
  86.8 0.6 collective-permute-start.13
  87.5 6.8 %rest.3 = (bf16[64,1024]{1,0:T(8,128)(2,1)S(1)}, bf16[64,1024]{1,0:T(8,128)(2,1)S(1)}, bf16[64,1024]{1,0:T(8,128)(2,1)S(1)}, bf16[64,1024]{1,0:T(8,128)(2,1)S(1)...) custom-call(bf16[512,1024]{1,0:T(8,128)(2,1)S(1)} %get-tuple-element, ...), custom_call_target="tpu_custom_call" | custom-call | flops 5637144576 | bytes 15204352 | tf_op jit(solution)/shard_map/rest/pallas_call | solution.py:226
  94.3 0.3 broadcast_in_dim.3
  94.6 2.9 %collective-permute-start.14 = (bf16[64,1024]{1,0:T(8,128)(2,1)S(1)}, bf16[64,1024]{1,0:T(8,128)(2,1)S(1)}, u32[]{:S(2)}, u32[]{:S(2)}) collective-permute-start(bf16[64,1024]{1,0:T(8,128)(2,1)S(1)} %get-tuple-element.39), channel_id=1, source_target_pairs={{0,10},{1,11},{2,8},{3,9},{4,14},{5,15},{6,12},{7,13},{8,2},{9,3},... | collective-permute-start | bytes 393224 | tf_op jit(solution)/shard_map/ppermute | solution.py:165
  97.5 1.0 collective-permute-start.15
  98.6 1.2 collective-permute-start.25
  99.7 6.7 %collective-permute-start.26 = (bf16[64,1024]{1,0:T(8,128)(2,1)S(1)}, bf16[64,1024]{1,0:T(8,128)(2,1)S(1)}, u32[]{:S(2)}, u32[]{:S(2)}) collective-permute-start(bf16[64,1024]{1,0:T(8,128)(2,1)S(1)} %get-tuple-element.47), channel_id=1, source_target_pairs={{0,6},{1,7},{2,4},{3,5},{4,2},{5,3},{6,0},{7,1},{8,14},{9,15},{10,... | collective-permute-start | bytes 393224 | tf_op jit(solution)/shard_map/ppermute | solution.py:165
  106.4 0.8 collective-permute-done.13
  107.2 2.4 %collective-permute-start.27 = (bf16[64,1024]{1,0:T(8,128)(2,1)S(1)}, bf16[64,1024]{1,0:T(8,128)(2,1)S(1)}, u32[]{:S(2)}, u32[]{:S(2)}) collective-permute-start(bf16[64,1024]{1,0:T(8,128)(2,1)S(1)} %get-tuple-element.48), channel_id=1, source_target_pairs={{0,12},{1,13},{2,14},{3,15},{4,8},{5,9},{6,10},{7,11},{8,4},{9,5},... | collective-permute-start | bytes 393224 | tf_op jit(solution)/shard_map/ppermute | solution.py:165
  109.7 2.0 %collective-permute-done.14 = bf16[64,1024]{1,0:T(8,128)(2,1)S(1)} collective-permute-done((bf16[64,1024]{1,0:T(8,128)(2,1)S(1)}, bf16[64,1024]{1,0:T(8,128)(2,1)S(1)}, u32[]{:S(2)}, u32[]{:S(2)}) %collective-permute-start.14) | collective-permute-done | bytes 131104 | tf_op jit(solution)/shard_map/ppermute | solution.py:165
  111.7 3.1 %collective-permute-start.28 = (bf16[64,1024]{1,0:T(8,128)(2,1)S(1)}, bf16[64,1024]{1,0:T(8,128)(2,1)S(1)}, u32[]{:S(2)}, u32[]{:S(2)}) collective-permute-start(bf16[64,1024]{1,0:T(8,128)(2,1)S(1)} %get-tuple-element.49), channel_id=1, source_target_pairs={{0,14},{1,15},{2,12},{3,13},{4,10},{5,11},{6,8},{7,9},{8,6},{9,7},... | collective-permute-start | bytes 393224 | tf_op jit(solution)/shard_map/ppermute | solution.py:165
  114.9 2.9 %collective-permute-start.30 = (bf16[64,1024]{1,0:T(8,128)(2,1)S(1)}, bf16[64,1024]{1,0:T(8,128)(2,1)S(1)}, u32[]{:S(2)}, u32[]{:S(2)}) collective-permute-start(bf16[64,1024]{1,0:T(8,128)(2,1)S(1)} %get-tuple-element.51), channel_id=1, source_target_pairs={{0,10},{1,11},{2,8},{3,9},{4,14},{5,15},{6,12},{7,13},{8,2},{9,3},... | collective-permute-start | bytes 393224 | tf_op jit(solution)/shard_map/ppermute | solution.py:165
  117.9 1.5 %collective-permute-start.31 = (bf16[64,1024]{1,0:T(8,128)(2,1)S(1)}, bf16[64,1024]{1,0:T(8,128)(2,1)S(1)}, u32[]{:S(2)}, u32[]{:S(2)}) collective-permute-start(bf16[64,1024]{1,0:T(8,128)(2,1)S(1)} %get-tuple-element.52), channel_id=1, source_target_pairs={{0,2},{1,3},{2,0},{3,1},{4,6},{5,7},{6,4},{7,5},{8,10},{9,11},{10,... | collective-permute-start | bytes 393224 | tf_op jit(solution)/shard_map/ppermute | solution.py:165
  119.5 0.6 collective-permute-done.28
  120.1 9.6 %collective-permute-done.29 = bf16[64,1024]{1,0:T(8,128)(2,1)S(1)} collective-permute-done((bf16[64,1024]{1,0:T(8,128)(2,1)S(1)}, bf16[64,1024]{1,0:T(8,128)(2,1)S(1)}, u32[]{:S(2)}, u32[]{:S(2)}) %collective-permute-start.29) | collective-permute-done | bytes 131104 | tf_op jit(solution)/shard_map/ppermute | solution.py:165
  129.7 1.9 %collective-permute-done.30 = bf16[64,1024]{1,0:T(8,128)(2,1)S(1)} collective-permute-done((bf16[64,1024]{1,0:T(8,128)(2,1)S(1)}, bf16[64,1024]{1,0:T(8,128)(2,1)S(1)}, u32[]{:S(2)}, u32[]{:S(2)}) %collective-permute-start.30) | collective-permute-done | bytes 131104 | tf_op jit(solution)/shard_map/ppermute | solution.py:165
  131.7 1.3 copy-done.5
  (57 shorter events, 0.5 us)
Async XLA Ops:
  0.0 29.2 %copy-start.3 = (f32[4,1024]{1,0:T(4,128)S(1)}, f32[4,1024]{1,0:T(4,128)}, u32[]{:S(2)}) copy-start(f32[4,1024]{1,0:T(4,128)} %gain.7) | copy-start | bytes 49156
  0.0 29.2 %copy-start.4 = (f32[4,1024]{1,0:T(4,128)S(1)}, f32[4,1024]{1,0:T(4,128)}, u32[]{:S(2)}) copy-start(f32[4,1024]{1,0:T(4,128)} %bias.7) | copy-start | bytes 49156
  0.0 63.4 %slice-start = ((s8[6291456]{0:T(1024)(128)(4,1)}), s8[4194304]{0:T(1024)(128)(4,1)S(1)}, s32[]{:S(2)}) async-start(s8[6291456]{0:T(1024)(128)(4,1)} %bitcast.98), calls=%async_computation | async-start | bytes 8388608
  2.0 9.0 %collective-permute-start = (bf16[64,1024]{1,0:T(8,128)(2,1)S(1)}, bf16[64,1024]{1,0:T(8,128)(2,1)S(1)}, u32[]{:S(2)}, u32[]{:S(2)}) collective-permute-start(bf16[64,1024]{1,0:T(8,128)(2,1)S(1)} %bitcast.118), channel_id=1, source_target_pairs={{0,2},{1,3},{2,0},{3,1},{4,6},{5,7},{6,4},{7,5},{8,10},{9,11},{10,... | collective-permute-start | bytes 393224 | tf_op jit(solution)/shard_map/ppermute | solution.py:165
  5.2 10.8 %collective-permute-start.1 = (bf16[64,1024]{1,0:T(8,128)(2,1)S(1)}, bf16[64,1024]{1,0:T(8,128)(2,1)S(1)}, u32[]{:S(2)}, u32[]{:S(2)}) collective-permute-start(bf16[64,1024]{1,0:T(8,128)(2,1)S(1)} %bitcast.117), channel_id=1, source_target_pairs={{0,4},{1,5},{2,6},{3,7},{4,0},{5,1},{6,2},{7,3},{8,12},{9,13},{10,... | collective-permute-start | bytes 393224 | tf_op jit(solution)/shard_map/ppermute | solution.py:165
  6.7 9.9 %collective-permute-start.2 = (bf16[64,1024]{1,0:T(8,128)(2,1)S(1)}, bf16[64,1024]{1,0:T(8,128)(2,1)S(1)}, u32[]{:S(2)}, u32[]{:S(2)}) collective-permute-start(bf16[64,1024]{1,0:T(8,128)(2,1)S(1)} %bitcast.116), channel_id=1, source_target_pairs={{0,6},{1,7},{2,4},{3,5},{4,2},{5,3},{6,0},{7,1},{8,14},{9,15},{10,... | collective-permute-start | bytes 393224 | tf_op jit(solution)/shard_map/ppermute | solution.py:165
  6.7 9.9 %collective-permute-start.3 = (bf16[64,1024]{1,0:T(8,128)(2,1)S(1)}, bf16[64,1024]{1,0:T(8,128)(2,1)S(1)}, u32[]{:S(2)}, u32[]{:S(2)}) collective-permute-start(bf16[64,1024]{1,0:T(8,128)(2,1)S(1)} %bitcast.115), channel_id=1, source_target_pairs={{0,8},{1,9},{2,10},{3,11},{4,12},{5,13},{6,14},{7,15},{8,0},{9,1},... | collective-permute-start | bytes 393224 | tf_op jit(solution)/shard_map/ppermute | solution.py:165
  9.7 19.4 %collective-permute-start.4 = (bf16[64,1024]{1,0:T(8,128)(2,1)S(1)}, bf16[64,1024]{1,0:T(8,128)(2,1)S(1)}, u32[]{:S(2)}, u32[]{:S(2)}) collective-permute-start(bf16[64,1024]{1,0:T(8,128)(2,1)S(1)} %bitcast.114), channel_id=1, source_target_pairs={{0,10},{1,11},{2,8},{3,9},{4,14},{5,15},{6,12},{7,13},{8,2},{9,3},... | collective-permute-start | bytes 393224 | tf_op jit(solution)/shard_map/ppermute | solution.py:165
  11.0 18.2 %collective-permute-start.5 = (bf16[64,1024]{1,0:T(8,128)(2,1)S(1)}, bf16[64,1024]{1,0:T(8,128)(2,1)S(1)}, u32[]{:S(2)}, u32[]{:S(2)}) collective-permute-start(bf16[64,1024]{1,0:T(8,128)(2,1)S(1)} %bitcast.113), channel_id=1, source_target_pairs={{0,12},{1,13},{2,14},{3,15},{4,8},{5,9},{6,10},{7,11},{8,4},{9,5},... | collective-permute-start | bytes 393224 | tf_op jit(solution)/shard_map/ppermute | solution.py:165
  15.9 13.2 %collective-permute-start.6 = (bf16[64,1024]{1,0:T(8,128)(2,1)S(1)}, bf16[64,1024]{1,0:T(8,128)(2,1)S(1)}, u32[]{:S(2)}, u32[]{:S(2)}) collective-permute-start(bf16[64,1024]{1,0:T(8,128)(2,1)S(1)} %bitcast.112), channel_id=1, source_target_pairs={{0,14},{1,15},{2,12},{3,13},{4,10},{5,11},{6,8},{7,9},{8,6},{9,7},... | collective-permute-start | bytes 393224 | tf_op jit(solution)/shard_map/ppermute | solution.py:165
  29.2 2.2 %copy-start = (bf16[4,1024,512]{2,1,0:T(8,128)(2,1)S(1)}, bf16[4,1024,512]{2,1,0:T(8,128)(2,1)}, u32[]{:S(2)}) copy-start(bf16[4,1024,512]{2,1,0:T(8,128)(2,1)} %proj.7) | copy-start | bytes 12582916
  31.4 30.7 %copy-start.1 = (bf16[4,1024,512]{2,1,0:T(8,128)(2,1)S(1)}, bf16[4,1024,512]{2,1,0:T(8,128)(2,1)}, u32[]{:S(2)}) copy-start(bf16[4,1024,512]{2,1,0:T(8,128)(2,1)} %proj.7) | copy-start | bytes 12582916
  31.4 32.0 %slice-start.1 = ((s8[6291456]{0:T(1024)(128)(4,1)}), s8[2097152]{0:T(1024)(128)(4,1)S(1)}, s32[]{:S(2)}) async-start(s8[6291456]{0:T(1024)(128)(4,1)} %bitcast.98), calls=%async_computation.1 | async-start | bytes 4194304
  32.6 30.7 %collective-permute-start.7 = (bf16[512,512]{1,0:T(8,128)(2,1)S(1)}, bf16[512,512]{1,0:T(8,128)(2,1)S(1)}, u32[]{:S(2)}, u32[]{:S(2)}) collective-permute-start(bf16[512,512]{1,0:T(8,128)(2,1)S(1)} %get-tuple-element.30.narrow), channel_id=1, source_target_pairs={{0,1},{1,0},{2,3},{3,2},{4,5},{5,4},{6,7},{7,6},{8,9},{9,8},{10,11... | collective-permute-start | bytes 1572872 | tf_op jit(solution)/shard_map/ppermute | solution.py:168
  32.7 10.1 %collective-permute-start.16 = (bf16[64,1024]{1,0:T(8,128)(2,1)S(1)}, bf16[64,1024]{1,0:T(8,128)(2,1)S(1)}, u32[]{:S(2)}, u32[]{:S(2)}) collective-permute-start(bf16[64,1024]{1,0:T(8,128)(2,1)S(1)} %bitcast.111), channel_id=1, source_target_pairs={{0,2},{1,3},{2,0},{3,1},{4,6},{5,7},{6,4},{7,5},{8,10},{9,11},{10,... | collective-permute-start | bytes 393224 | tf_op jit(solution)/shard_map/ppermute | solution.py:165
  33.5 11.7 %collective-permute-start.17 = (bf16[64,1024]{1,0:T(8,128)(2,1)S(1)}, bf16[64,1024]{1,0:T(8,128)(2,1)S(1)}, u32[]{:S(2)}, u32[]{:S(2)}) collective-permute-start(bf16[64,1024]{1,0:T(8,128)(2,1)S(1)} %bitcast.110), channel_id=1, source_target_pairs={{0,4},{1,5},{2,6},{3,7},{4,0},{5,1},{6,2},{7,3},{8,12},{9,13},{10,... | collective-permute-start | bytes 393224 | tf_op jit(solution)/shard_map/ppermute | solution.py:165
  38.2 12.3 %collective-permute-start.18 = (bf16[64,1024]{1,0:T(8,128)(2,1)S(1)}, bf16[64,1024]{1,0:T(8,128)(2,1)S(1)}, u32[]{:S(2)}, u32[]{:S(2)}) collective-permute-start(bf16[64,1024]{1,0:T(8,128)(2,1)S(1)} %bitcast.109), channel_id=1, source_target_pairs={{0,6},{1,7},{2,4},{3,5},{4,2},{5,3},{6,0},{7,1},{8,14},{9,15},{10,... | collective-permute-start | bytes 393224 | tf_op jit(solution)/shard_map/ppermute | solution.py:165
  39.3 12.3 %collective-permute-start.19 = (bf16[64,1024]{1,0:T(8,128)(2,1)S(1)}, bf16[64,1024]{1,0:T(8,128)(2,1)S(1)}, u32[]{:S(2)}, u32[]{:S(2)}) collective-permute-start(bf16[64,1024]{1,0:T(8,128)(2,1)S(1)} %bitcast.108), channel_id=1, source_target_pairs={{0,8},{1,9},{2,10},{3,11},{4,12},{5,13},{6,14},{7,15},{8,0},{9,1},... | collective-permute-start | bytes 393224 | tf_op jit(solution)/shard_map/ppermute | solution.py:165
  42.8 19.2 %collective-permute-start.20 = (bf16[64,1024]{1,0:T(8,128)(2,1)S(1)}, bf16[64,1024]{1,0:T(8,128)(2,1)S(1)}, u32[]{:S(2)}, u32[]{:S(2)}) collective-permute-start(bf16[64,1024]{1,0:T(8,128)(2,1)S(1)} %bitcast.107), channel_id=1, source_target_pairs={{0,10},{1,11},{2,8},{3,9},{4,14},{5,15},{6,12},{7,13},{8,2},{9,3},... | collective-permute-start | bytes 393224 | tf_op jit(solution)/shard_map/ppermute | solution.py:165
  45.2 16.9 %collective-permute-start.21 = (bf16[64,1024]{1,0:T(8,128)(2,1)S(1)}, bf16[64,1024]{1,0:T(8,128)(2,1)S(1)}, u32[]{:S(2)}, u32[]{:S(2)}) collective-permute-start(bf16[64,1024]{1,0:T(8,128)(2,1)S(1)} %bitcast.106), channel_id=1, source_target_pairs={{0,12},{1,13},{2,14},{3,15},{4,8},{5,9},{6,10},{7,11},{8,4},{9,5},... | collective-permute-start | bytes 393224 | tf_op jit(solution)/shard_map/ppermute | solution.py:165
  50.5 11.6 %collective-permute-start.22 = (bf16[64,1024]{1,0:T(8,128)(2,1)S(1)}, bf16[64,1024]{1,0:T(8,128)(2,1)S(1)}, u32[]{:S(2)}, u32[]{:S(2)}) collective-permute-start(bf16[64,1024]{1,0:T(8,128)(2,1)S(1)} %bitcast.105), channel_id=1, source_target_pairs={{0,14},{1,15},{2,12},{3,13},{4,10},{5,11},{6,8},{7,9},{8,6},{9,7},... | collective-permute-start | bytes 393224 | tf_op jit(solution)/shard_map/ppermute | solution.py:165
  62.0 2.2 %copy-start.2 = (bf16[4,512,1024]{2,1,0:T(8,128)(2,1)S(1)}, bf16[4,512,1024]{2,1,0:T(8,128)(2,1)}, u32[]{:S(2)}) copy-start(bf16[4,512,1024]{2,1,0:T(8,128)(2,1)} %output.7) | copy-start | bytes 12582916
  63.3 3.7 %collective-permute-start.23 = (bf16[512,512]{1,0:T(8,128)(2,1)S(1)}, bf16[512,512]{1,0:T(8,128)(2,1)S(1)}, u32[]{:S(2)}, u32[]{:S(2)}) collective-permute-start(bf16[512,512]{1,0:T(8,128)(2,1)S(1)} %get-tuple-element.42.narrow), channel_id=1, source_target_pairs={{0,1},{1,0},{2,3},{3,2},{4,5},{5,4},{6,7},{7,6},{8,9},{9,8},{10,11... | collective-permute-start | bytes 1572872 | tf_op jit(solution)/shard_map/ppermute | solution.py:168
  66.9 3.3 %collective-permute-start.8 = (bf16[512,512]{1,0:T(8,128)(2,1)S(1)}, bf16[512,512]{1,0:T(8,128)(2,1)S(1)}, u32[]{:S(2)}, u32[]{:S(2)}) collective-permute-start(bf16[512,512]{1,0:T(8,128)(2,1)S(1)} %get-tuple-element.32.narrow), channel_id=1, source_target_pairs={{0,1},{1,0},{2,3},{3,2},{4,5},{5,4},{6,7},{7,6},{8,9},{9,8},{10,11... | collective-permute-start | bytes 1572872 | tf_op jit(solution)/shard_map/ppermute | solution.py:168
  69.6 17.2 %collective-permute-start.24 = (bf16[512,512]{1,0:T(8,128)(2,1)S(1)}, bf16[512,512]{1,0:T(8,128)(2,1)S(1)}, u32[]{:S(2)}, u32[]{:S(2)}) collective-permute-start(bf16[512,512]{1,0:T(8,128)(2,1)S(1)} %get-tuple-element.44.narrow), channel_id=1, source_target_pairs={{0,1},{1,0},{2,3},{3,2},{4,5},{5,4},{6,7},{7,6},{8,9},{9,8},{10,11... | collective-permute-start | bytes 1572872 | tf_op jit(solution)/shard_map/ppermute | solution.py:168
  77.2 17.4 %collective-permute-start.9 = (bf16[64,1024]{1,0:T(8,128)(2,1)S(1)}, bf16[64,1024]{1,0:T(8,128)(2,1)S(1)}, u32[]{:S(2)}, u32[]{:S(2)}) collective-permute-start(bf16[64,1024]{1,0:T(8,128)(2,1)S(1)} %get-tuple-element.34), channel_id=1, source_target_pairs={{0,4},{1,5},{2,6},{3,7},{4,0},{5,1},{6,2},{7,3},{8,12},{9,13},{10,... | collective-permute-start | bytes 393224 | tf_op jit(solution)/shard_map/ppermute | solution.py:165
  82.0 15.4 %collective-permute-start.10 = (bf16[64,1024]{1,0:T(8,128)(2,1)S(1)}, bf16[64,1024]{1,0:T(8,128)(2,1)S(1)}, u32[]{:S(2)}, u32[]{:S(2)}) collective-permute-start(bf16[64,1024]{1,0:T(8,128)(2,1)S(1)} %get-tuple-element.35), channel_id=1, source_target_pairs={{0,6},{1,7},{2,4},{3,5},{4,2},{5,3},{6,0},{7,1},{8,14},{9,15},{10,... | collective-permute-start | bytes 393224 | tf_op jit(solution)/shard_map/ppermute | solution.py:165
  82.6 15.9 %collective-permute-start.11 = (bf16[64,1024]{1,0:T(8,128)(2,1)S(1)}, bf16[64,1024]{1,0:T(8,128)(2,1)S(1)}, u32[]{:S(2)}, u32[]{:S(2)}) collective-permute-start(bf16[64,1024]{1,0:T(8,128)(2,1)S(1)} %get-tuple-element.36), channel_id=1, source_target_pairs={{0,12},{1,13},{2,14},{3,15},{4,8},{5,9},{6,10},{7,11},{8,4},{9,5},... | collective-permute-start | bytes 393224 | tf_op jit(solution)/shard_map/ppermute | solution.py:165
  85.0 14.8 %collective-permute-start.12 = (bf16[64,1024]{1,0:T(8,128)(2,1)S(1)}, bf16[64,1024]{1,0:T(8,128)(2,1)S(1)}, u32[]{:S(2)}, u32[]{:S(2)}) collective-permute-start(bf16[64,1024]{1,0:T(8,128)(2,1)S(1)} %get-tuple-element.37), channel_id=1, source_target_pairs={{0,14},{1,15},{2,12},{3,13},{4,10},{5,11},{6,8},{7,9},{8,6},{9,7},... | collective-permute-start | bytes 393224 | tf_op jit(solution)/shard_map/ppermute | solution.py:165
  86.8 20.4 %collective-permute-start.13 = (bf16[64,1024]{1,0:T(8,128)(2,1)S(1)}, bf16[64,1024]{1,0:T(8,128)(2,1)S(1)}, u32[]{:S(2)}, u32[]{:S(2)}) collective-permute-start(bf16[64,1024]{1,0:T(8,128)(2,1)S(1)} %get-tuple-element.38), channel_id=1, source_target_pairs={{0,8},{1,9},{2,10},{3,11},{4,12},{5,13},{6,14},{7,15},{8,0},{9,1},... | collective-permute-start | bytes 393224 | tf_op jit(solution)/shard_map/ppermute | solution.py:165
  94.6 17.1 %collective-permute-start.14 = (bf16[64,1024]{1,0:T(8,128)(2,1)S(1)}, bf16[64,1024]{1,0:T(8,128)(2,1)S(1)}, u32[]{:S(2)}, u32[]{:S(2)}) collective-permute-start(bf16[64,1024]{1,0:T(8,128)(2,1)S(1)} %get-tuple-element.39), channel_id=1, source_target_pairs={{0,10},{1,11},{2,8},{3,9},{4,14},{5,15},{6,12},{7,13},{8,2},{9,3},... | collective-permute-start | bytes 393224 | tf_op jit(solution)/shard_map/ppermute | solution.py:165
  97.5 17.3 %collective-permute-start.15 = (bf16[64,1024]{1,0:T(8,128)(2,1)S(1)}, bf16[64,1024]{1,0:T(8,128)(2,1)S(1)}, u32[]{:S(2)}, u32[]{:S(2)}) collective-permute-start(bf16[64,1024]{1,0:T(8,128)(2,1)S(1)} %get-tuple-element.40), channel_id=1, source_target_pairs={{0,2},{1,3},{2,0},{3,1},{4,6},{5,7},{6,4},{7,5},{8,10},{9,11},{10,... | collective-permute-start | bytes 393224 | tf_op jit(solution)/shard_map/ppermute | solution.py:165
  98.6 16.4 %collective-permute-start.25 = (bf16[64,1024]{1,0:T(8,128)(2,1)S(1)}, bf16[64,1024]{1,0:T(8,128)(2,1)S(1)}, u32[]{:S(2)}, u32[]{:S(2)}) collective-permute-start(bf16[64,1024]{1,0:T(8,128)(2,1)S(1)} %get-tuple-element.46), channel_id=1, source_target_pairs={{0,4},{1,5},{2,6},{3,7},{4,0},{5,1},{6,2},{7,3},{8,12},{9,13},{10,... | collective-permute-start | bytes 393224 | tf_op jit(solution)/shard_map/ppermute | solution.py:165
  99.7 18.2 %collective-permute-start.26 = (bf16[64,1024]{1,0:T(8,128)(2,1)S(1)}, bf16[64,1024]{1,0:T(8,128)(2,1)S(1)}, u32[]{:S(2)}, u32[]{:S(2)}) collective-permute-start(bf16[64,1024]{1,0:T(8,128)(2,1)S(1)} %get-tuple-element.47), channel_id=1, source_target_pairs={{0,6},{1,7},{2,4},{3,5},{4,2},{5,3},{6,0},{7,1},{8,14},{9,15},{10,... | collective-permute-start | bytes 393224 | tf_op jit(solution)/shard_map/ppermute | solution.py:165
  107.2 12.2 %collective-permute-start.27 = (bf16[64,1024]{1,0:T(8,128)(2,1)S(1)}, bf16[64,1024]{1,0:T(8,128)(2,1)S(1)}, u32[]{:S(2)}, u32[]{:S(2)}) collective-permute-start(bf16[64,1024]{1,0:T(8,128)(2,1)S(1)} %get-tuple-element.48), channel_id=1, source_target_pairs={{0,12},{1,13},{2,14},{3,15},{4,8},{5,9},{6,10},{7,11},{8,4},{9,5},... | collective-permute-start | bytes 393224 | tf_op jit(solution)/shard_map/ppermute | solution.py:165
  111.7 8.4 %collective-permute-start.28 = (bf16[64,1024]{1,0:T(8,128)(2,1)S(1)}, bf16[64,1024]{1,0:T(8,128)(2,1)S(1)}, u32[]{:S(2)}, u32[]{:S(2)}) collective-permute-start(bf16[64,1024]{1,0:T(8,128)(2,1)S(1)} %get-tuple-element.49), channel_id=1, source_target_pairs={{0,14},{1,15},{2,12},{3,13},{4,10},{5,11},{6,8},{7,9},{8,6},{9,7},... | collective-permute-start | bytes 393224 | tf_op jit(solution)/shard_map/ppermute | solution.py:165
  114.8 14.9 %collective-permute-start.29 = (bf16[64,1024]{1,0:T(8,128)(2,1)S(1)}, bf16[64,1024]{1,0:T(8,128)(2,1)S(1)}, u32[]{:S(2)}, u32[]{:S(2)}) collective-permute-start(bf16[64,1024]{1,0:T(8,128)(2,1)S(1)} %get-tuple-element.50), channel_id=1, source_target_pairs={{0,8},{1,9},{2,10},{3,11},{4,12},{5,13},{6,14},{7,15},{8,0},{9,1},... | collective-permute-start | bytes 393224 | tf_op jit(solution)/shard_map/ppermute | solution.py:165
  114.9 16.7 %collective-permute-start.30 = (bf16[64,1024]{1,0:T(8,128)(2,1)S(1)}, bf16[64,1024]{1,0:T(8,128)(2,1)S(1)}, u32[]{:S(2)}, u32[]{:S(2)}) collective-permute-start(bf16[64,1024]{1,0:T(8,128)(2,1)S(1)} %get-tuple-element.51), channel_id=1, source_target_pairs={{0,10},{1,11},{2,8},{3,9},{4,14},{5,15},{6,12},{7,13},{8,2},{9,3},... | collective-permute-start | bytes 393224 | tf_op jit(solution)/shard_map/ppermute | solution.py:165
  117.9 13.7 %collective-permute-start.31 = (bf16[64,1024]{1,0:T(8,128)(2,1)S(1)}, bf16[64,1024]{1,0:T(8,128)(2,1)S(1)}, u32[]{:S(2)}, u32[]{:S(2)}) collective-permute-start(bf16[64,1024]{1,0:T(8,128)(2,1)S(1)} %get-tuple-element.52), channel_id=1, source_target_pairs={{0,2},{1,3},{2,0},{3,1},{4,6},{5,7},{6,4},{7,5},{8,10},{9,11},{10,... | collective-permute-start | bytes 393224 | tf_op jit(solution)/shard_map/ppermute | solution.py:165
  131.7 1.3 copy-start.5

commit v3 on v2

--- a/solution.py
+++ b/solution.py
@@ -51,8 +51,12 @@
     return index // CORES, index % CORES
 
 
+def load_kernel(taps, output, proj, token):
+    token[...] = jnp.zeros_like(token)
+
+
 def enter_kernel(chips, width, *refs):
-    pieces, (gain, bias, proj, x_ref, narrow_ref) = refs[:chips], refs[chips:]
+    pieces, (gain, bias, proj, _, x_ref, narrow_ref) = refs[:chips], refs[chips:]
     chip, _ = position()
     for k in range(chips):
         x_ref[pl.ds(pl.multiple_of((chip ^ k) * width, width), width), :] = pieces[k][...]
@@ -168,10 +172,18 @@
         return lax.ppermute(narrow, "blk", [(i, i ^ 1) for i in range(peers)])
 
     shape = jax.ShapeDtypeStruct
+    load = pl.pallas_call(
+        load_kernel,
+        out_shape=shape((8, 128), jnp.float32),
+        in_specs=[VMEM] * 3,
+        out_specs=VMEM,
+        compiler_params=LIMIT,
+        name="load",
+    )
     enter = pl.pallas_call(
         functools.partial(enter_kernel, chips, width),
         out_shape=(shape((count, model), bf16), shape((count, neck), bf16)),
-        in_specs=[VMEM] * (chips + 3),
+        in_specs=[VMEM] * (chips + 4),
         out_specs=(VMEM, VMEM),
         cost_estimate=estimate(count, model, neck, 1),
         compiler_params=LIMIT,
@@ -217,11 +229,13 @@
             pieces[k] = to_chip(piece, k) if k else piece
         arrived.append([pieces[k] for k in range(chips)])
 
+    weights = (norm_gain, norm_bias, convolution_taps, output_projection, proj_in)
+    token = load(convolution_taps, output_projection, proj_in)
     left = []
     for j in range(chunks):
-        x, narrow = enter(*arrived[j], norm_gain, norm_bias, proj_in)
-        weights = (norm_gain, norm_bias, convolution_taps, output_projection, proj_in)
-        x, narrow = slot_block(x, narrow, other_core(narrow), *weights)
+        x, narrow = enter(*arrived[j], norm_gain, norm_bias, proj_in, token)
+        partner = other_core(narrow)
+        x, narrow = slot_block(x, narrow, partner, *weights)
         partner = other_core(narrow)
         pieces = rest(x, narrow, partner, *weights)
         gone = {0: pieces[0]}

time: 133 us -> 132 us (level)
  waiting for transfers between devices: 43.9 us -> 39 us
  local copies, waits for them, and re-layouts: 6.81 us -> 10.2 us
    ppermute x28, waiting for transfers between devices: 43.9 us -> 39 us  [to_chip(): lax.ppermute(piece, 'blk', [(i, i ^ k * CORES) for i in range(peers)])]
    unnamed x16, local copies, waits for them, and re-layouts: 4.34 us -> 7.73 us
    pallas_call x4 -> x5, Pallas kernels: 7.79 us -> 7.81 us  [the longest x2 5.31 us: body(): x, narrow = slot_block(x, narrow, partner, *weights)]
  transfers between devices with their start and end apart: 32 -> 32, of which waited for: 9 -> 9; matrix products, arithmetic and copies ran while one was open for 0% -> 0% of each run, Pallas kernels for 15% -> 16%
where the time goes in v3:
time: 132 us; the launch traced here: 131 us
  starting transfers between devices  60.1 us (46%)
  waiting for transfers between devices  39 us (30%)
  Pallas kernels  21.7 us (16%)
  local copies, waits for them, and re-layouts  10.2 us (8%)
    ppermute x28, starting transfers between devices, to_chip(): lax.ppermute(piece, 'blk', [(i, i ^ k * CORES) for i in range(peers)])  59.4 us
    ppermute x28, waiting for transfers between devices, to_chip(): lax.ppermute(piece, 'blk', [(i, i ^ k * CORES) for i in range(peers)])  39 us
    pallas_call x2, Pallas kernels, body(): pieces = rest(x, narrow, partner, *weights)  13.9 us
    unnamed x16, local copies, waits for them, and re-layouts  7.73 us
    pallas_call x2, Pallas kernels, body(): x, narrow = slot_block(x, narrow, partner, *weights)  5.31 us
  transfers between devices with their start and end apart: 32, of which 9 were waited for; matrix products, arithmetic and copies ran while one was open for 0% of the time, Pallas kernels for 16%

profile of v3, /device:TPU:0, one launch (start us, length us, event | category | flops | bytes accessed | tf_op | source)
XLA Modules:
  0.0 131.4 jit_solution(2141525681857150235)
XLA Ops:
  0.0 2.0 %constant_dynamic-slice_fusion = (bf16[2,1,32,1024]{3,2,1,0:T(8,128)(2,1)S(1)}, bf16[2,1,32,1024]{3,2,1,0:T(8,128)(2,1)S(1)}, bf16[2,1,32,1024]{3,2,1,0:T(8,128)...) fusion(bf16[2,16,32,1024]{3,2,1,0:T(8,128)(2,1)} %bitcast.102, ...), kind=kLoop, calls=%fused_computation.8 | loop fusion | bytes 4194368 | tf_op jit(solution)/shard_map/dynamic_slice | solution.py:228
  2.0 3.1 %collective-permute-start = (bf16[64,1024]{1,0:T(8,128)(2,1)S(1)}, bf16[64,1024]{1,0:T(8,128)(2,1)S(1)}, u32[]{:S(2)}, u32[]{:S(2)}) collective-permute-start(bf16[64,1024]{1,0:T(8,128)(2,1)S(1)} %bitcast.116), channel_id=1, source_target_pairs={{0,2},{1,3},{2,0},{3,1},{4,6},{5,7},{6,4},{7,5},{8,10},{9,11},{10,... | collective-permute-start | bytes 393224 | tf_op jit(solution)/shard_map/ppermute | solution.py:169
  5.1 1.6 %collective-permute-start.1 = (bf16[64,1024]{1,0:T(8,128)(2,1)S(1)}, bf16[64,1024]{1,0:T(8,128)(2,1)S(1)}, u32[]{:S(2)}, u32[]{:S(2)}) collective-permute-start(bf16[64,1024]{1,0:T(8,128)(2,1)S(1)} %bitcast.115), channel_id=1, source_target_pairs={{0,4},{1,5},{2,6},{3,7},{4,0},{5,1},{6,2},{7,3},{8,12},{9,13},{10,... | collective-permute-start | bytes 393224 | tf_op jit(solution)/shard_map/ppermute | solution.py:169
  6.7 3.0 %collective-permute-start.3 = (bf16[64,1024]{1,0:T(8,128)(2,1)S(1)}, bf16[64,1024]{1,0:T(8,128)(2,1)S(1)}, u32[]{:S(2)}, u32[]{:S(2)}) collective-permute-start(bf16[64,1024]{1,0:T(8,128)(2,1)S(1)} %bitcast.113), channel_id=1, source_target_pairs={{0,8},{1,9},{2,10},{3,11},{4,12},{5,13},{6,14},{7,15},{8,0},{9,1},... | collective-permute-start | bytes 393224 | tf_op jit(solution)/shard_map/ppermute | solution.py:169
  9.6 1.3 collective-permute-start.4
  10.9 3.6 %collective-permute-start.5 = (bf16[64,1024]{1,0:T(8,128)(2,1)S(1)}, bf16[64,1024]{1,0:T(8,128)(2,1)S(1)}, u32[]{:S(2)}, u32[]{:S(2)}) collective-permute-start(bf16[64,1024]{1,0:T(8,128)(2,1)S(1)} %bitcast.111), channel_id=1, source_target_pairs={{0,12},{1,13},{2,14},{3,15},{4,8},{5,9},{6,10},{7,11},{8,4},{9,5},... | collective-permute-start | bytes 393224 | tf_op jit(solution)/shard_map/ppermute | solution.py:169
  14.5 1.3 %collective-permute-done.1.refs_2_ = bf16[64,1024]{1,0:T(8,128)(2,1)S(1)} collective-permute-done((bf16[64,1024]{1,0:T(8,128)(2,1)S(1)}, bf16[64,1024]{1,0:T(8,128)(2,1)S(1)}, u32[]{:S(2)}, u32[]{:S(2)}) %collective-permute-start.1) | collective-permute-done | bytes 131104 | tf_op jit(solution)/shard_map/ppermute | solution.py:169
  15.9 0.7 collective-permute-start.6
  16.5 2.8 %copy-done = bf16[4,3,512,512]{3,2,1,0:T(8,128)(2,1)S(1)} copy-done((bf16[4,3,512,512]{3,2,1,0:T(8,128)(2,1)S(1)}, bf16[4,3,512,512]{3,2,1,0:T(8,128)(2,1)}, u32[]{:S(2)}) %copy-start) | copy-done | bytes 6291480
  19.3 2.2 %copy-done.3 = bf16[4,512,1024]{2,1,0:T(8,128)(2,1)S(1)} copy-done((bf16[4,512,1024]{2,1,0:T(8,128)(2,1)S(1)}, bf16[4,512,1024]{2,1,0:T(8,128)(2,1)}, u32[]{:S(2)}) %copy-start.3) | copy-done | bytes 4194328
  21.5 7.6 %collective-permute-done.4.refs_5_ = bf16[64,1024]{1,0:T(8,128)(2,1)S(1)} collective-permute-done((bf16[64,1024]{1,0:T(8,128)(2,1)S(1)}, bf16[64,1024]{1,0:T(8,128)(2,1)S(1)}, u32[]{:S(2)}, u32[]{:S(2)}) %collective-permute-start.4) | collective-permute-done | bytes 131104 | tf_op jit(solution)/shard_map/ppermute | solution.py:169
  29.1 1.3 enter.2
  30.5 0.7 collective-permute-start.16
  31.2 4.7 %collective-permute-start.17 = (bf16[64,1024]{1,0:T(8,128)(2,1)S(1)}, bf16[64,1024]{1,0:T(8,128)(2,1)S(1)}, u32[]{:S(2)}, u32[]{:S(2)}) collective-permute-start(bf16[64,1024]{1,0:T(8,128)(2,1)S(1)} %bitcast.108), channel_id=1, source_target_pairs={{0,4},{1,5},{2,6},{3,7},{4,0},{5,1},{6,2},{7,3},{8,12},{9,13},{10,... | collective-permute-start | bytes 393224 | tf_op jit(solution)/shard_map/ppermute | solution.py:169
  35.9 1.1 collective-permute-start.18
  37.0 3.5 %collective-permute-start.19 = (bf16[64,1024]{1,0:T(8,128)(2,1)S(1)}, bf16[64,1024]{1,0:T(8,128)(2,1)S(1)}, u32[]{:S(2)}, u32[]{:S(2)}) collective-permute-start(bf16[64,1024]{1,0:T(8,128)(2,1)S(1)} %bitcast.106), channel_id=1, source_target_pairs={{0,8},{1,9},{2,10},{3,11},{4,12},{5,13},{6,14},{7,15},{8,0},{9,1},... | collective-permute-start | bytes 393224 | tf_op jit(solution)/shard_map/ppermute | solution.py:169
  40.6 2.3 %collective-permute-start.20 = (bf16[64,1024]{1,0:T(8,128)(2,1)S(1)}, bf16[64,1024]{1,0:T(8,128)(2,1)S(1)}, u32[]{:S(2)}, u32[]{:S(2)}) collective-permute-start(bf16[64,1024]{1,0:T(8,128)(2,1)S(1)} %bitcast.105), channel_id=1, source_target_pairs={{0,10},{1,11},{2,8},{3,9},{4,14},{5,15},{6,12},{7,13},{8,2},{9,3},... | collective-permute-start | bytes 393224 | tf_op jit(solution)/shard_map/ppermute | solution.py:169
  42.9 0.6 collective-permute-start.21
  43.5 4.7 %collective-permute-done.18.refs_3_ = bf16[64,1024]{1,0:T(8,128)(2,1)S(1)} collective-permute-done((bf16[64,1024]{1,0:T(8,128)(2,1)S(1)}, bf16[64,1024]{1,0:T(8,128)(2,1)S(1)}, u32[]{:S(2)}, u32[]{:S(2)}) %collective-permute-start.18) | collective-permute-done | bytes 131104 | tf_op jit(solution)/shard_map/ppermute | solution.py:169
  48.2 1.2 collective-permute-start.22
  49.4 10.4 %collective-permute-done.20.refs_5_ = bf16[64,1024]{1,0:T(8,128)(2,1)S(1)} collective-permute-done((bf16[64,1024]{1,0:T(8,128)(2,1)S(1)}, bf16[64,1024]{1,0:T(8,128)(2,1)S(1)}, u32[]{:S(2)}, u32[]{:S(2)}) %collective-permute-start.20) | collective-permute-done | bytes 131104 | tf_op jit(solution)/shard_map/ppermute | solution.py:169
  59.8 1.3 enter.3
  61.1 1.4 %copy-done.1 = bf16[4,3,512,512]{3,2,1,0:T(8,128)(2,1)S(1)} copy-done((bf16[4,3,512,512]{3,2,1,0:T(8,128)(2,1)S(1)}, bf16[4,3,512,512]{3,2,1,0:T(8,128)(2,1)}, u32[]{:S(2)}) %copy-start.1) | copy-done | bytes 6291480
  62.6 2.7 %slot_block.2 = (bf16[512,1024]{1,0:T(8,128)(2,1)S(1)}, bf16[512,512]{1,0:T(8,128)(2,1)S(1)}) custom-call(bf16[512,1024]{1,0:T(8,128)(2,1)S(1)} %get-tuple-element.29.x_in, bf16[512,512]{1,0:T(8,128)(2,1)S(1)} %get-tuple-element.30.narrow, bf16[512,512]{1,0:T(8,128)(2,1)S(1)} %collective-permute-done.7.partner, f32[4,1024]{1,0:T(4,128)S(1)} %copy-done.5, ...), custom_call_target="tpu_custom_call" | custom-call | flops 1879048192 | bytes 7864320 | tf_op jit(solution)/shard_map/slot_block/pallas_call | solution.py:238
  65.3 2.7 %slot_block.3 = (bf16[512,1024]{1,0:T(8,128)(2,1)S(1)}, bf16[512,512]{1,0:T(8,128)(2,1)S(1)}) custom-call(bf16[512,1024]{1,0:T(8,128)(2,1)S(1)} %get-tuple-element.41.x_in, bf16[512,512]{1,0:T(8,128)(2,1)S(1)} %get-tuple-element.42.narrow, bf16[512,512]{1,0:T(8,128)(2,1)S(1)} %collective-permute-done.23.partner, f32[4,1024]{1,0:T(4,128)S(1)} %copy-done.5, ...), custom_call_target="tpu_custom_call" | custom-call | flops 1879048192 | bytes 7864320 | tf_op jit(solution)/shard_map/slot_block/pallas_call | solution.py:238
  68.0 0.6 collective-permute-start.24
  68.5 7.1 %rest.2 = (bf16[64,1024]{1,0:T(8,128)(2,1)S(1)}, bf16[64,1024]{1,0:T(8,128)(2,1)S(1)}, bf16[64,1024]{1,0:T(8,128)(2,1)S(1)}, bf16[64,1024]{1,0:T(8,128)(2,1)S(1)...) custom-call(bf16[512,1024]{1,0:T(8,128)(2,1)S(1)} %get-tuple-element, ...), custom_call_target="tpu_custom_call" | custom-call | flops 5637144576 | bytes 15204352 | tf_op jit(solution)/shard_map/rest/pallas_call | solution.py:240
  75.6 4.8 %collective-permute-start.9 = (bf16[64,1024]{1,0:T(8,128)(2,1)S(1)}, bf16[64,1024]{1,0:T(8,128)(2,1)S(1)}, u32[]{:S(2)}, u32[]{:S(2)}) collective-permute-start(bf16[64,1024]{1,0:T(8,128)(2,1)S(1)} %get-tuple-element.34), channel_id=1, source_target_pairs={{0,4},{1,5},{2,6},{3,7},{4,0},{5,1},{6,2},{7,3},{8,12},{9,13},{10,... | collective-permute-start | bytes 393224 | tf_op jit(solution)/shard_map/ppermute | solution.py:169
  80.4 0.6 collective-permute-start.10
  81.0 2.4 %collective-permute-start.11 = (bf16[64,1024]{1,0:T(8,128)(2,1)S(1)}, bf16[64,1024]{1,0:T(8,128)(2,1)S(1)}, u32[]{:S(2)}, u32[]{:S(2)}) collective-permute-start(bf16[64,1024]{1,0:T(8,128)(2,1)S(1)} %get-tuple-element.36), channel_id=1, source_target_pairs={{0,12},{1,13},{2,14},{3,15},{4,8},{5,9},{6,10},{7,11},{8,4},{9,5},... | collective-permute-start | bytes 393224 | tf_op jit(solution)/shard_map/ppermute | solution.py:169
  83.3 1.9 %collective-permute-start.12 = (bf16[64,1024]{1,0:T(8,128)(2,1)S(1)}, bf16[64,1024]{1,0:T(8,128)(2,1)S(1)}, u32[]{:S(2)}, u32[]{:S(2)}) collective-permute-start(bf16[64,1024]{1,0:T(8,128)(2,1)S(1)} %get-tuple-element.37), channel_id=1, source_target_pairs={{0,14},{1,15},{2,12},{3,13},{4,10},{5,11},{6,8},{7,9},{8,6},{9,7},... | collective-permute-start | bytes 393224 | tf_op jit(solution)/shard_map/ppermute | solution.py:169
  85.2 0.6 collective-permute-start.13
  85.8 6.8 %rest.3 = (bf16[64,1024]{1,0:T(8,128)(2,1)S(1)}, bf16[64,1024]{1,0:T(8,128)(2,1)S(1)}, bf16[64,1024]{1,0:T(8,128)(2,1)S(1)}, bf16[64,1024]{1,0:T(8,128)(2,1)S(1)...) custom-call(bf16[512,1024]{1,0:T(8,128)(2,1)S(1)} %get-tuple-element, ...), custom_call_target="tpu_custom_call" | custom-call | flops 5637144576 | bytes 15204352 | tf_op jit(solution)/shard_map/rest/pallas_call | solution.py:240
  92.7 0.3 broadcast_in_dim.3
  93.0 2.8 %collective-permute-start.14 = (bf16[64,1024]{1,0:T(8,128)(2,1)S(1)}, bf16[64,1024]{1,0:T(8,128)(2,1)S(1)}, u32[]{:S(2)}, u32[]{:S(2)}) collective-permute-start(bf16[64,1024]{1,0:T(8,128)(2,1)S(1)} %get-tuple-element.39), channel_id=1, source_target_pairs={{0,10},{1,11},{2,8},{3,9},{4,14},{5,15},{6,12},{7,13},{8,2},{9,3},... | collective-permute-start | bytes 393224 | tf_op jit(solution)/shard_map/ppermute | solution.py:169
  95.8 1.0 collective-permute-start.15
  96.9 1.2 collective-permute-start.25
  98.1 6.7 %collective-permute-start.26 = (bf16[64,1024]{1,0:T(8,128)(2,1)S(1)}, bf16[64,1024]{1,0:T(8,128)(2,1)S(1)}, u32[]{:S(2)}, u32[]{:S(2)}) collective-permute-start(bf16[64,1024]{1,0:T(8,128)(2,1)S(1)} %get-tuple-element.47), channel_id=1, source_target_pairs={{0,6},{1,7},{2,4},{3,5},{4,2},{5,3},{6,0},{7,1},{8,14},{9,15},{10,... | collective-permute-start | bytes 393224 | tf_op jit(solution)/shard_map/ppermute | solution.py:169
  104.8 0.8 collective-permute-done.13
  105.6 2.4 %collective-permute-start.27 = (bf16[64,1024]{1,0:T(8,128)(2,1)S(1)}, bf16[64,1024]{1,0:T(8,128)(2,1)S(1)}, u32[]{:S(2)}, u32[]{:S(2)}) collective-permute-start(bf16[64,1024]{1,0:T(8,128)(2,1)S(1)} %get-tuple-element.48), channel_id=1, source_target_pairs={{0,12},{1,13},{2,14},{3,15},{4,8},{5,9},{6,10},{7,11},{8,4},{9,5},... | collective-permute-start | bytes 393224 | tf_op jit(solution)/shard_map/ppermute | solution.py:169
  108.0 2.1 %collective-permute-done.14 = bf16[64,1024]{1,0:T(8,128)(2,1)S(1)} collective-permute-done((bf16[64,1024]{1,0:T(8,128)(2,1)S(1)}, bf16[64,1024]{1,0:T(8,128)(2,1)S(1)}, u32[]{:S(2)}, u32[]{:S(2)}) %collective-permute-start.14) | collective-permute-done | bytes 131104 | tf_op jit(solution)/shard_map/ppermute | solution.py:169
  110.1 3.0 %collective-permute-start.28 = (bf16[64,1024]{1,0:T(8,128)(2,1)S(1)}, bf16[64,1024]{1,0:T(8,128)(2,1)S(1)}, u32[]{:S(2)}, u32[]{:S(2)}) collective-permute-start(bf16[64,1024]{1,0:T(8,128)(2,1)S(1)} %get-tuple-element.49), channel_id=1, source_target_pairs={{0,14},{1,15},{2,12},{3,13},{4,10},{5,11},{6,8},{7,9},{8,6},{9,7},... | collective-permute-start | bytes 393224 | tf_op jit(solution)/shard_map/ppermute | solution.py:169
  113.3 3.0 %collective-permute-start.30 = (bf16[64,1024]{1,0:T(8,128)(2,1)S(1)}, bf16[64,1024]{1,0:T(8,128)(2,1)S(1)}, u32[]{:S(2)}, u32[]{:S(2)}) collective-permute-start(bf16[64,1024]{1,0:T(8,128)(2,1)S(1)} %get-tuple-element.51), channel_id=1, source_target_pairs={{0,10},{1,11},{2,8},{3,9},{4,14},{5,15},{6,12},{7,13},{8,2},{9,3},... | collective-permute-start | bytes 393224 | tf_op jit(solution)/shard_map/ppermute | solution.py:169
  116.3 1.5 %collective-permute-start.31 = (bf16[64,1024]{1,0:T(8,128)(2,1)S(1)}, bf16[64,1024]{1,0:T(8,128)(2,1)S(1)}, u32[]{:S(2)}, u32[]{:S(2)}) collective-permute-start(bf16[64,1024]{1,0:T(8,128)(2,1)S(1)} %get-tuple-element.52), channel_id=1, source_target_pairs={{0,2},{1,3},{2,0},{3,1},{4,6},{5,7},{6,4},{7,5},{8,10},{9,11},{10,... | collective-permute-start | bytes 393224 | tf_op jit(solution)/shard_map/ppermute | solution.py:169
  117.9 0.6 collective-permute-done.28
  118.5 9.6 %collective-permute-done.29 = bf16[64,1024]{1,0:T(8,128)(2,1)S(1)} collective-permute-done((bf16[64,1024]{1,0:T(8,128)(2,1)S(1)}, bf16[64,1024]{1,0:T(8,128)(2,1)S(1)}, u32[]{:S(2)}, u32[]{:S(2)}) %collective-permute-start.29) | collective-permute-done | bytes 131104 | tf_op jit(solution)/shard_map/ppermute | solution.py:169
  128.0 2.0 %collective-permute-done.30 = bf16[64,1024]{1,0:T(8,128)(2,1)S(1)} collective-permute-done((bf16[64,1024]{1,0:T(8,128)(2,1)S(1)}, bf16[64,1024]{1,0:T(8,128)(2,1)S(1)}, u32[]{:S(2)}, u32[]{:S(2)}) %collective-permute-start.30) | collective-permute-done | bytes 131104 | tf_op jit(solution)/shard_map/ppermute | solution.py:169
  130.1 1.3 copy-done.7
  (57 shorter events, 0.6 us)
Async XLA Ops:
  0.0 16.5 %copy-start.2 = (bf16[4,1024,512]{2,1,0:T(8,128)(2,1)S(1)}, bf16[4,1024,512]{2,1,0:T(8,128)(2,1)}, u32[]{:S(2)}) copy-start(bf16[4,1024,512]{2,1,0:T(8,128)(2,1)} %proj.9) | copy-start | bytes 12582916
  2.0 8.9 %collective-permute-start = (bf16[64,1024]{1,0:T(8,128)(2,1)S(1)}, bf16[64,1024]{1,0:T(8,128)(2,1)S(1)}, u32[]{:S(2)}, u32[]{:S(2)}) collective-permute-start(bf16[64,1024]{1,0:T(8,128)(2,1)S(1)} %bitcast.116), channel_id=1, source_target_pairs={{0,2},{1,3},{2,0},{3,1},{4,6},{5,7},{6,4},{7,5},{8,10},{9,11},{10,... | collective-permute-start | bytes 393224 | tf_op jit(solution)/shard_map/ppermute | solution.py:169
  5.1 10.8 %collective-permute-start.1 = (bf16[64,1024]{1,0:T(8,128)(2,1)S(1)}, bf16[64,1024]{1,0:T(8,128)(2,1)S(1)}, u32[]{:S(2)}, u32[]{:S(2)}) collective-permute-start(bf16[64,1024]{1,0:T(8,128)(2,1)S(1)} %bitcast.115), channel_id=1, source_target_pairs={{0,4},{1,5},{2,6},{3,7},{4,0},{5,1},{6,2},{7,3},{8,12},{9,13},{10,... | collective-permute-start | bytes 393224 | tf_op jit(solution)/shard_map/ppermute | solution.py:169
  6.7 14.9 %collective-permute-start.2 = (bf16[64,1024]{1,0:T(8,128)(2,1)S(1)}, bf16[64,1024]{1,0:T(8,128)(2,1)S(1)}, u32[]{:S(2)}, u32[]{:S(2)}) collective-permute-start(bf16[64,1024]{1,0:T(8,128)(2,1)S(1)} %bitcast.114), channel_id=1, source_target_pairs={{0,6},{1,7},{2,4},{3,5},{4,2},{5,3},{6,0},{7,1},{8,14},{9,15},{10,... | collective-permute-start | bytes 393224 | tf_op jit(solution)/shard_map/ppermute | solution.py:169
  6.7 14.9 %collective-permute-start.3 = (bf16[64,1024]{1,0:T(8,128)(2,1)S(1)}, bf16[64,1024]{1,0:T(8,128)(2,1)S(1)}, u32[]{:S(2)}, u32[]{:S(2)}) collective-permute-start(bf16[64,1024]{1,0:T(8,128)(2,1)S(1)} %bitcast.113), channel_id=1, source_target_pairs={{0,8},{1,9},{2,10},{3,11},{4,12},{5,13},{6,14},{7,15},{8,0},{9,1},... | collective-permute-start | bytes 393224 | tf_op jit(solution)/shard_map/ppermute | solution.py:169
  9.6 19.4 %collective-permute-start.4 = (bf16[64,1024]{1,0:T(8,128)(2,1)S(1)}, bf16[64,1024]{1,0:T(8,128)(2,1)S(1)}, u32[]{:S(2)}, u32[]{:S(2)}) collective-permute-start(bf16[64,1024]{1,0:T(8,128)(2,1)S(1)} %bitcast.112), channel_id=1, source_target_pairs={{0,10},{1,11},{2,8},{3,9},{4,14},{5,15},{6,12},{7,13},{8,2},{9,3},... | collective-permute-start | bytes 393224 | tf_op jit(solution)/shard_map/ppermute | solution.py:169
  10.9 18.2 %collective-permute-start.5 = (bf16[64,1024]{1,0:T(8,128)(2,1)S(1)}, bf16[64,1024]{1,0:T(8,128)(2,1)S(1)}, u32[]{:S(2)}, u32[]{:S(2)}) collective-permute-start(bf16[64,1024]{1,0:T(8,128)(2,1)S(1)} %bitcast.111), channel_id=1, source_target_pairs={{0,12},{1,13},{2,14},{3,15},{4,8},{5,9},{6,10},{7,11},{8,4},{9,5},... | collective-permute-start | bytes 393224 | tf_op jit(solution)/shard_map/ppermute | solution.py:169
  15.9 13.2 %collective-permute-start.6 = (bf16[64,1024]{1,0:T(8,128)(2,1)S(1)}, bf16[64,1024]{1,0:T(8,128)(2,1)S(1)}, u32[]{:S(2)}, u32[]{:S(2)}) collective-permute-start(bf16[64,1024]{1,0:T(8,128)(2,1)S(1)} %bitcast.110), channel_id=1, source_target_pairs={{0,14},{1,15},{2,12},{3,13},{4,10},{5,11},{6,8},{7,9},{8,6},{9,7},... | collective-permute-start | bytes 393224 | tf_op jit(solution)/shard_map/ppermute | solution.py:169
  16.5 2.8 %copy-start = (bf16[4,3,512,512]{3,2,1,0:T(8,128)(2,1)S(1)}, bf16[4,3,512,512]{3,2,1,0:T(8,128)(2,1)}, u32[]{:S(2)}) copy-start(bf16[4,3,512,512]{3,2,1,0:T(8,128)(2,1)} %taps.9) | copy-start | bytes 18874372
  19.3 2.2 %copy-start.3 = (bf16[4,512,1024]{2,1,0:T(8,128)(2,1)S(1)}, bf16[4,512,1024]{2,1,0:T(8,128)(2,1)}, u32[]{:S(2)}) copy-start(bf16[4,512,1024]{2,1,0:T(8,128)(2,1)} %output.9) | copy-start | bytes 12582916
  21.5 7.6 %copy-start.5 = (f32[4,1024]{1,0:T(4,128)S(1)}, f32[4,1024]{1,0:T(4,128)}, u32[]{:S(2)}) copy-start(f32[4,1024]{1,0:T(4,128)} %gain.7) | copy-start | bytes 49156
  21.5 7.6 %copy-start.6 = (f32[4,1024]{1,0:T(4,128)S(1)}, f32[4,1024]{1,0:T(4,128)}, u32[]{:S(2)}) copy-start(f32[4,1024]{1,0:T(4,128)} %bias.7) | copy-start | bytes 49156
  29.1 32.0 %copy-start.4 = (bf16[4,512,1024]{2,1,0:T(8,128)(2,1)S(1)}, bf16[4,512,1024]{2,1,0:T(8,128)(2,1)}, u32[]{:S(2)}) copy-start(bf16[4,512,1024]{2,1,0:T(8,128)(2,1)} %output.9) | copy-start | bytes 12582916
  30.4 30.7 %collective-permute-start.7 = (bf16[512,512]{1,0:T(8,128)(2,1)S(1)}, bf16[512,512]{1,0:T(8,128)(2,1)S(1)}, u32[]{:S(2)}, u32[]{:S(2)}) collective-permute-start(bf16[512,512]{1,0:T(8,128)(2,1)S(1)} %get-tuple-element.30.narrow), channel_id=1, source_target_pairs={{0,1},{1,0},{2,3},{3,2},{4,5},{5,4},{6,7},{7,6},{8,9},{9,8},{10,11... | collective-permute-start | bytes 1572872 | tf_op jit(solution)/shard_map/ppermute | solution.py:172
  30.5 10.1 %collective-permute-start.16 = (bf16[64,1024]{1,0:T(8,128)(2,1)S(1)}, bf16[64,1024]{1,0:T(8,128)(2,1)S(1)}, u32[]{:S(2)}, u32[]{:S(2)}) collective-permute-start(bf16[64,1024]{1,0:T(8,128)(2,1)S(1)} %bitcast.109), channel_id=1, source_target_pairs={{0,2},{1,3},{2,0},{3,1},{4,6},{5,7},{6,4},{7,5},{8,10},{9,11},{10,... | collective-permute-start | bytes 393224 | tf_op jit(solution)/shard_map/ppermute | solution.py:169
  31.2 11.7 %collective-permute-start.17 = (bf16[64,1024]{1,0:T(8,128)(2,1)S(1)}, bf16[64,1024]{1,0:T(8,128)(2,1)S(1)}, u32[]{:S(2)}, u32[]{:S(2)}) collective-permute-start(bf16[64,1024]{1,0:T(8,128)(2,1)S(1)} %bitcast.108), channel_id=1, source_target_pairs={{0,4},{1,5},{2,6},{3,7},{4,0},{5,1},{6,2},{7,3},{8,12},{9,13},{10,... | collective-permute-start | bytes 393224 | tf_op jit(solution)/shard_map/ppermute | solution.py:169
  35.9 12.3 %collective-permute-start.18 = (bf16[64,1024]{1,0:T(8,128)(2,1)S(1)}, bf16[64,1024]{1,0:T(8,128)(2,1)S(1)}, u32[]{:S(2)}, u32[]{:S(2)}) collective-permute-start(bf16[64,1024]{1,0:T(8,128)(2,1)S(1)} %bitcast.107), channel_id=1, source_target_pairs={{0,6},{1,7},{2,4},{3,5},{4,2},{5,3},{6,0},{7,1},{8,14},{9,15},{10,... | collective-permute-start | bytes 393224 | tf_op jit(solution)/shard_map/ppermute | solution.py:169
  37.0 12.3 %collective-permute-start.19 = (bf16[64,1024]{1,0:T(8,128)(2,1)S(1)}, bf16[64,1024]{1,0:T(8,128)(2,1)S(1)}, u32[]{:S(2)}, u32[]{:S(2)}) collective-permute-start(bf16[64,1024]{1,0:T(8,128)(2,1)S(1)} %bitcast.106), channel_id=1, source_target_pairs={{0,8},{1,9},{2,10},{3,11},{4,12},{5,13},{6,14},{7,15},{8,0},{9,1},... | collective-permute-start | bytes 393224 | tf_op jit(solution)/shard_map/ppermute | solution.py:169
  40.6 19.2 %collective-permute-start.20 = (bf16[64,1024]{1,0:T(8,128)(2,1)S(1)}, bf16[64,1024]{1,0:T(8,128)(2,1)S(1)}, u32[]{:S(2)}, u32[]{:S(2)}) collective-permute-start(bf16[64,1024]{1,0:T(8,128)(2,1)S(1)} %bitcast.105), channel_id=1, source_target_pairs={{0,10},{1,11},{2,8},{3,9},{4,14},{5,15},{6,12},{7,13},{8,2},{9,3},... | collective-permute-start | bytes 393224 | tf_op jit(solution)/shard_map/ppermute | solution.py:169
  42.9 16.9 %collective-permute-start.21 = (bf16[64,1024]{1,0:T(8,128)(2,1)S(1)}, bf16[64,1024]{1,0:T(8,128)(2,1)S(1)}, u32[]{:S(2)}, u32[]{:S(2)}) collective-permute-start(bf16[64,1024]{1,0:T(8,128)(2,1)S(1)} %bitcast.104), channel_id=1, source_target_pairs={{0,12},{1,13},{2,14},{3,15},{4,8},{5,9},{6,10},{7,11},{8,4},{9,5},... | collective-permute-start | bytes 393224 | tf_op jit(solution)/shard_map/ppermute | solution.py:169
  48.2 11.6 %collective-permute-start.22 = (bf16[64,1024]{1,0:T(8,128)(2,1)S(1)}, bf16[64,1024]{1,0:T(8,128)(2,1)S(1)}, u32[]{:S(2)}, u32[]{:S(2)}) collective-permute-start(bf16[64,1024]{1,0:T(8,128)(2,1)S(1)} %bitcast.103), channel_id=1, source_target_pairs={{0,14},{1,15},{2,12},{3,13},{4,10},{5,11},{6,8},{7,9},{8,6},{9,7},... | collective-permute-start | bytes 393224 | tf_op jit(solution)/shard_map/ppermute | solution.py:169
  59.8 2.8 %copy-start.1 = (bf16[4,3,512,512]{3,2,1,0:T(8,128)(2,1)S(1)}, bf16[4,3,512,512]{3,2,1,0:T(8,128)(2,1)}, u32[]{:S(2)}) copy-start(bf16[4,3,512,512]{3,2,1,0:T(8,128)(2,1)} %taps.9) | copy-start | bytes 18874372
  61.0 4.3 %collective-permute-start.23 = (bf16[512,512]{1,0:T(8,128)(2,1)S(1)}, bf16[512,512]{1,0:T(8,128)(2,1)S(1)}, u32[]{:S(2)}, u32[]{:S(2)}) collective-permute-start(bf16[512,512]{1,0:T(8,128)(2,1)S(1)} %get-tuple-element.42.narrow), channel_id=1, source_target_pairs={{0,1},{1,0},{2,3},{3,2},{4,5},{5,4},{6,7},{7,6},{8,9},{9,8},{10,11... | collective-permute-start | bytes 1572872 | tf_op jit(solution)/shard_map/ppermute | solution.py:172
  65.2 3.3 %collective-permute-start.8 = (bf16[512,512]{1,0:T(8,128)(2,1)S(1)}, bf16[512,512]{1,0:T(8,128)(2,1)S(1)}, u32[]{:S(2)}, u32[]{:S(2)}) collective-permute-start(bf16[512,512]{1,0:T(8,128)(2,1)S(1)} %get-tuple-element.32.narrow), channel_id=1, source_target_pairs={{0,1},{1,0},{2,3},{3,2},{4,5},{5,4},{6,7},{7,6},{8,9},{9,8},{10,11... | collective-permute-start | bytes 1572872 | tf_op jit(solution)/shard_map/ppermute | solution.py:172
  68.0 17.2 %collective-permute-start.24 = (bf16[512,512]{1,0:T(8,128)(2,1)S(1)}, bf16[512,512]{1,0:T(8,128)(2,1)S(1)}, u32[]{:S(2)}, u32[]{:S(2)}) collective-permute-start(bf16[512,512]{1,0:T(8,128)(2,1)S(1)} %get-tuple-element.44.narrow), channel_id=1, source_target_pairs={{0,1},{1,0},{2,3},{3,2},{4,5},{5,4},{6,7},{7,6},{8,9},{9,8},{10,11... | collective-permute-start | bytes 1572872 | tf_op jit(solution)/shard_map/ppermute | solution.py:172
  75.6 17.4 %collective-permute-start.9 = (bf16[64,1024]{1,0:T(8,128)(2,1)S(1)}, bf16[64,1024]{1,0:T(8,128)(2,1)S(1)}, u32[]{:S(2)}, u32[]{:S(2)}) collective-permute-start(bf16[64,1024]{1,0:T(8,128)(2,1)S(1)} %get-tuple-element.34), channel_id=1, source_target_pairs={{0,4},{1,5},{2,6},{3,7},{4,0},{5,1},{6,2},{7,3},{8,12},{9,13},{10,... | collective-permute-start | bytes 393224 | tf_op jit(solution)/shard_map/ppermute | solution.py:169
  80.4 15.4 %collective-permute-start.10 = (bf16[64,1024]{1,0:T(8,128)(2,1)S(1)}, bf16[64,1024]{1,0:T(8,128)(2,1)S(1)}, u32[]{:S(2)}, u32[]{:S(2)}) collective-permute-start(bf16[64,1024]{1,0:T(8,128)(2,1)S(1)} %get-tuple-element.35), channel_id=1, source_target_pairs={{0,6},{1,7},{2,4},{3,5},{4,2},{5,3},{6,0},{7,1},{8,14},{9,15},{10,... | collective-permute-start | bytes 393224 | tf_op jit(solution)/shard_map/ppermute | solution.py:169
  81.0 15.9 %collective-permute-start.11 = (bf16[64,1024]{1,0:T(8,128)(2,1)S(1)}, bf16[64,1024]{1,0:T(8,128)(2,1)S(1)}, u32[]{:S(2)}, u32[]{:S(2)}) collective-permute-start(bf16[64,1024]{1,0:T(8,128)(2,1)S(1)} %get-tuple-element.36), channel_id=1, source_target_pairs={{0,12},{1,13},{2,14},{3,15},{4,8},{5,9},{6,10},{7,11},{8,4},{9,5},... | collective-permute-start | bytes 393224 | tf_op jit(solution)/shard_map/ppermute | solution.py:169
  83.3 14.8 %collective-permute-start.12 = (bf16[64,1024]{1,0:T(8,128)(2,1)S(1)}, bf16[64,1024]{1,0:T(8,128)(2,1)S(1)}, u32[]{:S(2)}, u32[]{:S(2)}) collective-permute-start(bf16[64,1024]{1,0:T(8,128)(2,1)S(1)} %get-tuple-element.37), channel_id=1, source_target_pairs={{0,14},{1,15},{2,12},{3,13},{4,10},{5,11},{6,8},{7,9},{8,6},{9,7},... | collective-permute-start | bytes 393224 | tf_op jit(solution)/shard_map/ppermute | solution.py:169
  85.2 20.4 %collective-permute-start.13 = (bf16[64,1024]{1,0:T(8,128)(2,1)S(1)}, bf16[64,1024]{1,0:T(8,128)(2,1)S(1)}, u32[]{:S(2)}, u32[]{:S(2)}) collective-permute-start(bf16[64,1024]{1,0:T(8,128)(2,1)S(1)} %get-tuple-element.38), channel_id=1, source_target_pairs={{0,8},{1,9},{2,10},{3,11},{4,12},{5,13},{6,14},{7,15},{8,0},{9,1},... | collective-permute-start | bytes 393224 | tf_op jit(solution)/shard_map/ppermute | solution.py:169
  93.0 17.1 %collective-permute-start.14 = (bf16[64,1024]{1,0:T(8,128)(2,1)S(1)}, bf16[64,1024]{1,0:T(8,128)(2,1)S(1)}, u32[]{:S(2)}, u32[]{:S(2)}) collective-permute-start(bf16[64,1024]{1,0:T(8,128)(2,1)S(1)} %get-tuple-element.39), channel_id=1, source_target_pairs={{0,10},{1,11},{2,8},{3,9},{4,14},{5,15},{6,12},{7,13},{8,2},{9,3},... | collective-permute-start | bytes 393224 | tf_op jit(solution)/shard_map/ppermute | solution.py:169
  95.8 17.3 %collective-permute-start.15 = (bf16[64,1024]{1,0:T(8,128)(2,1)S(1)}, bf16[64,1024]{1,0:T(8,128)(2,1)S(1)}, u32[]{:S(2)}, u32[]{:S(2)}) collective-permute-start(bf16[64,1024]{1,0:T(8,128)(2,1)S(1)} %get-tuple-element.40), channel_id=1, source_target_pairs={{0,2},{1,3},{2,0},{3,1},{4,6},{5,7},{6,4},{7,5},{8,10},{9,11},{10,... | collective-permute-start | bytes 393224 | tf_op jit(solution)/shard_map/ppermute | solution.py:169
  96.9 16.4 %collective-permute-start.25 = (bf16[64,1024]{1,0:T(8,128)(2,1)S(1)}, bf16[64,1024]{1,0:T(8,128)(2,1)S(1)}, u32[]{:S(2)}, u32[]{:S(2)}) collective-permute-start(bf16[64,1024]{1,0:T(8,128)(2,1)S(1)} %get-tuple-element.46), channel_id=1, source_target_pairs={{0,4},{1,5},{2,6},{3,7},{4,0},{5,1},{6,2},{7,3},{8,12},{9,13},{10,... | collective-permute-start | bytes 393224 | tf_op jit(solution)/shard_map/ppermute | solution.py:169
  98.1 18.2 %collective-permute-start.26 = (bf16[64,1024]{1,0:T(8,128)(2,1)S(1)}, bf16[64,1024]{1,0:T(8,128)(2,1)S(1)}, u32[]{:S(2)}, u32[]{:S(2)}) collective-permute-start(bf16[64,1024]{1,0:T(8,128)(2,1)S(1)} %get-tuple-element.47), channel_id=1, source_target_pairs={{0,6},{1,7},{2,4},{3,5},{4,2},{5,3},{6,0},{7,1},{8,14},{9,15},{10,... | collective-permute-start | bytes 393224 | tf_op jit(solution)/shard_map/ppermute | solution.py:169
  105.6 12.2 %collective-permute-start.27 = (bf16[64,1024]{1,0:T(8,128)(2,1)S(1)}, bf16[64,1024]{1,0:T(8,128)(2,1)S(1)}, u32[]{:S(2)}, u32[]{:S(2)}) collective-permute-start(bf16[64,1024]{1,0:T(8,128)(2,1)S(1)} %get-tuple-element.48), channel_id=1, source_target_pairs={{0,12},{1,13},{2,14},{3,15},{4,8},{5,9},{6,10},{7,11},{8,4},{9,5},... | collective-permute-start | bytes 393224 | tf_op jit(solution)/shard_map/ppermute | solution.py:169
  110.1 8.3 %collective-permute-start.28 = (bf16[64,1024]{1,0:T(8,128)(2,1)S(1)}, bf16[64,1024]{1,0:T(8,128)(2,1)S(1)}, u32[]{:S(2)}, u32[]{:S(2)}) collective-permute-start(bf16[64,1024]{1,0:T(8,128)(2,1)S(1)} %get-tuple-element.49), channel_id=1, source_target_pairs={{0,14},{1,15},{2,12},{3,13},{4,10},{5,11},{6,8},{7,9},{8,6},{9,7},... | collective-permute-start | bytes 393224 | tf_op jit(solution)/shard_map/ppermute | solution.py:169
  113.2 14.9 %collective-permute-start.29 = (bf16[64,1024]{1,0:T(8,128)(2,1)S(1)}, bf16[64,1024]{1,0:T(8,128)(2,1)S(1)}, u32[]{:S(2)}, u32[]{:S(2)}) collective-permute-start(bf16[64,1024]{1,0:T(8,128)(2,1)S(1)} %get-tuple-element.50), channel_id=1, source_target_pairs={{0,8},{1,9},{2,10},{3,11},{4,12},{5,13},{6,14},{7,15},{8,0},{9,1},... | collective-permute-start | bytes 393224 | tf_op jit(solution)/shard_map/ppermute | solution.py:169
  113.3 16.7 %collective-permute-start.30 = (bf16[64,1024]{1,0:T(8,128)(2,1)S(1)}, bf16[64,1024]{1,0:T(8,128)(2,1)S(1)}, u32[]{:S(2)}, u32[]{:S(2)}) collective-permute-start(bf16[64,1024]{1,0:T(8,128)(2,1)S(1)} %get-tuple-element.51), channel_id=1, source_target_pairs={{0,10},{1,11},{2,8},{3,9},{4,14},{5,15},{6,12},{7,13},{8,2},{9,3},... | collective-permute-start | bytes 393224 | tf_op jit(solution)/shard_map/ppermute | solution.py:169
  116.3 13.7 %collective-permute-start.31 = (bf16[64,1024]{1,0:T(8,128)(2,1)S(1)}, bf16[64,1024]{1,0:T(8,128)(2,1)S(1)}, u32[]{:S(2)}, u32[]{:S(2)}) collective-permute-start(bf16[64,1024]{1,0:T(8,128)(2,1)S(1)} %get-tuple-element.52), channel_id=1, source_target_pairs={{0,2},{1,3},{2,0},{3,1},{4,6},{5,7},{6,4},{7,5},{8,10},{9,11},{10,... | collective-permute-start | bytes 393224 | tf_op jit(solution)/shard_map/ppermute | solution.py:169
  130.1 1.3 %copy-start.7 = (bf16[2,16,32,1024]{3,2,1,0:T(8,128)(2,1)}, bf16[2,16,32,1024]{3,2,1,0:T(8,128)(2,1)S(1)}, u32[]{:S(2)}) copy-start(bf16[2,16,32,1024]{3,2,1,0:T(8,128)(2,1)S(1)} %constant_dynamic-update-slice_fusion) | copy-start | bytes 6291460

commit v4 on v3

--- a/solution.py
+++ b/solution.py
@@ -133,6 +133,24 @@
         pieces[k][...] = x_ref[pl.ds(pl.multiple_of((chip ^ k) * width, width), width), :]
 
 
+def collect_kernel(chips, slots, part, chunks, chunk, *refs):
+    pieces, (result, sems) = refs[:chips], refs[-2:]
+    chip, _ = position()
+    copies = [
+        pltpu.make_async_copy(
+            pieces[k].at[pl.ds(slot * part, part), :],
+            result.at[slot, (chip ^ k) * chunks + chunk],
+            sems.at[k, slot],
+        )
+        for k in range(chips)
+        for slot in range(slots)
+    ]
+    for copy in copies:
+        copy.start()
+    for copy in copies:
+        copy.wait()
+
+
 def estimate(rows, model, neck, blocks):
     return pl.CostEstimate(
         flops=2 * rows * blocks * (2 * model * neck + 3 * neck * neck),
@@ -144,7 +162,12 @@
 def travel_order(chips):
     half = chips // 2
     far = sorted(range(max(2, half), chips), key=lambda k: (-(k >> 1), k))
-    return [*range(2, half), *far, *range(1, min(2, chips))]
+    return list(range(2, half)), far, list(range(1, min(2, chips)))
+
+
+def leave_order(chips):
+    near, far, next_to = travel_order(chips)
+    return far[:2] + near + far[2:] + next_to
 
 
 def chunk_count(chips):
@@ -224,7 +247,8 @@
     arrived = []
     for j in range(chunks):
         pieces = {}
-        for k in [0, *travel_order(chips)]:
+        grid = lax.optimization_barrier(grid)
+        for k in [0, *leave_order(chips)]:
             piece = lax.dynamic_slice_in_dim(grid, (chip ^ k) * chunks + j, 1, axis=1).reshape(width, model)
             pieces[k] = to_chip(piece, k) if k else piece
         arrived.append([pieces[k] for k in range(chips)])
@@ -239,15 +263,23 @@
         partner = other_core(narrow)
         pieces = rest(x, narrow, partner, *weights)
         gone = {0: pieces[0]}
-        for k in travel_order(chips):
+        for k in leave_order(chips):
             gone[k] = to_chip(pieces[k], k)
         left.append(gone)
 
-    result = jnp.zeros(grid.shape, bf16)
+    result = None
     for j in range(chunks):
-        for k in [0, *travel_order(chips)]:
-            piece = left[j][k].reshape(slots, 1, part, model)
-            result = lax.dynamic_update_slice_in_dim(result, piece, (chip ^ k) * chunks + j, axis=1)
+        collect = pl.pallas_call(
+            functools.partial(collect_kernel, chips, slots, part, chunks, j),
+            out_shape=shape(grid.shape, bf16),
+            in_specs=[VMEM] * chips + [pl.BlockSpec(memory_space=pl.ANY)] * (j > 0),
+            out_specs=pl.BlockSpec(memory_space=pl.ANY),
+            scratch_shapes=[pltpu.SemaphoreType.DMA((chips, slots))],
+            input_output_aliases={chips: 0} if j else {},
+            compiler_params=LIMIT,
+            name="collect",
+        )
+        result = collect(*[left[j][k] for k in range(chips)], *([result] if j else []))
     return result.reshape(rows, model)
 
 

time: 132 us -> 139 us (1.053)
  the two profiles are of different devices: /device:TPU:0 before, /device:TPU:16 now
where the time goes in v4:
time: 139 us; the launch traced here: 138 us
  waiting for transfers between devices  63.8 us (46%)
  starting transfers between devices  40 us (29%)
  Pallas kernels  23.9 us (17%)
  local copies, waits for them, and re-layouts  10.4 us (7%)
    ppermute x28, waiting for transfers between devices, to_chip(): lax.ppermute(piece, 'blk', [(i, i ^ k * CORES) for i in range(peers)])  63.7 us
    ppermute x28, starting transfers between devices, to_chip(): lax.ppermute(piece, 'blk', [(i, i ^ k * CORES) for i in range(peers)])  39.2 us
    pallas_call x2, Pallas kernels, body(): pieces = rest(x, narrow, partner, *weights)  13.9 us
    unnamed x18, local copies, waits for them, and re-layouts  8.92 us
    pallas_call x2, Pallas kernels, body(): x, narrow = slot_block(x, narrow, partner, *weights)  5.3 us
  transfers between devices with their start and end apart: 32, of which 17 were waited for; matrix products, arithmetic and copies ran while one was open for 0% of the time, Pallas kernels for 16%

profile of v4, /device:TPU:16, one launch (start us, length us, event | category | flops | bytes accessed | tf_op | source)
XLA Modules:
  0.0 138.4 jit_solution(16096871933710474391)
XLA Ops:
  0.0 1.4 constant_dynamic-slice_fusion.8
  1.9 2.5 %collective-permute-start.6 = (bf16[64,1024]{1,0:T(8,128)(2,1)S(1)}, bf16[64,1024]{1,0:T(8,128)(2,1)S(1)}, u32[]{:S(2)}, u32[]{:S(2)}) collective-permute-start(bf16[64,1024]{1,0:T(8,128)(2,1)S(1)} %bitcast.66), channel_id=1, source_target_pairs={{0,14},{1,15},{2,12},{3,13},{4,10},{5,11},{6,8},{7,9},{8,6},{9,7},... | collective-permute-start | bytes 393224 | tf_op jit(solution)/shard_map/ppermute | solution.py:192
  4.4 1.9 %collective-permute-start.4 = (bf16[64,1024]{1,0:T(8,128)(2,1)S(1)}, bf16[64,1024]{1,0:T(8,128)(2,1)S(1)}, u32[]{:S(2)}, u32[]{:S(2)}) collective-permute-start(bf16[64,1024]{1,0:T(8,128)(2,1)S(1)} %bitcast.60), channel_id=1, source_target_pairs={{0,10},{1,11},{2,8},{3,9},{4,14},{5,15},{6,12},{7,13},{8,2},{9,3},... | collective-permute-start | bytes 393224 | tf_op jit(solution)/shard_map/ppermute | solution.py:192
  6.4 0.9 collective-permute-start.3
  7.3 4.3 %collective-permute-start.2 = (bf16[64,1024]{1,0:T(8,128)(2,1)S(1)}, bf16[64,1024]{1,0:T(8,128)(2,1)S(1)}, u32[]{:S(2)}, u32[]{:S(2)}) collective-permute-start(bf16[64,1024]{1,0:T(8,128)(2,1)S(1)} %bitcast.58), channel_id=1, source_target_pairs={{0,6},{1,7},{2,4},{3,5},{4,2},{5,3},{6,0},{7,1},{8,14},{9,15},{10,... | collective-permute-start | bytes 393224 | tf_op jit(solution)/shard_map/ppermute | solution.py:192
  11.6 7.4 %collective-permute-done.5.refs_6_ = bf16[64,1024]{1,0:T(8,128)(2,1)S(1)} collective-permute-done((bf16[64,1024]{1,0:T(8,128)(2,1)S(1)}, bf16[64,1024]{1,0:T(8,128)(2,1)S(1)}, u32[]{:S(2)}, u32[]{:S(2)}) %collective-permute-start.5) | collective-permute-done | bytes 131104 | tf_op jit(solution)/shard_map/ppermute | solution.py:192
  19.1 3.8 %collective-permute-done.6.refs_7_ = bf16[64,1024]{1,0:T(8,128)(2,1)S(1)} collective-permute-done((bf16[64,1024]{1,0:T(8,128)(2,1)S(1)}, bf16[64,1024]{1,0:T(8,128)(2,1)S(1)}, u32[]{:S(2)}, u32[]{:S(2)}) %collective-permute-start.6) | collective-permute-done | bytes 131104 | tf_op jit(solution)/shard_map/ppermute | solution.py:192
  23.3 2.8 %copy-done = bf16[4,3,512,512]{3,2,1,0:T(8,128)(2,1)S(1)} copy-done((bf16[4,3,512,512]{3,2,1,0:T(8,128)(2,1)S(1)}, bf16[4,3,512,512]{3,2,1,0:T(8,128)(2,1)}, u32[]{:S(2)}) %copy-start) | copy-done | bytes 6291480
  26.1 2.2 %copy-done.1 = bf16[4,1024,512]{2,1,0:T(8,128)(2,1)S(1)} copy-done((bf16[4,1024,512]{2,1,0:T(8,128)(2,1)S(1)}, bf16[4,1024,512]{2,1,0:T(8,128)(2,1)}, u32[]{:S(2)}) %copy-start.1) | copy-done | bytes 4194328
  28.3 2.2 %copy-done.2 = bf16[4,512,1024]{2,1,0:T(8,128)(2,1)S(1)} copy-done((bf16[4,512,1024]{2,1,0:T(8,128)(2,1)S(1)}, bf16[4,512,1024]{2,1,0:T(8,128)(2,1)}, u32[]{:S(2)}) %copy-start.2) | copy-done | bytes 4194328
  30.5 0.7 copy-done.4
  31.2 1.2 enter.2
  32.9 0.7 collective-permute-start.21
  33.6 2.4 %collective-permute-start.22 = (bf16[64,1024]{1,0:T(8,128)(2,1)S(1)}, bf16[64,1024]{1,0:T(8,128)(2,1)S(1)}, u32[]{:S(2)}, u32[]{:S(2)}) collective-permute-start(bf16[64,1024]{1,0:T(8,128)(2,1)S(1)} %bitcast.67), channel_id=1, source_target_pairs={{0,14},{1,15},{2,12},{3,13},{4,10},{5,11},{6,8},{7,9},{8,6},{9,7},... | collective-permute-start | bytes 393224 | tf_op jit(solution)/shard_map/ppermute | solution.py:192
  36.0 0.7 collective-permute-start.20
  36.7 2.1 %collective-permute-start.19 = (bf16[64,1024]{1,0:T(8,128)(2,1)S(1)}, bf16[64,1024]{1,0:T(8,128)(2,1)S(1)}, u32[]{:S(2)}, u32[]{:S(2)}) collective-permute-start(bf16[64,1024]{1,0:T(8,128)(2,1)S(1)} %bitcast.64), channel_id=1, source_target_pairs={{0,8},{1,9},{2,10},{3,11},{4,12},{5,13},{6,14},{7,15},{8,0},{9,1},... | collective-permute-start | bytes 393224 | tf_op jit(solution)/shard_map/ppermute | solution.py:192
  38.8 10.7 %collective-permute-done.21.refs_6_ = bf16[64,1024]{1,0:T(8,128)(2,1)S(1)} collective-permute-done((bf16[64,1024]{1,0:T(8,128)(2,1)S(1)}, bf16[64,1024]{1,0:T(8,128)(2,1)S(1)}, u32[]{:S(2)}, u32[]{:S(2)}) %collective-permute-start.21) | collective-permute-done | bytes 131104 | tf_op jit(solution)/shard_map/ppermute | solution.py:192
  49.6 2.8 %collective-permute-done.22.refs_7_ = bf16[64,1024]{1,0:T(8,128)(2,1)S(1)} collective-permute-done((bf16[64,1024]{1,0:T(8,128)(2,1)S(1)}, bf16[64,1024]{1,0:T(8,128)(2,1)S(1)}, u32[]{:S(2)}, u32[]{:S(2)}) %collective-permute-start.22) | collective-permute-done | bytes 131104 | tf_op jit(solution)/shard_map/ppermute | solution.py:192
  52.3 0.7 collective-permute-done.20.refs_5_
  53.0 1.0 collective-permute-start.16
  54.1 1.7 %collective-permute-done.19.refs_4_ = bf16[64,1024]{1,0:T(8,128)(2,1)S(1)} collective-permute-done((bf16[64,1024]{1,0:T(8,128)(2,1)S(1)}, bf16[64,1024]{1,0:T(8,128)(2,1)S(1)}, u32[]{:S(2)}, u32[]{:S(2)}) %collective-permute-start.19) | collective-permute-done | bytes 131104 | tf_op jit(solution)/shard_map/ppermute | solution.py:192
  55.8 3.3 %collective-permute-done.18.refs_3_ = bf16[64,1024]{1,0:T(8,128)(2,1)S(1)} collective-permute-done((bf16[64,1024]{1,0:T(8,128)(2,1)S(1)}, bf16[64,1024]{1,0:T(8,128)(2,1)S(1)}, u32[]{:S(2)}, u32[]{:S(2)}) %collective-permute-start.18) | collective-permute-done | bytes 131104 | tf_op jit(solution)/shard_map/ppermute | solution.py:192
  59.1 2.1 %collective-permute-done.17.refs_2_ = bf16[64,1024]{1,0:T(8,128)(2,1)S(1)} collective-permute-done((bf16[64,1024]{1,0:T(8,128)(2,1)S(1)}, bf16[64,1024]{1,0:T(8,128)(2,1)S(1)}, u32[]{:S(2)}, u32[]{:S(2)}) %collective-permute-start.17) | collective-permute-done | bytes 131104 | tf_op jit(solution)/shard_map/ppermute | solution.py:192
  61.2 1.3 enter.3
  62.6 0.8 copy-done.3
  63.4 2.6 %slot_block.2 = (bf16[512,1024]{1,0:T(8,128)(2,1)S(1)}, bf16[512,512]{1,0:T(8,128)(2,1)S(1)}) custom-call(bf16[512,1024]{1,0:T(8,128)(2,1)S(1)} %get-tuple-element.29.x_in, bf16[512,512]{1,0:T(8,128)(2,1)S(1)} %get-tuple-element.30.narrow, bf16[512,512]{1,0:T(8,128)(2,1)S(1)} %collective-permute-done.7.partner, f32[4,1024]{1,0:T(4,128)S(1)} %copy-done.4, ...), custom_call_target="tpu_custom_call" | custom-call | flops 1879048192 | bytes 7864320 | tf_op jit(solution)/shard_map/slot_block/pallas_call | solution.py:262
  66.1 2.7 %slot_block.3 = (bf16[512,1024]{1,0:T(8,128)(2,1)S(1)}, bf16[512,512]{1,0:T(8,128)(2,1)S(1)}) custom-call(bf16[512,1024]{1,0:T(8,128)(2,1)S(1)} %get-tuple-element.41.x_in, bf16[512,512]{1,0:T(8,128)(2,1)S(1)} %get-tuple-element.42.narrow, bf16[512,512]{1,0:T(8,128)(2,1)S(1)} %collective-permute-done.23.partner, f32[4,1024]{1,0:T(4,128)S(1)} %copy-done.4, ...), custom_call_target="tpu_custom_call" | custom-call | flops 1879048192 | bytes 7864320 | tf_op jit(solution)/shard_map/slot_block/pallas_call | solution.py:262
  69.3 7.0 %rest.2 = (bf16[64,1024]{1,0:T(8,128)(2,1)S(1)}, bf16[64,1024]{1,0:T(8,128)(2,1)S(1)}, bf16[64,1024]{1,0:T(8,128)(2,1)S(1)}, bf16[64,1024]{1,0:T(8,128)(2,1)S(1)...) custom-call(bf16[512,1024]{1,0:T(8,128)(2,1)S(1)} %get-tuple-element, ...), custom_call_target="tpu_custom_call" | custom-call | flops 5637144576 | bytes 15204352 | tf_op jit(solution)/shard_map/rest/pallas_call | solution.py:264
  76.4 0.6 collective-permute-start.9
  77.0 3.2 %collective-permute-start.10 = (bf16[64,1024]{1,0:T(8,128)(2,1)S(1)}, bf16[64,1024]{1,0:T(8,128)(2,1)S(1)}, u32[]{:S(2)}, u32[]{:S(2)}) collective-permute-start(bf16[64,1024]{1,0:T(8,128)(2,1)S(1)} %get-tuple-element.35), channel_id=1, source_target_pairs={{0,4},{1,5},{2,6},{3,7},{4,0},{5,1},{6,2},{7,3},{8,12},{9,13},{10,... | collective-permute-start | bytes 393224 | tf_op jit(solution)/shard_map/ppermute | solution.py:192
  80.2 6.8 %rest.3 = (bf16[64,1024]{1,0:T(8,128)(2,1)S(1)}, bf16[64,1024]{1,0:T(8,128)(2,1)S(1)}, bf16[64,1024]{1,0:T(8,128)(2,1)S(1)}, bf16[64,1024]{1,0:T(8,128)(2,1)S(1)...) custom-call(bf16[512,1024]{1,0:T(8,128)(2,1)S(1)} %get-tuple-element, ...), custom_call_target="tpu_custom_call" | custom-call | flops 5637144576 | bytes 15204352 | tf_op jit(solution)/shard_map/rest/pallas_call | solution.py:264
  87.0 0.9 collective-permute-start.25
  87.9 2.7 %collective-permute-start.27 = (bf16[64,1024]{1,0:T(8,128)(2,1)S(1)}, bf16[64,1024]{1,0:T(8,128)(2,1)S(1)}, u32[]{:S(2)}, u32[]{:S(2)}) collective-permute-start(bf16[64,1024]{1,0:T(8,128)(2,1)S(1)} %get-tuple-element.48), channel_id=1, source_target_pairs={{0,6},{1,7},{2,4},{3,5},{4,2},{5,3},{6,0},{7,1},{8,14},{9,15},{10,... | collective-permute-start | bytes 393224 | tf_op jit(solution)/shard_map/ppermute | solution.py:192
  90.6 3.1 %collective-permute-start.29 = (bf16[64,1024]{1,0:T(8,128)(2,1)S(1)}, bf16[64,1024]{1,0:T(8,128)(2,1)S(1)}, u32[]{:S(2)}, u32[]{:S(2)}) collective-permute-start(bf16[64,1024]{1,0:T(8,128)(2,1)S(1)} %get-tuple-element.50), channel_id=1, source_target_pairs={{0,10},{1,11},{2,8},{3,9},{4,14},{5,15},{6,12},{7,13},{8,2},{9,3},... | collective-permute-start | bytes 393224 | tf_op jit(solution)/shard_map/ppermute | solution.py:192
  94.3 2.2 %collective-permute-start.31 = (bf16[64,1024]{1,0:T(8,128)(2,1)S(1)}, bf16[64,1024]{1,0:T(8,128)(2,1)S(1)}, u32[]{:S(2)}, u32[]{:S(2)}) collective-permute-start(bf16[64,1024]{1,0:T(8,128)(2,1)S(1)} %get-tuple-element.52), channel_id=1, source_target_pairs={{0,14},{1,15},{2,12},{3,13},{4,10},{5,11},{6,8},{7,9},{8,6},{9,7},... | collective-permute-start | bytes 393224 | tf_op jit(solution)/shard_map/ppermute | solution.py:192
  96.5 1.3 collective-permute-done.27.refs_3_
  97.7 2.3 %collective-permute-start.11 = (bf16[64,1024]{1,0:T(8,128)(2,1)S(1)}, bf16[64,1024]{1,0:T(8,128)(2,1)S(1)}, u32[]{:S(2)}, u32[]{:S(2)}) collective-permute-start(bf16[64,1024]{1,0:T(8,128)(2,1)S(1)} %get-tuple-element.36), channel_id=1, source_target_pairs={{0,6},{1,7},{2,4},{3,5},{4,2},{5,3},{6,0},{7,1},{8,14},{9,15},{10,... | collective-permute-start | bytes 393224 | tf_op jit(solution)/shard_map/ppermute | solution.py:192
  100.5 8.4 %collective-permute-done.29.refs_5_ = bf16[64,1024]{1,0:T(8,128)(2,1)S(1)} collective-permute-done((bf16[64,1024]{1,0:T(8,128)(2,1)S(1)}, bf16[64,1024]{1,0:T(8,128)(2,1)S(1)}, u32[]{:S(2)}, u32[]{:S(2)}) %collective-permute-start.29) | collective-permute-done | bytes 131104 | tf_op jit(solution)/shard_map/ppermute | solution.py:192
  109.0 4.8 %collective-permute-start.13 = (bf16[64,1024]{1,0:T(8,128)(2,1)S(1)}, bf16[64,1024]{1,0:T(8,128)(2,1)S(1)}, u32[]{:S(2)}, u32[]{:S(2)}) collective-permute-start(bf16[64,1024]{1,0:T(8,128)(2,1)S(1)} %get-tuple-element.38), channel_id=1, source_target_pairs={{0,10},{1,11},{2,8},{3,9},{4,14},{5,15},{6,12},{7,13},{8,2},{9,3},... | collective-permute-start | bytes 393224 | tf_op jit(solution)/shard_map/ppermute | solution.py:192
  113.7 7.8 %collective-permute-done.30.refs_6_ = bf16[64,1024]{1,0:T(8,128)(2,1)S(1)} collective-permute-done((bf16[64,1024]{1,0:T(8,128)(2,1)S(1)}, bf16[64,1024]{1,0:T(8,128)(2,1)S(1)}, u32[]{:S(2)}, u32[]{:S(2)}) %collective-permute-start.30) | collective-permute-done | bytes 131104 | tf_op jit(solution)/shard_map/ppermute | solution.py:192
  121.5 1.0 collective-permute-start.14
  122.5 2.2 %collective-permute-done.31.refs_7_ = bf16[64,1024]{1,0:T(8,128)(2,1)S(1)} collective-permute-done((bf16[64,1024]{1,0:T(8,128)(2,1)S(1)}, bf16[64,1024]{1,0:T(8,128)(2,1)S(1)}, u32[]{:S(2)}, u32[]{:S(2)}) %collective-permute-start.31) | collective-permute-done | bytes 131104 | tf_op jit(solution)/shard_map/ppermute | solution.py:192
  124.8 1.1 collect.2.refs_8_
  125.9 1.7 %collective-permute-done.12.refs_4_ = bf16[64,1024]{1,0:T(8,128)(2,1)S(1)} collective-permute-done((bf16[64,1024]{1,0:T(8,128)(2,1)S(1)}, bf16[64,1024]{1,0:T(8,128)(2,1)S(1)}, u32[]{:S(2)}, u32[]{:S(2)}) %collective-permute-start.12) | collective-permute-done | bytes 131104 | tf_op jit(solution)/shard_map/ppermute | solution.py:192
  127.6 3.0 %collective-permute-done.13.refs_5_ = bf16[64,1024]{1,0:T(8,128)(2,1)S(1)} collective-permute-done((bf16[64,1024]{1,0:T(8,128)(2,1)S(1)}, bf16[64,1024]{1,0:T(8,128)(2,1)S(1)}, u32[]{:S(2)}, u32[]{:S(2)}) %collective-permute-start.13) | collective-permute-done | bytes 131104 | tf_op jit(solution)/shard_map/ppermute | solution.py:192
  130.5 4.6 %collective-permute-done.14.refs_6_ = bf16[64,1024]{1,0:T(8,128)(2,1)S(1)} collective-permute-done((bf16[64,1024]{1,0:T(8,128)(2,1)S(1)}, bf16[64,1024]{1,0:T(8,128)(2,1)S(1)}, u32[]{:S(2)}, u32[]{:S(2)}) %collective-permute-start.14) | collective-permute-done | bytes 131104 | tf_op jit(solution)/shard_map/ppermute | solution.py:192
  135.2 2.0 %collective-permute-done.15.refs_7_ = bf16[64,1024]{1,0:T(8,128)(2,1)S(1)} collective-permute-done((bf16[64,1024]{1,0:T(8,128)(2,1)S(1)}, bf16[64,1024]{1,0:T(8,128)(2,1)S(1)}, u32[]{:S(2)}, u32[]{:S(2)}) %collective-permute-start.15) | collective-permute-done | bytes 131104 | tf_op jit(solution)/shard_map/ppermute | solution.py:192
  137.2 1.1 collect.3
  (46 shorter events, 3.2 us)
Async XLA Ops:
  1.4 17.7 %collective-permute-start.5 = (bf16[64,1024]{1,0:T(8,128)(2,1)S(1)}, bf16[64,1024]{1,0:T(8,128)(2,1)S(1)}, u32[]{:S(2)}, u32[]{:S(2)}) collective-permute-start(bf16[64,1024]{1,0:T(8,128)(2,1)S(1)} %bitcast.68), channel_id=1, source_target_pairs={{0,12},{1,13},{2,14},{3,15},{4,8},{5,9},{6,10},{7,11},{8,4},{9,5},... | collective-permute-start | bytes 393224 | tf_op jit(solution)/shard_map/ppermute | solution.py:192
  1.9 20.9 %collective-permute-start.6 = (bf16[64,1024]{1,0:T(8,128)(2,1)S(1)}, bf16[64,1024]{1,0:T(8,128)(2,1)S(1)}, u32[]{:S(2)}, u32[]{:S(2)}) collective-permute-start(bf16[64,1024]{1,0:T(8,128)(2,1)S(1)} %bitcast.66), channel_id=1, source_target_pairs={{0,14},{1,15},{2,12},{3,13},{4,10},{5,11},{6,8},{7,9},{8,6},{9,7},... | collective-permute-start | bytes 393224 | tf_op jit(solution)/shard_map/ppermute | solution.py:192
  4.4 26.1 %collective-permute-start.4 = (bf16[64,1024]{1,0:T(8,128)(2,1)S(1)}, bf16[64,1024]{1,0:T(8,128)(2,1)S(1)}, u32[]{:S(2)}, u32[]{:S(2)}) collective-permute-start(bf16[64,1024]{1,0:T(8,128)(2,1)S(1)} %bitcast.60), channel_id=1, source_target_pairs={{0,10},{1,11},{2,8},{3,9},{4,14},{5,15},{6,12},{7,13},{8,2},{9,3},... | collective-permute-start | bytes 393224 | tf_op jit(solution)/shard_map/ppermute | solution.py:192
  6.4 24.1 %collective-permute-start.3 = (bf16[64,1024]{1,0:T(8,128)(2,1)S(1)}, bf16[64,1024]{1,0:T(8,128)(2,1)S(1)}, u32[]{:S(2)}, u32[]{:S(2)}) collective-permute-start(bf16[64,1024]{1,0:T(8,128)(2,1)S(1)} %bitcast.59), channel_id=1, source_target_pairs={{0,8},{1,9},{2,10},{3,11},{4,12},{5,13},{6,14},{7,15},{8,0},{9,1},... | collective-permute-start | bytes 393224 | tf_op jit(solution)/shard_map/ppermute | solution.py:192
  7.3 23.2 %collective-permute-start.2 = (bf16[64,1024]{1,0:T(8,128)(2,1)S(1)}, bf16[64,1024]{1,0:T(8,128)(2,1)S(1)}, u32[]{:S(2)}, u32[]{:S(2)}) collective-permute-start(bf16[64,1024]{1,0:T(8,128)(2,1)S(1)} %bitcast.58), channel_id=1, source_target_pairs={{0,6},{1,7},{2,4},{3,5},{4,2},{5,3},{6,0},{7,1},{8,14},{9,15},{10,... | collective-permute-start | bytes 393224 | tf_op jit(solution)/shard_map/ppermute | solution.py:192
  19.1 11.5 %collective-permute-start.1 = (bf16[64,1024]{1,0:T(8,128)(2,1)S(1)}, bf16[64,1024]{1,0:T(8,128)(2,1)S(1)}, u32[]{:S(2)}, u32[]{:S(2)}) collective-permute-start(bf16[64,1024]{1,0:T(8,128)(2,1)S(1)} %bitcast.57), channel_id=1, source_target_pairs={{0,4},{1,5},{2,6},{3,7},{4,0},{5,1},{6,2},{7,3},{8,12},{9,13},{10,... | collective-permute-start | bytes 393224 | tf_op jit(solution)/shard_map/ppermute | solution.py:192
  22.8 7.7 %collective-permute-start = (bf16[64,1024]{1,0:T(8,128)(2,1)S(1)}, bf16[64,1024]{1,0:T(8,128)(2,1)S(1)}, u32[]{:S(2)}, u32[]{:S(2)}) collective-permute-start(bf16[64,1024]{1,0:T(8,128)(2,1)S(1)} %bitcast.56), channel_id=1, source_target_pairs={{0,2},{1,3},{2,0},{3,1},{4,6},{5,7},{6,4},{7,5},{8,10},{9,11},{10,... | collective-permute-start | bytes 393224 | tf_op jit(solution)/shard_map/ppermute | solution.py:192
  23.3 2.8 %copy-start = (bf16[4,3,512,512]{3,2,1,0:T(8,128)(2,1)S(1)}, bf16[4,3,512,512]{3,2,1,0:T(8,128)(2,1)}, u32[]{:S(2)}) copy-start(bf16[4,3,512,512]{3,2,1,0:T(8,128)(2,1)} %taps.9) | copy-start | bytes 18874372
  26.1 2.2 %copy-start.1 = (bf16[4,1024,512]{2,1,0:T(8,128)(2,1)S(1)}, bf16[4,1024,512]{2,1,0:T(8,128)(2,1)}, u32[]{:S(2)}) copy-start(bf16[4,1024,512]{2,1,0:T(8,128)(2,1)} %proj.9) | copy-start | bytes 12582916
  28.3 2.2 %copy-start.2 = (bf16[4,512,1024]{2,1,0:T(8,128)(2,1)S(1)}, bf16[4,512,1024]{2,1,0:T(8,128)(2,1)}, u32[]{:S(2)}) copy-start(bf16[4,512,1024]{2,1,0:T(8,128)(2,1)} %output.9) | copy-start | bytes 12582916
  30.5 0.7 copy-start.4
  30.5 0.7 copy-start.5
  31.2 1.6 %copy-start.6 = (bf16[1024,1024]{1,0:T(8,128)(2,1)S(1)}, bf16[1024,1024]{1,0:T(8,128)(2,1)}, u32[]{:S(2)}) copy-start(bf16[1024,1024]{1,0:T(8,128)(2,1)} %param.6) | copy-start | bytes 6291460
  31.2 31.3 %slice-start = ((s8[6291456]{0:T(1024)(128)(4,1)}), s8[4194304]{0:T(1024)(128)(4,1)S(1)}, s32[]{:S(2)}) async-start(s8[6291456]{0:T(1024)(128)(4,1)} %bitcast.50), calls=%async_computation | async-start | bytes 8388608
  32.5 30.1 %slice-start.1 = ((s8[6291456]{0:T(1024)(128)(4,1)}), s8[2097152]{0:T(1024)(128)(4,1)S(1)}, s32[]{:S(2)}) async-start(s8[6291456]{0:T(1024)(128)(4,1)} %bitcast.50), calls=%async_computation.1 | async-start | bytes 4194304
  32.5 30.0 %collective-permute-start.7 = (bf16[512,512]{1,0:T(8,128)(2,1)S(1)}, bf16[512,512]{1,0:T(8,128)(2,1)S(1)}, u32[]{:S(2)}, u32[]{:S(2)}) collective-permute-start(bf16[512,512]{1,0:T(8,128)(2,1)S(1)} %get-tuple-element.30.narrow), channel_id=1, source_target_pairs={{0,1},{1,0},{2,3},{3,2},{4,5},{5,4},{6,7},{7,6},{8,9},{9,8},{10,11... | collective-permute-start | bytes 1572872 | tf_op jit(solution)/shard_map/ppermute | solution.py:195
  32.9 16.6 %collective-permute-start.21 = (bf16[64,1024]{1,0:T(8,128)(2,1)S(1)}, bf16[64,1024]{1,0:T(8,128)(2,1)S(1)}, u32[]{:S(2)}, u32[]{:S(2)}) collective-permute-start(bf16[64,1024]{1,0:T(8,128)(2,1)S(1)} %bitcast.69), channel_id=1, source_target_pairs={{0,12},{1,13},{2,14},{3,15},{4,8},{5,9},{6,10},{7,11},{8,4},{9,5},... | collective-permute-start | bytes 393224 | tf_op jit(solution)/shard_map/ppermute | solution.py:192
  33.6 18.7 %collective-permute-start.22 = (bf16[64,1024]{1,0:T(8,128)(2,1)S(1)}, bf16[64,1024]{1,0:T(8,128)(2,1)S(1)}, u32[]{:S(2)}, u32[]{:S(2)}) collective-permute-start(bf16[64,1024]{1,0:T(8,128)(2,1)S(1)} %bitcast.67), channel_id=1, source_target_pairs={{0,14},{1,15},{2,12},{3,13},{4,10},{5,11},{6,8},{7,9},{8,6},{9,7},... | collective-permute-start | bytes 393224 | tf_op jit(solution)/shard_map/ppermute | solution.py:192
  36.0 17.0 %collective-permute-start.20 = (bf16[64,1024]{1,0:T(8,128)(2,1)S(1)}, bf16[64,1024]{1,0:T(8,128)(2,1)S(1)}, u32[]{:S(2)}, u32[]{:S(2)}) collective-permute-start(bf16[64,1024]{1,0:T(8,128)(2,1)S(1)} %bitcast.65), channel_id=1, source_target_pairs={{0,10},{1,11},{2,8},{3,9},{4,14},{5,15},{6,12},{7,13},{8,2},{9,3},... | collective-permute-start | bytes 393224 | tf_op jit(solution)/shard_map/ppermute | solution.py:192
  36.7 19.1 %collective-permute-start.19 = (bf16[64,1024]{1,0:T(8,128)(2,1)S(1)}, bf16[64,1024]{1,0:T(8,128)(2,1)S(1)}, u32[]{:S(2)}, u32[]{:S(2)}) collective-permute-start(bf16[64,1024]{1,0:T(8,128)(2,1)S(1)} %bitcast.64), channel_id=1, source_target_pairs={{0,8},{1,9},{2,10},{3,11},{4,12},{5,13},{6,14},{7,15},{8,0},{9,1},... | collective-permute-start | bytes 393224 | tf_op jit(solution)/shard_map/ppermute | solution.py:192
  49.6 9.5 %collective-permute-start.18 = (bf16[64,1024]{1,0:T(8,128)(2,1)S(1)}, bf16[64,1024]{1,0:T(8,128)(2,1)S(1)}, u32[]{:S(2)}, u32[]{:S(2)}) collective-permute-start(bf16[64,1024]{1,0:T(8,128)(2,1)S(1)} %bitcast.63), channel_id=1, source_target_pairs={{0,6},{1,7},{2,4},{3,5},{4,2},{5,3},{6,0},{7,1},{8,14},{9,15},{10,... | collective-permute-start | bytes 393224 | tf_op jit(solution)/shard_map/ppermute | solution.py:192
  52.3 8.9 %collective-permute-start.17 = (bf16[64,1024]{1,0:T(8,128)(2,1)S(1)}, bf16[64,1024]{1,0:T(8,128)(2,1)S(1)}, u32[]{:S(2)}, u32[]{:S(2)}) collective-permute-start(bf16[64,1024]{1,0:T(8,128)(2,1)S(1)} %bitcast.62), channel_id=1, source_target_pairs={{0,4},{1,5},{2,6},{3,7},{4,0},{5,1},{6,2},{7,3},{8,12},{9,13},{10,... | collective-permute-start | bytes 393224 | tf_op jit(solution)/shard_map/ppermute | solution.py:192
  53.0 8.2 %collective-permute-start.16 = (bf16[64,1024]{1,0:T(8,128)(2,1)S(1)}, bf16[64,1024]{1,0:T(8,128)(2,1)S(1)}, u32[]{:S(2)}, u32[]{:S(2)}) collective-permute-start(bf16[64,1024]{1,0:T(8,128)(2,1)S(1)} %bitcast.61), channel_id=1, source_target_pairs={{0,2},{1,3},{2,0},{3,1},{4,6},{5,7},{6,4},{7,5},{8,10},{9,11},{10,... | collective-permute-start | bytes 393224 | tf_op jit(solution)/shard_map/ppermute | solution.py:192
  61.2 2.2 %copy-start.3 = (bf16[4,512,1024]{2,1,0:T(8,128)(2,1)S(1)}, bf16[4,512,1024]{2,1,0:T(8,128)(2,1)}, u32[]{:S(2)}) copy-start(bf16[4,512,1024]{2,1,0:T(8,128)(2,1)} %output.9) | copy-start | bytes 12582916
  62.4 3.7 %collective-permute-start.23 = (bf16[512,512]{1,0:T(8,128)(2,1)S(1)}, bf16[512,512]{1,0:T(8,128)(2,1)S(1)}, u32[]{:S(2)}, u32[]{:S(2)}) collective-permute-start(bf16[512,512]{1,0:T(8,128)(2,1)S(1)} %get-tuple-element.42.narrow), channel_id=1, source_target_pairs={{0,1},{1,0},{2,3},{3,2},{4,5},{5,4},{6,7},{7,6},{8,9},{9,8},{10,11... | collective-permute-start | bytes 1572872 | tf_op jit(solution)/shard_map/ppermute | solution.py:195
  66.0 3.3 %collective-permute-start.8 = (bf16[512,512]{1,0:T(8,128)(2,1)S(1)}, bf16[512,512]{1,0:T(8,128)(2,1)S(1)}, u32[]{:S(2)}, u32[]{:S(2)}) collective-permute-start(bf16[512,512]{1,0:T(8,128)(2,1)S(1)} %get-tuple-element.32.narrow), channel_id=1, source_target_pairs={{0,1},{1,0},{2,3},{3,2},{4,5},{5,4},{6,7},{7,6},{8,9},{9,8},{10,11... | collective-permute-start | bytes 1572872 | tf_op jit(solution)/shard_map/ppermute | solution.py:195
  68.8 11.4 %collective-permute-start.24 = (bf16[512,512]{1,0:T(8,128)(2,1)S(1)}, bf16[512,512]{1,0:T(8,128)(2,1)S(1)}, u32[]{:S(2)}, u32[]{:S(2)}) collective-permute-start(bf16[512,512]{1,0:T(8,128)(2,1)S(1)} %get-tuple-element.44.narrow), channel_id=1, source_target_pairs={{0,1},{1,0},{2,3},{3,2},{4,5},{5,4},{6,7},{7,6},{8,9},{9,8},{10,11... | collective-permute-start | bytes 1572872 | tf_op jit(solution)/shard_map/ppermute | solution.py:195
  76.4 14.2 %collective-permute-start.9 = (bf16[64,1024]{1,0:T(8,128)(2,1)S(1)}, bf16[64,1024]{1,0:T(8,128)(2,1)S(1)}, u32[]{:S(2)}, u32[]{:S(2)}) collective-permute-start(bf16[64,1024]{1,0:T(8,128)(2,1)S(1)} %get-tuple-element.34), channel_id=1, source_target_pairs={{0,2},{1,3},{2,0},{3,1},{4,6},{5,7},{6,4},{7,5},{8,10},{9,11},{10,... | collective-permute-start | bytes 393224 | tf_op jit(solution)/shard_map/ppermute | solution.py:192
  77.0 13.6 %collective-permute-start.10 = (bf16[64,1024]{1,0:T(8,128)(2,1)S(1)}, bf16[64,1024]{1,0:T(8,128)(2,1)S(1)}, u32[]{:S(2)}, u32[]{:S(2)}) collective-permute-start(bf16[64,1024]{1,0:T(8,128)(2,1)S(1)} %get-tuple-element.35), channel_id=1, source_target_pairs={{0,4},{1,5},{2,6},{3,7},{4,0},{5,1},{6,2},{7,3},{8,12},{9,13},{10,... | collective-permute-start | bytes 393224 | tf_op jit(solution)/shard_map/ppermute | solution.py:192
  87.0 6.7 %collective-permute-start.25 = (bf16[64,1024]{1,0:T(8,128)(2,1)S(1)}, bf16[64,1024]{1,0:T(8,128)(2,1)S(1)}, u32[]{:S(2)}, u32[]{:S(2)}) collective-permute-start(bf16[64,1024]{1,0:T(8,128)(2,1)S(1)} %get-tuple-element.46), channel_id=1, source_target_pairs={{0,2},{1,3},{2,0},{3,1},{4,6},{5,7},{6,4},{7,5},{8,10},{9,11},{10,... | collective-permute-start | bytes 393224 | tf_op jit(solution)/shard_map/ppermute | solution.py:192
  87.9 6.4 %collective-permute-start.26 = (bf16[64,1024]{1,0:T(8,128)(2,1)S(1)}, bf16[64,1024]{1,0:T(8,128)(2,1)S(1)}, u32[]{:S(2)}, u32[]{:S(2)}) collective-permute-start(bf16[64,1024]{1,0:T(8,128)(2,1)S(1)} %get-tuple-element.47), channel_id=1, source_target_pairs={{0,4},{1,5},{2,6},{3,7},{4,0},{5,1},{6,2},{7,3},{8,12},{9,13},{10,... | collective-permute-start | bytes 393224 | tf_op jit(solution)/shard_map/ppermute | solution.py:192
  87.9 9.8 %collective-permute-start.27 = (bf16[64,1024]{1,0:T(8,128)(2,1)S(1)}, bf16[64,1024]{1,0:T(8,128)(2,1)S(1)}, u32[]{:S(2)}, u32[]{:S(2)}) collective-permute-start(bf16[64,1024]{1,0:T(8,128)(2,1)S(1)} %get-tuple-element.48), channel_id=1, source_target_pairs={{0,6},{1,7},{2,4},{3,5},{4,2},{5,3},{6,0},{7,1},{8,14},{9,15},{10,... | collective-permute-start | bytes 393224 | tf_op jit(solution)/shard_map/ppermute | solution.py:192
  90.6 9.5 %collective-permute-start.28 = (bf16[64,1024]{1,0:T(8,128)(2,1)S(1)}, bf16[64,1024]{1,0:T(8,128)(2,1)S(1)}, u32[]{:S(2)}, u32[]{:S(2)}) collective-permute-start(bf16[64,1024]{1,0:T(8,128)(2,1)S(1)} %get-tuple-element.49), channel_id=1, source_target_pairs={{0,8},{1,9},{2,10},{3,11},{4,12},{5,13},{6,14},{7,15},{8,0},{9,1},... | collective-permute-start | bytes 393224 | tf_op jit(solution)/shard_map/ppermute | solution.py:192
  90.6 18.4 %collective-permute-start.29 = (bf16[64,1024]{1,0:T(8,128)(2,1)S(1)}, bf16[64,1024]{1,0:T(8,128)(2,1)S(1)}, u32[]{:S(2)}, u32[]{:S(2)}) collective-permute-start(bf16[64,1024]{1,0:T(8,128)(2,1)S(1)} %get-tuple-element.50), channel_id=1, source_target_pairs={{0,10},{1,11},{2,8},{3,9},{4,14},{5,15},{6,12},{7,13},{8,2},{9,3},... | collective-permute-start | bytes 393224 | tf_op jit(solution)/shard_map/ppermute | solution.py:192
  93.7 27.8 %collective-permute-start.30 = (bf16[64,1024]{1,0:T(8,128)(2,1)S(1)}, bf16[64,1024]{1,0:T(8,128)(2,1)S(1)}, u32[]{:S(2)}, u32[]{:S(2)}) collective-permute-start(bf16[64,1024]{1,0:T(8,128)(2,1)S(1)} %get-tuple-element.51), channel_id=1, source_target_pairs={{0,12},{1,13},{2,14},{3,15},{4,8},{5,9},{6,10},{7,11},{8,4},{9,5},... | collective-permute-start | bytes 393224 | tf_op jit(solution)/shard_map/ppermute | solution.py:192
  94.3 30.5 %collective-permute-start.31 = (bf16[64,1024]{1,0:T(8,128)(2,1)S(1)}, bf16[64,1024]{1,0:T(8,128)(2,1)S(1)}, u32[]{:S(2)}, u32[]{:S(2)}) collective-permute-start(bf16[64,1024]{1,0:T(8,128)(2,1)S(1)} %get-tuple-element.52), channel_id=1, source_target_pairs={{0,14},{1,15},{2,12},{3,13},{4,10},{5,11},{6,8},{7,9},{8,6},{9,7},... | collective-permute-start | bytes 393224 | tf_op jit(solution)/shard_map/ppermute | solution.py:192
  97.7 28.1 %collective-permute-start.11 = (bf16[64,1024]{1,0:T(8,128)(2,1)S(1)}, bf16[64,1024]{1,0:T(8,128)(2,1)S(1)}, u32[]{:S(2)}, u32[]{:S(2)}) collective-permute-start(bf16[64,1024]{1,0:T(8,128)(2,1)S(1)} %get-tuple-element.36), channel_id=1, source_target_pairs={{0,6},{1,7},{2,4},{3,5},{4,2},{5,3},{6,0},{7,1},{8,14},{9,15},{10,... | collective-permute-start | bytes 393224 | tf_op jit(solution)/shard_map/ppermute | solution.py:192
  100.1 27.5 %collective-permute-start.12 = (bf16[64,1024]{1,0:T(8,128)(2,1)S(1)}, bf16[64,1024]{1,0:T(8,128)(2,1)S(1)}, u32[]{:S(2)}, u32[]{:S(2)}) collective-permute-start(bf16[64,1024]{1,0:T(8,128)(2,1)S(1)} %get-tuple-element.37), channel_id=1, source_target_pairs={{0,8},{1,9},{2,10},{3,11},{4,12},{5,13},{6,14},{7,15},{8,0},{9,1},... | collective-permute-start | bytes 393224 | tf_op jit(solution)/shard_map/ppermute | solution.py:192
  109.0 21.5 %collective-permute-start.13 = (bf16[64,1024]{1,0:T(8,128)(2,1)S(1)}, bf16[64,1024]{1,0:T(8,128)(2,1)S(1)}, u32[]{:S(2)}, u32[]{:S(2)}) collective-permute-start(bf16[64,1024]{1,0:T(8,128)(2,1)S(1)} %get-tuple-element.38), channel_id=1, source_target_pairs={{0,10},{1,11},{2,8},{3,9},{4,14},{5,15},{6,12},{7,13},{8,2},{9,3},... | collective-permute-start | bytes 393224 | tf_op jit(solution)/shard_map/ppermute | solution.py:192
  121.5 13.6 %collective-permute-start.14 = (bf16[64,1024]{1,0:T(8,128)(2,1)S(1)}, bf16[64,1024]{1,0:T(8,128)(2,1)S(1)}, u32[]{:S(2)}, u32[]{:S(2)}) collective-permute-start(bf16[64,1024]{1,0:T(8,128)(2,1)S(1)} %get-tuple-element.39), channel_id=1, source_target_pairs={{0,12},{1,13},{2,14},{3,15},{4,8},{5,9},{6,10},{7,11},{8,4},{9,5},... | collective-permute-start | bytes 393224 | tf_op jit(solution)/shard_map/ppermute | solution.py:192
  124.8 12.4 %collective-permute-start.15 = (bf16[64,1024]{1,0:T(8,128)(2,1)S(1)}, bf16[64,1024]{1,0:T(8,128)(2,1)S(1)}, u32[]{:S(2)}, u32[]{:S(2)}) collective-permute-start(bf16[64,1024]{1,0:T(8,128)(2,1)S(1)} %get-tuple-element.40), channel_id=1, source_target_pairs={{0,14},{1,15},{2,12},{3,13},{4,10},{5,11},{6,8},{7,9},{8,6},{9,7},... | collective-permute-start | bytes 393224 | tf_op jit(solution)/shard_map/ppermute | solution.py:192

commit v5 on v4

--- a/solution.py
+++ b/solution.py
@@ -133,16 +133,16 @@
         pieces[k][...] = x_ref[pl.ds(pl.multiple_of((chip ^ k) * width, width), width), :]
 
 
-def collect_kernel(chips, slots, part, chunks, chunk, *refs):
-    pieces, (result, sems) = refs[:chips], refs[-2:]
+def collect_kernel(ways, slots, part, chunks, chunk, *refs):
+    pieces, (result, sems) = refs[: len(ways)], refs[-2:]
     chip, _ = position()
     copies = [
         pltpu.make_async_copy(
-            pieces[k].at[pl.ds(slot * part, part), :],
+            pieces[n].at[pl.ds(slot * part, part), :],
             result.at[slot, (chip ^ k) * chunks + chunk],
-            sems.at[k, slot],
+            sems.at[n, slot],
         )
-        for k in range(chips)
+        for n, k in enumerate(ways)
         for slot in range(slots)
     ]
     for copy in copies:
@@ -248,7 +248,9 @@
     for j in range(chunks):
         pieces = {}
         grid = lax.optimization_barrier(grid)
-        for k in [0, *leave_order(chips)]:
+        for n, k in enumerate([*leave_order(chips), 0]):
+            if j == 0 and n == 2:
+                grid = lax.optimization_barrier(grid)
             piece = lax.dynamic_slice_in_dim(grid, (chip ^ k) * chunks + j, 1, axis=1).reshape(width, model)
             pieces[k] = to_chip(piece, k) if k else piece
         arrived.append([pieces[k] for k in range(chips)])
@@ -268,18 +270,22 @@
         left.append(gone)
 
     result = None
-    for j in range(chunks):
+    leave = [0, *leave_order(chips)]
+    late = travel_order(chips)[1][2:]
+    groups = [(j, leave) for j in range(chunks - 1)]
+    groups += [(chunks - 1, [k for k in leave if k not in late]), (chunks - 1, late)]
+    for n, (j, ways) in enumerate(groups):
         collect = pl.pallas_call(
-            functools.partial(collect_kernel, chips, slots, part, chunks, j),
+            functools.partial(collect_kernel, ways, slots, part, chunks, j),
             out_shape=shape(grid.shape, bf16),
-            in_specs=[VMEM] * chips + [pl.BlockSpec(memory_space=pl.ANY)] * (j > 0),
+            in_specs=[VMEM] * len(ways) + [pl.BlockSpec(memory_space=pl.ANY)] * (n > 0),
             out_specs=pl.BlockSpec(memory_space=pl.ANY),
-            scratch_shapes=[pltpu.SemaphoreType.DMA((chips, slots))],
-            input_output_aliases={chips: 0} if j else {},
+            scratch_shapes=[pltpu.SemaphoreType.DMA((len(ways), slots))],
+            input_output_aliases={len(ways): 0} if n else {},
             compiler_params=LIMIT,
             name="collect",
         )
-        result = collect(*[left[j][k] for k in range(chips)], *([result] if j else []))
+        result = collect(*[left[j][k] for k in ways], *([result] if n else []))
     return result.reshape(rows, model)
 
 

time: 139 us -> 129 us (0.928)
  the two profiles are of different devices: /device:TPU:16 before, /device:TPU:0 now
where the time goes in v5:
time: 129 us
  starting transfers between devices  72.7 us (56%)
  Pallas kernels  24.5 us (19%)
  waiting for transfers between devices  20.1 us (16%)
  local copies, waits for them, and re-layouts  11.3 us (9%)
    ppermute x28, starting transfers between devices, to_chip(): lax.ppermute(piece, 'blk', [(i, i ^ k * CORES) for i in range(peers)])  72 us
    ppermute x28, waiting for transfers between devices, to_chip(): lax.ppermute(piece, 'blk', [(i, i ^ k * CORES) for i in range(peers)])  20.1 us
    pallas_call x2, Pallas kernels, body(): pieces = rest(x, narrow, partner, *weights)  13.9 us
    unnamed x18, local copies, waits for them, and re-layouts  8.92 us
    pallas_call x2, Pallas kernels, body(): x, narrow = slot_block(x, narrow, partner, *weights)  5.31 us
    pallas_call x3, Pallas kernels, body(): result = collect(*[left[j][k] for k in ways], *([result] if n else []))  2.8 us
  transfers between devices with their start and end apart: 32, of which 6 were waited for; matrix products, arithmetic and copies ran while one was open for 1% of the time, Pallas kernels for 17%

profile of v5, /device:TPU:0, one launch (start us, length us, event | category | flops | bytes accessed | tf_op | source)
XLA Modules:
  0.0 129.1 jit_solution(8029380730576096471)
XLA Ops:
  0.0 1.0 constant_dynamic-slice_fusion
  1.0 5.1 %collective-permute-start.21 = (bf16[64,1024]{1,0:T(8,128)(2,1)S(1)}, bf16[64,1024]{1,0:T(8,128)(2,1)S(1)}, u32[]{:S(2)}, u32[]{:S(2)}) collective-permute-start(bf16[64,1024]{1,0:T(8,128)(2,1)S(1)} %bitcast.65), channel_id=1, source_target_pairs={{0,12},{1,13},{2,14},{3,15},{4,8},{5,9},{6,10},{7,11},{8,4},{9,5},... | collective-permute-start | bytes 393224 | tf_op jit(solution)/shard_map/ppermute | solution.py:192
  6.1 1.2 collective-permute-start.22
  7.3 1.3 constant_dynamic-slice_fusion.2
  8.6 0.9 collective-permute-start.19
  9.5 1.9 %collective-permute-start.20 = (bf16[64,1024]{1,0:T(8,128)(2,1)S(1)}, bf16[64,1024]{1,0:T(8,128)(2,1)S(1)}, u32[]{:S(2)}, u32[]{:S(2)}) collective-permute-start(bf16[64,1024]{1,0:T(8,128)(2,1)S(1)} %bitcast.69), channel_id=1, source_target_pairs={{0,10},{1,11},{2,8},{3,9},{4,14},{5,15},{6,12},{7,13},{8,2},{9,3},... | collective-permute-start | bytes 393224 | tf_op jit(solution)/shard_map/ppermute | solution.py:192
  11.4 2.4 %collective-permute-start.18 = (bf16[64,1024]{1,0:T(8,128)(2,1)S(1)}, bf16[64,1024]{1,0:T(8,128)(2,1)S(1)}, u32[]{:S(2)}, u32[]{:S(2)}) collective-permute-start(bf16[64,1024]{1,0:T(8,128)(2,1)S(1)} %bitcast.68), channel_id=1, source_target_pairs={{0,6},{1,7},{2,4},{3,5},{4,2},{5,3},{6,0},{7,1},{8,14},{9,15},{10,... | collective-permute-start | bytes 393224 | tf_op jit(solution)/shard_map/ppermute | solution.py:192
  13.8 7.7 %collective-permute-start.17 = (bf16[64,1024]{1,0:T(8,128)(2,1)S(1)}, bf16[64,1024]{1,0:T(8,128)(2,1)S(1)}, u32[]{:S(2)}, u32[]{:S(2)}) collective-permute-start(bf16[64,1024]{1,0:T(8,128)(2,1)S(1)} %bitcast.67), channel_id=1, source_target_pairs={{0,4},{1,5},{2,6},{3,7},{4,0},{5,1},{6,2},{7,3},{8,12},{9,13},{10,... | collective-permute-start | bytes 393224 | tf_op jit(solution)/shard_map/ppermute | solution.py:192
  21.5 1.5 %collective-permute-start.16 = (bf16[64,1024]{1,0:T(8,128)(2,1)S(1)}, bf16[64,1024]{1,0:T(8,128)(2,1)S(1)}, u32[]{:S(2)}, u32[]{:S(2)}) collective-permute-start(bf16[64,1024]{1,0:T(8,128)(2,1)S(1)} %bitcast.66), channel_id=1, source_target_pairs={{0,2},{1,3},{2,0},{3,1},{4,6},{5,7},{6,4},{7,5},{8,10},{9,11},{10,... | collective-permute-start | bytes 393224 | tf_op jit(solution)/shard_map/ppermute | solution.py:192
  23.0 2.8 %copy-done = bf16[4,3,512,512]{3,2,1,0:T(8,128)(2,1)S(1)} copy-done((bf16[4,3,512,512]{3,2,1,0:T(8,128)(2,1)S(1)}, bf16[4,3,512,512]{3,2,1,0:T(8,128)(2,1)}, u32[]{:S(2)}) %copy-start) | copy-done | bytes 6291480
  25.8 2.2 %copy-done.1 = bf16[4,1024,512]{2,1,0:T(8,128)(2,1)S(1)} copy-done((bf16[4,1024,512]{2,1,0:T(8,128)(2,1)S(1)}, bf16[4,1024,512]{2,1,0:T(8,128)(2,1)}, u32[]{:S(2)}) %copy-start.1) | copy-done | bytes 4194328
  28.0 2.2 %copy-done.2 = bf16[4,512,1024]{2,1,0:T(8,128)(2,1)S(1)} copy-done((bf16[4,512,1024]{2,1,0:T(8,128)(2,1)S(1)}, bf16[4,512,1024]{2,1,0:T(8,128)(2,1)}, u32[]{:S(2)}) %copy-start.2) | copy-done | bytes 4194328
  30.3 0.7 copy-done.4
  30.9 1.2 enter.3
  32.6 3.2 %collective-permute-start.5 = (bf16[64,1024]{1,0:T(8,128)(2,1)S(1)}, bf16[64,1024]{1,0:T(8,128)(2,1)S(1)}, u32[]{:S(2)}, u32[]{:S(2)}) collective-permute-start(bf16[64,1024]{1,0:T(8,128)(2,1)S(1)} %bitcast.63), channel_id=1, source_target_pairs={{0,12},{1,13},{2,14},{3,15},{4,8},{5,9},{6,10},{7,11},{8,4},{9,5},... | collective-permute-start | bytes 393224 | tf_op jit(solution)/shard_map/ppermute | solution.py:192
  35.9 0.6 collective-permute-start.6
  36.5 3.6 %collective-permute-start.4 = (bf16[64,1024]{1,0:T(8,128)(2,1)S(1)}, bf16[64,1024]{1,0:T(8,128)(2,1)S(1)}, u32[]{:S(2)}, u32[]{:S(2)}) collective-permute-start(bf16[64,1024]{1,0:T(8,128)(2,1)S(1)} %bitcast.61), channel_id=1, source_target_pairs={{0,10},{1,11},{2,8},{3,9},{4,14},{5,15},{6,12},{7,13},{8,2},{9,3},... | collective-permute-start | bytes 393224 | tf_op jit(solution)/shard_map/ppermute | solution.py:192
  40.1 0.5 collective-permute-start.3
  40.6 11.4 %collective-permute-start.2 = (bf16[64,1024]{1,0:T(8,128)(2,1)S(1)}, bf16[64,1024]{1,0:T(8,128)(2,1)S(1)}, u32[]{:S(2)}, u32[]{:S(2)}) collective-permute-start(bf16[64,1024]{1,0:T(8,128)(2,1)S(1)} %bitcast.59), channel_id=1, source_target_pairs={{0,6},{1,7},{2,4},{3,5},{4,2},{5,3},{6,0},{7,1},{8,14},{9,15},{10,... | collective-permute-start | bytes 393224 | tf_op jit(solution)/shard_map/ppermute | solution.py:192
  51.9 2.8 %collective-permute-start.1 = (bf16[64,1024]{1,0:T(8,128)(2,1)S(1)}, bf16[64,1024]{1,0:T(8,128)(2,1)S(1)}, u32[]{:S(2)}, u32[]{:S(2)}) collective-permute-start(bf16[64,1024]{1,0:T(8,128)(2,1)S(1)} %bitcast.58), channel_id=1, source_target_pairs={{0,4},{1,5},{2,6},{3,7},{4,0},{5,1},{6,2},{7,3},{8,12},{9,13},{10,... | collective-permute-start | bytes 393224 | tf_op jit(solution)/shard_map/ppermute | solution.py:192
  54.8 2.3 %collective-permute-done.4.refs_5_ = bf16[64,1024]{1,0:T(8,128)(2,1)S(1)} collective-permute-done((bf16[64,1024]{1,0:T(8,128)(2,1)S(1)}, bf16[64,1024]{1,0:T(8,128)(2,1)S(1)}, u32[]{:S(2)}, u32[]{:S(2)}) %collective-permute-start.4) | collective-permute-done | bytes 131104 | tf_op jit(solution)/shard_map/ppermute | solution.py:192
  57.1 1.5 %collective-permute-start = (bf16[64,1024]{1,0:T(8,128)(2,1)S(1)}, bf16[64,1024]{1,0:T(8,128)(2,1)S(1)}, u32[]{:S(2)}, u32[]{:S(2)}) collective-permute-start(bf16[64,1024]{1,0:T(8,128)(2,1)S(1)} %bitcast.57), channel_id=1, source_target_pairs={{0,2},{1,3},{2,0},{3,1},{4,6},{5,7},{6,4},{7,5},{8,10},{9,11},{10,... | collective-permute-start | bytes 393224 | tf_op jit(solution)/shard_map/ppermute | solution.py:192
  58.6 1.3 collective-permute-done.3.refs_4_
  59.9 2.0 %collective-permute-done.2.refs_3_ = bf16[64,1024]{1,0:T(8,128)(2,1)S(1)} collective-permute-done((bf16[64,1024]{1,0:T(8,128)(2,1)S(1)}, bf16[64,1024]{1,0:T(8,128)(2,1)S(1)}, u32[]{:S(2)}, u32[]{:S(2)}) %collective-permute-start.2) | collective-permute-done | bytes 131104 | tf_op jit(solution)/shard_map/ppermute | solution.py:192
  61.9 2.2 %collective-permute-done.1.refs_2_ = bf16[64,1024]{1,0:T(8,128)(2,1)S(1)} collective-permute-done((bf16[64,1024]{1,0:T(8,128)(2,1)S(1)}, bf16[64,1024]{1,0:T(8,128)(2,1)S(1)}, u32[]{:S(2)}, u32[]{:S(2)}) %collective-permute-start.1) | collective-permute-done | bytes 131104 | tf_op jit(solution)/shard_map/ppermute | solution.py:192
  64.1 1.3 enter.2
  65.5 0.8 copy-done.3
  66.3 2.7 %slot_block.3 = (bf16[512,1024]{1,0:T(8,128)(2,1)S(1)}, bf16[512,512]{1,0:T(8,128)(2,1)S(1)}) custom-call(bf16[512,1024]{1,0:T(8,128)(2,1)S(1)} %get-tuple-element.41.x_in, bf16[512,512]{1,0:T(8,128)(2,1)S(1)} %get-tuple-element.42.narrow, bf16[512,512]{1,0:T(8,128)(2,1)S(1)} %collective-permute-done.23.partner, f32[4,1024]{1,0:T(4,128)S(1)} %copy-done.4, ...), custom_call_target="tpu_custom_call" | custom-call | flops 1879048192 | bytes 7864320 | tf_op jit(solution)/shard_map/slot_block/pallas_call | solution.py:264
  69.0 2.7 %slot_block.2 = (bf16[512,1024]{1,0:T(8,128)(2,1)S(1)}, bf16[512,512]{1,0:T(8,128)(2,1)S(1)}) custom-call(bf16[512,1024]{1,0:T(8,128)(2,1)S(1)} %get-tuple-element.29.x_in, bf16[512,512]{1,0:T(8,128)(2,1)S(1)} %get-tuple-element.30.narrow, bf16[512,512]{1,0:T(8,128)(2,1)S(1)} %collective-permute-done.7.partner, f32[4,1024]{1,0:T(4,128)S(1)} %copy-done.4, ...), custom_call_target="tpu_custom_call" | custom-call | flops 1879048192 | bytes 7864320 | tf_op jit(solution)/shard_map/slot_block/pallas_call | solution.py:264
  71.7 0.6 collective-permute-start.8
  72.3 7.1 %rest.3 = (bf16[64,1024]{1,0:T(8,128)(2,1)S(1)}, bf16[64,1024]{1,0:T(8,128)(2,1)S(1)}, bf16[64,1024]{1,0:T(8,128)(2,1)S(1)}, bf16[64,1024]{1,0:T(8,128)(2,1)S(1)...) custom-call(bf16[512,1024]{1,0:T(8,128)(2,1)S(1)} %get-tuple-element, ...), custom_call_target="tpu_custom_call" | custom-call | flops 5637144576 | bytes 15204352 | tf_op jit(solution)/shard_map/rest/pallas_call | solution.py:266
  79.3 3.2 %collective-permute-start.25 = (bf16[64,1024]{1,0:T(8,128)(2,1)S(1)}, bf16[64,1024]{1,0:T(8,128)(2,1)S(1)}, u32[]{:S(2)}, u32[]{:S(2)}) collective-permute-start(bf16[64,1024]{1,0:T(8,128)(2,1)S(1)} %get-tuple-element.46), channel_id=1, source_target_pairs={{0,12},{1,13},{2,14},{3,15},{4,8},{5,9},{6,10},{7,11},{8,4},{9,5},... | collective-permute-start | bytes 393224 | tf_op jit(solution)/shard_map/ppermute | solution.py:192
  82.5 1.4 %collective-permute-start.26 = (bf16[64,1024]{1,0:T(8,128)(2,1)S(1)}, bf16[64,1024]{1,0:T(8,128)(2,1)S(1)}, u32[]{:S(2)}, u32[]{:S(2)}) collective-permute-start(bf16[64,1024]{1,0:T(8,128)(2,1)S(1)} %get-tuple-element.47), channel_id=1, source_target_pairs={{0,14},{1,15},{2,12},{3,13},{4,10},{5,11},{6,8},{7,9},{8,6},{9,7},... | collective-permute-start | bytes 393224 | tf_op jit(solution)/shard_map/ppermute | solution.py:192
  83.9 2.3 %collective-permute-start.28 = (bf16[64,1024]{1,0:T(8,128)(2,1)S(1)}, bf16[64,1024]{1,0:T(8,128)(2,1)S(1)}, u32[]{:S(2)}, u32[]{:S(2)}) collective-permute-start(bf16[64,1024]{1,0:T(8,128)(2,1)S(1)} %get-tuple-element.49), channel_id=1, source_target_pairs={{0,6},{1,7},{2,4},{3,5},{4,2},{5,3},{6,0},{7,1},{8,14},{9,15},{10,... | collective-permute-start | bytes 393224 | tf_op jit(solution)/shard_map/ppermute | solution.py:192
  86.2 1.7 %collective-permute-start.29 = (bf16[64,1024]{1,0:T(8,128)(2,1)S(1)}, bf16[64,1024]{1,0:T(8,128)(2,1)S(1)}, u32[]{:S(2)}, u32[]{:S(2)}) collective-permute-start(bf16[64,1024]{1,0:T(8,128)(2,1)S(1)} %get-tuple-element.50), channel_id=1, source_target_pairs={{0,8},{1,9},{2,10},{3,11},{4,12},{5,13},{6,14},{7,15},{8,0},{9,1},... | collective-permute-start | bytes 393224 | tf_op jit(solution)/shard_map/ppermute | solution.py:192
  87.8 6.8 %rest.2 = (bf16[64,1024]{1,0:T(8,128)(2,1)S(1)}, bf16[64,1024]{1,0:T(8,128)(2,1)S(1)}, bf16[64,1024]{1,0:T(8,128)(2,1)S(1)}, bf16[64,1024]{1,0:T(8,128)(2,1)S(1)...) custom-call(bf16[512,1024]{1,0:T(8,128)(2,1)S(1)} %get-tuple-element, ...), custom_call_target="tpu_custom_call" | custom-call | flops 5637144576 | bytes 15204352 | tf_op jit(solution)/shard_map/rest/pallas_call | solution.py:266
  94.7 2.0 %collective-permute-start.30 = (bf16[64,1024]{1,0:T(8,128)(2,1)S(1)}, bf16[64,1024]{1,0:T(8,128)(2,1)S(1)}, u32[]{:S(2)}, u32[]{:S(2)}) collective-permute-start(bf16[64,1024]{1,0:T(8,128)(2,1)S(1)} %get-tuple-element.51), channel_id=1, source_target_pairs={{0,10},{1,11},{2,8},{3,9},{4,14},{5,15},{6,12},{7,13},{8,2},{9,3},... | collective-permute-start | bytes 393224 | tf_op jit(solution)/shard_map/ppermute | solution.py:192
  96.7 0.8 collective-permute-start.31
  97.5 3.1 %collective-permute-start.11 = (bf16[64,1024]{1,0:T(8,128)(2,1)S(1)}, bf16[64,1024]{1,0:T(8,128)(2,1)S(1)}, u32[]{:S(2)}, u32[]{:S(2)}) collective-permute-start(bf16[64,1024]{1,0:T(8,128)(2,1)S(1)} %get-tuple-element.36), channel_id=1, source_target_pairs={{0,12},{1,13},{2,14},{3,15},{4,8},{5,9},{6,10},{7,11},{8,4},{9,5},... | collective-permute-start | bytes 393224 | tf_op jit(solution)/shard_map/ppermute | solution.py:192
  100.6 1.5 %collective-permute-start.12 = (bf16[64,1024]{1,0:T(8,128)(2,1)S(1)}, bf16[64,1024]{1,0:T(8,128)(2,1)S(1)}, u32[]{:S(2)}, u32[]{:S(2)}) collective-permute-start(bf16[64,1024]{1,0:T(8,128)(2,1)S(1)} %get-tuple-element.37), channel_id=1, source_target_pairs={{0,14},{1,15},{2,12},{3,13},{4,10},{5,11},{6,8},{7,9},{8,6},{9,7},... | collective-permute-start | bytes 393224 | tf_op jit(solution)/shard_map/ppermute | solution.py:192
  102.1 8.4 %collective-permute-done.30.refs_6_ = bf16[64,1024]{1,0:T(8,128)(2,1)S(1)} collective-permute-done((bf16[64,1024]{1,0:T(8,128)(2,1)S(1)}, bf16[64,1024]{1,0:T(8,128)(2,1)S(1)}, u32[]{:S(2)}, u32[]{:S(2)}) %collective-permute-start.30) | collective-permute-done | bytes 131104 | tf_op jit(solution)/shard_map/ppermute | solution.py:192
  110.5 1.2 collective-permute-start.15
  111.8 3.4 %collective-permute-start.9 = (bf16[64,1024]{1,0:T(8,128)(2,1)S(1)}, bf16[64,1024]{1,0:T(8,128)(2,1)S(1)}, u32[]{:S(2)}, u32[]{:S(2)}) collective-permute-start(bf16[64,1024]{1,0:T(8,128)(2,1)S(1)} %get-tuple-element.33), channel_id=1, source_target_pairs={{0,8},{1,9},{2,10},{3,11},{4,12},{5,13},{6,14},{7,15},{8,0},{9,1},... | collective-permute-start | bytes 393224 | tf_op jit(solution)/shard_map/ppermute | solution.py:192
  115.2 7.0 %collective-permute-start.10 = (bf16[64,1024]{1,0:T(8,128)(2,1)S(1)}, bf16[64,1024]{1,0:T(8,128)(2,1)S(1)}, u32[]{:S(2)}, u32[]{:S(2)}) collective-permute-start(bf16[64,1024]{1,0:T(8,128)(2,1)S(1)} %get-tuple-element.34), channel_id=1, source_target_pairs={{0,10},{1,11},{2,8},{3,9},{4,14},{5,15},{6,12},{7,13},{8,2},{9,3},... | collective-permute-start | bytes 393224 | tf_op jit(solution)/shard_map/ppermute | solution.py:192
  122.2 1.1 collect.3.refs_6_
  123.3 1.0 collect.4.refs_2_
  124.3 3.9 %collective-permute-done.10.refs_1_ = bf16[64,1024]{1,0:T(8,128)(2,1)S(1)} collective-permute-done((bf16[64,1024]{1,0:T(8,128)(2,1)S(1)}, bf16[64,1024]{1,0:T(8,128)(2,1)S(1)}, u32[]{:S(2)}, u32[]{:S(2)}) %collective-permute-start.10) | collective-permute-done | bytes 131104 | tf_op jit(solution)/shard_map/ppermute | solution.py:192
  128.2 0.7 collect.5
  (48 shorter events, 0.7 us)
Async XLA Ops:
  1.0 12.8 %collective-permute-start.21 = (bf16[64,1024]{1,0:T(8,128)(2,1)S(1)}, bf16[64,1024]{1,0:T(8,128)(2,1)S(1)}, u32[]{:S(2)}, u32[]{:S(2)}) collective-permute-start(bf16[64,1024]{1,0:T(8,128)(2,1)S(1)} %bitcast.65), channel_id=1, source_target_pairs={{0,12},{1,13},{2,14},{3,15},{4,8},{5,9},{6,10},{7,11},{8,4},{9,5},... | collective-permute-start | bytes 393224 | tf_op jit(solution)/shard_map/ppermute | solution.py:192
  6.1 15.4 %collective-permute-start.22 = (bf16[64,1024]{1,0:T(8,128)(2,1)S(1)}, bf16[64,1024]{1,0:T(8,128)(2,1)S(1)}, u32[]{:S(2)}, u32[]{:S(2)}) collective-permute-start(bf16[64,1024]{1,0:T(8,128)(2,1)S(1)} %bitcast.64), channel_id=1, source_target_pairs={{0,14},{1,15},{2,12},{3,13},{4,10},{5,11},{6,8},{7,9},{8,6},{9,7},... | collective-permute-start | bytes 393224 | tf_op jit(solution)/shard_map/ppermute | solution.py:192
  8.6 21.6 %collective-permute-start.19 = (bf16[64,1024]{1,0:T(8,128)(2,1)S(1)}, bf16[64,1024]{1,0:T(8,128)(2,1)S(1)}, u32[]{:S(2)}, u32[]{:S(2)}) collective-permute-start(bf16[64,1024]{1,0:T(8,128)(2,1)S(1)} %bitcast.70), channel_id=1, source_target_pairs={{0,8},{1,9},{2,10},{3,11},{4,12},{5,13},{6,14},{7,15},{8,0},{9,1},... | collective-permute-start | bytes 393224 | tf_op jit(solution)/shard_map/ppermute | solution.py:192
  9.5 20.8 %collective-permute-start.20 = (bf16[64,1024]{1,0:T(8,128)(2,1)S(1)}, bf16[64,1024]{1,0:T(8,128)(2,1)S(1)}, u32[]{:S(2)}, u32[]{:S(2)}) collective-permute-start(bf16[64,1024]{1,0:T(8,128)(2,1)S(1)} %bitcast.69), channel_id=1, source_target_pairs={{0,10},{1,11},{2,8},{3,9},{4,14},{5,15},{6,12},{7,13},{8,2},{9,3},... | collective-permute-start | bytes 393224 | tf_op jit(solution)/shard_map/ppermute | solution.py:192
  11.4 18.8 %collective-permute-start.18 = (bf16[64,1024]{1,0:T(8,128)(2,1)S(1)}, bf16[64,1024]{1,0:T(8,128)(2,1)S(1)}, u32[]{:S(2)}, u32[]{:S(2)}) collective-permute-start(bf16[64,1024]{1,0:T(8,128)(2,1)S(1)} %bitcast.68), channel_id=1, source_target_pairs={{0,6},{1,7},{2,4},{3,5},{4,2},{5,3},{6,0},{7,1},{8,14},{9,15},{10,... | collective-permute-start | bytes 393224 | tf_op jit(solution)/shard_map/ppermute | solution.py:192
  13.8 16.4 %collective-permute-start.17 = (bf16[64,1024]{1,0:T(8,128)(2,1)S(1)}, bf16[64,1024]{1,0:T(8,128)(2,1)S(1)}, u32[]{:S(2)}, u32[]{:S(2)}) collective-permute-start(bf16[64,1024]{1,0:T(8,128)(2,1)S(1)} %bitcast.67), channel_id=1, source_target_pairs={{0,4},{1,5},{2,6},{3,7},{4,0},{5,1},{6,2},{7,3},{8,12},{9,13},{10,... | collective-permute-start | bytes 393224 | tf_op jit(solution)/shard_map/ppermute | solution.py:192
  21.5 8.7 %collective-permute-start.16 = (bf16[64,1024]{1,0:T(8,128)(2,1)S(1)}, bf16[64,1024]{1,0:T(8,128)(2,1)S(1)}, u32[]{:S(2)}, u32[]{:S(2)}) collective-permute-start(bf16[64,1024]{1,0:T(8,128)(2,1)S(1)} %bitcast.66), channel_id=1, source_target_pairs={{0,2},{1,3},{2,0},{3,1},{4,6},{5,7},{6,4},{7,5},{8,10},{9,11},{10,... | collective-permute-start | bytes 393224 | tf_op jit(solution)/shard_map/ppermute | solution.py:192
  23.0 2.8 %copy-start = (bf16[4,3,512,512]{3,2,1,0:T(8,128)(2,1)S(1)}, bf16[4,3,512,512]{3,2,1,0:T(8,128)(2,1)}, u32[]{:S(2)}) copy-start(bf16[4,3,512,512]{3,2,1,0:T(8,128)(2,1)} %taps.9) | copy-start | bytes 18874372
  25.8 2.2 %copy-start.1 = (bf16[4,1024,512]{2,1,0:T(8,128)(2,1)S(1)}, bf16[4,1024,512]{2,1,0:T(8,128)(2,1)}, u32[]{:S(2)}) copy-start(bf16[4,1024,512]{2,1,0:T(8,128)(2,1)} %proj.9) | copy-start | bytes 12582916
  28.0 2.2 %copy-start.2 = (bf16[4,512,1024]{2,1,0:T(8,128)(2,1)S(1)}, bf16[4,512,1024]{2,1,0:T(8,128)(2,1)}, u32[]{:S(2)}) copy-start(bf16[4,512,1024]{2,1,0:T(8,128)(2,1)} %output.9) | copy-start | bytes 12582916
  30.2 0.7 copy-start.4
  30.2 0.7 copy-start.5
  30.9 1.6 %copy-start.6 = (bf16[1024,1024]{1,0:T(8,128)(2,1)S(1)}, bf16[1024,1024]{1,0:T(8,128)(2,1)}, u32[]{:S(2)}) copy-start(bf16[1024,1024]{1,0:T(8,128)(2,1)} %param.6) | copy-start | bytes 6291460
  30.9 34.5 %slice-start = ((s8[6291456]{0:T(1024)(128)(4,1)}), s8[4194304]{0:T(1024)(128)(4,1)S(1)}, s32[]{:S(2)}) async-start(s8[6291456]{0:T(1024)(128)(4,1)} %bitcast.50), calls=%async_computation | async-start | bytes 8388608
  32.2 33.3 %slice-start.1 = ((s8[6291456]{0:T(1024)(128)(4,1)}), s8[2097152]{0:T(1024)(128)(4,1)S(1)}, s32[]{:S(2)}) async-start(s8[6291456]{0:T(1024)(128)(4,1)} %bitcast.50), calls=%async_computation.1 | async-start | bytes 4194304
  32.2 33.2 %collective-permute-start.23 = (bf16[512,512]{1,0:T(8,128)(2,1)S(1)}, bf16[512,512]{1,0:T(8,128)(2,1)S(1)}, u32[]{:S(2)}, u32[]{:S(2)}) collective-permute-start(bf16[512,512]{1,0:T(8,128)(2,1)S(1)} %get-tuple-element.42.narrow), channel_id=1, source_target_pairs={{0,1},{1,0},{2,3},{3,2},{4,5},{5,4},{6,7},{7,6},{8,9},{9,8},{10,11... | collective-permute-start | bytes 1572872 | tf_op jit(solution)/shard_map/ppermute | solution.py:195
  32.6 7.9 %collective-permute-start.5 = (bf16[64,1024]{1,0:T(8,128)(2,1)S(1)}, bf16[64,1024]{1,0:T(8,128)(2,1)S(1)}, u32[]{:S(2)}, u32[]{:S(2)}) collective-permute-start(bf16[64,1024]{1,0:T(8,128)(2,1)S(1)} %bitcast.63), channel_id=1, source_target_pairs={{0,12},{1,13},{2,14},{3,15},{4,8},{5,9},{6,10},{7,11},{8,4},{9,5},... | collective-permute-start | bytes 393224 | tf_op jit(solution)/shard_map/ppermute | solution.py:192
  35.9 16.1 %collective-permute-start.6 = (bf16[64,1024]{1,0:T(8,128)(2,1)S(1)}, bf16[64,1024]{1,0:T(8,128)(2,1)S(1)}, u32[]{:S(2)}, u32[]{:S(2)}) collective-permute-start(bf16[64,1024]{1,0:T(8,128)(2,1)S(1)} %bitcast.62), channel_id=1, source_target_pairs={{0,14},{1,15},{2,12},{3,13},{4,10},{5,11},{6,8},{7,9},{8,6},{9,7},... | collective-permute-start | bytes 393224 | tf_op jit(solution)/shard_map/ppermute | solution.py:192
  36.5 20.6 %collective-permute-start.4 = (bf16[64,1024]{1,0:T(8,128)(2,1)S(1)}, bf16[64,1024]{1,0:T(8,128)(2,1)S(1)}, u32[]{:S(2)}, u32[]{:S(2)}) collective-permute-start(bf16[64,1024]{1,0:T(8,128)(2,1)S(1)} %bitcast.61), channel_id=1, source_target_pairs={{0,10},{1,11},{2,8},{3,9},{4,14},{5,15},{6,12},{7,13},{8,2},{9,3},... | collective-permute-start | bytes 393224 | tf_op jit(solution)/shard_map/ppermute | solution.py:192
  40.1 19.8 %collective-permute-start.3 = (bf16[64,1024]{1,0:T(8,128)(2,1)S(1)}, bf16[64,1024]{1,0:T(8,128)(2,1)S(1)}, u32[]{:S(2)}, u32[]{:S(2)}) collective-permute-start(bf16[64,1024]{1,0:T(8,128)(2,1)S(1)} %bitcast.60), channel_id=1, source_target_pairs={{0,8},{1,9},{2,10},{3,11},{4,12},{5,13},{6,14},{7,15},{8,0},{9,1},... | collective-permute-start | bytes 393224 | tf_op jit(solution)/shard_map/ppermute | solution.py:192
  40.6 21.3 %collective-permute-start.2 = (bf16[64,1024]{1,0:T(8,128)(2,1)S(1)}, bf16[64,1024]{1,0:T(8,128)(2,1)S(1)}, u32[]{:S(2)}, u32[]{:S(2)}) collective-permute-start(bf16[64,1024]{1,0:T(8,128)(2,1)S(1)} %bitcast.59), channel_id=1, source_target_pairs={{0,6},{1,7},{2,4},{3,5},{4,2},{5,3},{6,0},{7,1},{8,14},{9,15},{10,... | collective-permute-start | bytes 393224 | tf_op jit(solution)/shard_map/ppermute | solution.py:192
  51.9 12.2 %collective-permute-start.1 = (bf16[64,1024]{1,0:T(8,128)(2,1)S(1)}, bf16[64,1024]{1,0:T(8,128)(2,1)S(1)}, u32[]{:S(2)}, u32[]{:S(2)}) collective-permute-start(bf16[64,1024]{1,0:T(8,128)(2,1)S(1)} %bitcast.58), channel_id=1, source_target_pairs={{0,4},{1,5},{2,6},{3,7},{4,0},{5,1},{6,2},{7,3},{8,12},{9,13},{10,... | collective-permute-start | bytes 393224 | tf_op jit(solution)/shard_map/ppermute | solution.py:192
  57.1 7.0 %collective-permute-start = (bf16[64,1024]{1,0:T(8,128)(2,1)S(1)}, bf16[64,1024]{1,0:T(8,128)(2,1)S(1)}, u32[]{:S(2)}, u32[]{:S(2)}) collective-permute-start(bf16[64,1024]{1,0:T(8,128)(2,1)S(1)} %bitcast.57), channel_id=1, source_target_pairs={{0,2},{1,3},{2,0},{3,1},{4,6},{5,7},{6,4},{7,5},{8,10},{9,11},{10,... | collective-permute-start | bytes 393224 | tf_op jit(solution)/shard_map/ppermute | solution.py:192
  64.1 2.2 %copy-start.3 = (bf16[4,512,1024]{2,1,0:T(8,128)(2,1)S(1)}, bf16[4,512,1024]{2,1,0:T(8,128)(2,1)}, u32[]{:S(2)}) copy-start(bf16[4,512,1024]{2,1,0:T(8,128)(2,1)} %output.9) | copy-start | bytes 12582916
  65.4 3.7 %collective-permute-start.7 = (bf16[512,512]{1,0:T(8,128)(2,1)S(1)}, bf16[512,512]{1,0:T(8,128)(2,1)S(1)}, u32[]{:S(2)}, u32[]{:S(2)}) collective-permute-start(bf16[512,512]{1,0:T(8,128)(2,1)S(1)} %get-tuple-element.30.narrow), channel_id=1, source_target_pairs={{0,1},{1,0},{2,3},{3,2},{4,5},{5,4},{6,7},{7,6},{8,9},{9,8},{10,11... | collective-permute-start | bytes 1572872 | tf_op jit(solution)/shard_map/ppermute | solution.py:195
  69.0 3.3 %collective-permute-start.24 = (bf16[512,512]{1,0:T(8,128)(2,1)S(1)}, bf16[512,512]{1,0:T(8,128)(2,1)S(1)}, u32[]{:S(2)}, u32[]{:S(2)}) collective-permute-start(bf16[512,512]{1,0:T(8,128)(2,1)S(1)} %get-tuple-element.44.narrow), channel_id=1, source_target_pairs={{0,1},{1,0},{2,3},{3,2},{4,5},{5,4},{6,7},{7,6},{8,9},{9,8},{10,11... | collective-permute-start | bytes 1572872 | tf_op jit(solution)/shard_map/ppermute | solution.py:195
  71.7 14.5 %collective-permute-start.8 = (bf16[512,512]{1,0:T(8,128)(2,1)S(1)}, bf16[512,512]{1,0:T(8,128)(2,1)S(1)}, u32[]{:S(2)}, u32[]{:S(2)}) collective-permute-start(bf16[512,512]{1,0:T(8,128)(2,1)S(1)} %get-tuple-element.32.narrow), channel_id=1, source_target_pairs={{0,1},{1,0},{2,3},{3,2},{4,5},{5,4},{6,7},{7,6},{8,9},{9,8},{10,11... | collective-permute-start | bytes 1572872 | tf_op jit(solution)/shard_map/ppermute | solution.py:195
  79.3 15.3 %collective-permute-start.25 = (bf16[64,1024]{1,0:T(8,128)(2,1)S(1)}, bf16[64,1024]{1,0:T(8,128)(2,1)S(1)}, u32[]{:S(2)}, u32[]{:S(2)}) collective-permute-start(bf16[64,1024]{1,0:T(8,128)(2,1)S(1)} %get-tuple-element.46), channel_id=1, source_target_pairs={{0,12},{1,13},{2,14},{3,15},{4,8},{5,9},{6,10},{7,11},{8,4},{9,5},... | collective-permute-start | bytes 393224 | tf_op jit(solution)/shard_map/ppermute | solution.py:192
  82.5 14.1 %collective-permute-start.26 = (bf16[64,1024]{1,0:T(8,128)(2,1)S(1)}, bf16[64,1024]{1,0:T(8,128)(2,1)S(1)}, u32[]{:S(2)}, u32[]{:S(2)}) collective-permute-start(bf16[64,1024]{1,0:T(8,128)(2,1)S(1)} %get-tuple-element.47), channel_id=1, source_target_pairs={{0,14},{1,15},{2,12},{3,13},{4,10},{5,11},{6,8},{7,9},{8,6},{9,7},... | collective-permute-start | bytes 393224 | tf_op jit(solution)/shard_map/ppermute | solution.py:192
  83.9 13.6 %collective-permute-start.27 = (bf16[64,1024]{1,0:T(8,128)(2,1)S(1)}, bf16[64,1024]{1,0:T(8,128)(2,1)S(1)}, u32[]{:S(2)}, u32[]{:S(2)}) collective-permute-start(bf16[64,1024]{1,0:T(8,128)(2,1)S(1)} %get-tuple-element.48), channel_id=1, source_target_pairs={{0,4},{1,5},{2,6},{3,7},{4,0},{5,1},{6,2},{7,3},{8,12},{9,13},{10,... | collective-permute-start | bytes 393224 | tf_op jit(solution)/shard_map/ppermute | solution.py:192
  83.9 16.7 %collective-permute-start.28 = (bf16[64,1024]{1,0:T(8,128)(2,1)S(1)}, bf16[64,1024]{1,0:T(8,128)(2,1)S(1)}, u32[]{:S(2)}, u32[]{:S(2)}) collective-permute-start(bf16[64,1024]{1,0:T(8,128)(2,1)S(1)} %get-tuple-element.49), channel_id=1, source_target_pairs={{0,6},{1,7},{2,4},{3,5},{4,2},{5,3},{6,0},{7,1},{8,14},{9,15},{10,... | collective-permute-start | bytes 393224 | tf_op jit(solution)/shard_map/ppermute | solution.py:192
  86.2 15.9 %collective-permute-start.29 = (bf16[64,1024]{1,0:T(8,128)(2,1)S(1)}, bf16[64,1024]{1,0:T(8,128)(2,1)S(1)}, u32[]{:S(2)}, u32[]{:S(2)}) collective-permute-start(bf16[64,1024]{1,0:T(8,128)(2,1)S(1)} %get-tuple-element.50), channel_id=1, source_target_pairs={{0,8},{1,9},{2,10},{3,11},{4,12},{5,13},{6,14},{7,15},{8,0},{9,1},... | collective-permute-start | bytes 393224 | tf_op jit(solution)/shard_map/ppermute | solution.py:192
  94.7 15.8 %collective-permute-start.30 = (bf16[64,1024]{1,0:T(8,128)(2,1)S(1)}, bf16[64,1024]{1,0:T(8,128)(2,1)S(1)}, u32[]{:S(2)}, u32[]{:S(2)}) collective-permute-start(bf16[64,1024]{1,0:T(8,128)(2,1)S(1)} %get-tuple-element.51), channel_id=1, source_target_pairs={{0,10},{1,11},{2,8},{3,9},{4,14},{5,15},{6,12},{7,13},{8,2},{9,3},... | collective-permute-start | bytes 393224 | tf_op jit(solution)/shard_map/ppermute | solution.py:192
  96.7 13.8 %collective-permute-start.31 = (bf16[64,1024]{1,0:T(8,128)(2,1)S(1)}, bf16[64,1024]{1,0:T(8,128)(2,1)S(1)}, u32[]{:S(2)}, u32[]{:S(2)}) collective-permute-start(bf16[64,1024]{1,0:T(8,128)(2,1)S(1)} %get-tuple-element.52), channel_id=1, source_target_pairs={{0,2},{1,3},{2,0},{3,1},{4,6},{5,7},{6,4},{7,5},{8,10},{9,11},{10,... | collective-permute-start | bytes 393224 | tf_op jit(solution)/shard_map/ppermute | solution.py:192
  97.5 14.3 %collective-permute-start.11 = (bf16[64,1024]{1,0:T(8,128)(2,1)S(1)}, bf16[64,1024]{1,0:T(8,128)(2,1)S(1)}, u32[]{:S(2)}, u32[]{:S(2)}) collective-permute-start(bf16[64,1024]{1,0:T(8,128)(2,1)S(1)} %get-tuple-element.36), channel_id=1, source_target_pairs={{0,12},{1,13},{2,14},{3,15},{4,8},{5,9},{6,10},{7,11},{8,4},{9,5},... | collective-permute-start | bytes 393224 | tf_op jit(solution)/shard_map/ppermute | solution.py:192
  100.6 14.6 %collective-permute-start.12 = (bf16[64,1024]{1,0:T(8,128)(2,1)S(1)}, bf16[64,1024]{1,0:T(8,128)(2,1)S(1)}, u32[]{:S(2)}, u32[]{:S(2)}) collective-permute-start(bf16[64,1024]{1,0:T(8,128)(2,1)S(1)} %get-tuple-element.37), channel_id=1, source_target_pairs={{0,14},{1,15},{2,12},{3,13},{4,10},{5,11},{6,8},{7,9},{8,6},{9,7},... | collective-permute-start | bytes 393224 | tf_op jit(solution)/shard_map/ppermute | solution.py:192
  102.1 21.2 %collective-permute-start.13 = (bf16[64,1024]{1,0:T(8,128)(2,1)S(1)}, bf16[64,1024]{1,0:T(8,128)(2,1)S(1)}, u32[]{:S(2)}, u32[]{:S(2)}) collective-permute-start(bf16[64,1024]{1,0:T(8,128)(2,1)S(1)} %get-tuple-element.38), channel_id=1, source_target_pairs={{0,4},{1,5},{2,6},{3,7},{4,0},{5,1},{6,2},{7,3},{8,12},{9,13},{10,... | collective-permute-start | bytes 393224 | tf_op jit(solution)/shard_map/ppermute | solution.py:192
  110.5 12.8 %collective-permute-start.14 = (bf16[64,1024]{1,0:T(8,128)(2,1)S(1)}, bf16[64,1024]{1,0:T(8,128)(2,1)S(1)}, u32[]{:S(2)}, u32[]{:S(2)}) collective-permute-start(bf16[64,1024]{1,0:T(8,128)(2,1)S(1)} %get-tuple-element.39), channel_id=1, source_target_pairs={{0,6},{1,7},{2,4},{3,5},{4,2},{5,3},{6,0},{7,1},{8,14},{9,15},{10,... | collective-permute-start | bytes 393224 | tf_op jit(solution)/shard_map/ppermute | solution.py:192
  110.5 12.8 %collective-permute-start.15 = (bf16[64,1024]{1,0:T(8,128)(2,1)S(1)}, bf16[64,1024]{1,0:T(8,128)(2,1)S(1)}, u32[]{:S(2)}, u32[]{:S(2)}) collective-permute-start(bf16[64,1024]{1,0:T(8,128)(2,1)S(1)} %get-tuple-element.40), channel_id=1, source_target_pairs={{0,2},{1,3},{2,0},{3,1},{4,6},{5,7},{6,4},{7,5},{8,10},{9,11},{10,... | collective-permute-start | bytes 393224 | tf_op jit(solution)/shard_map/ppermute | solution.py:192
  111.8 12.6 %collective-permute-start.9 = (bf16[64,1024]{1,0:T(8,128)(2,1)S(1)}, bf16[64,1024]{1,0:T(8,128)(2,1)S(1)}, u32[]{:S(2)}, u32[]{:S(2)}) collective-permute-start(bf16[64,1024]{1,0:T(8,128)(2,1)S(1)} %get-tuple-element.33), channel_id=1, source_target_pairs={{0,8},{1,9},{2,10},{3,11},{4,12},{5,13},{6,14},{7,15},{8,0},{9,1},... | collective-permute-start | bytes 393224 | tf_op jit(solution)/shard_map/ppermute | solution.py:192
  115.2 13.0 %collective-permute-start.10 = (bf16[64,1024]{1,0:T(8,128)(2,1)S(1)}, bf16[64,1024]{1,0:T(8,128)(2,1)S(1)}, u32[]{:S(2)}, u32[]{:S(2)}) collective-permute-start(bf16[64,1024]{1,0:T(8,128)(2,1)S(1)} %get-tuple-element.34), channel_id=1, source_target_pairs={{0,10},{1,11},{2,8},{3,9},{4,14},{5,15},{6,12},{7,13},{8,2},{9,3},... | collective-permute-start | bytes 393224 | tf_op jit(solution)/shard_map/ppermute | solution.py:192

commit v6 on v5

--- a/solution.py
+++ b/solution.py
@@ -273,7 +273,7 @@
     leave = [0, *leave_order(chips)]
     late = travel_order(chips)[1][2:]
     groups = [(j, leave) for j in range(chunks - 1)]
-    groups += [(chunks - 1, [k for k in leave if k not in late]), (chunks - 1, late)]
+    groups.append((chunks - 1, [k for k in leave if k not in late]))
     for n, (j, ways) in enumerate(groups):
         collect = pl.pallas_call(
             functools.partial(collect_kernel, ways, slots, part, chunks, j),
@@ -286,6 +286,9 @@
             name="collect",
         )
         result = collect(*[left[j][k] for k in ways], *([result] if n else []))
+    for k in late:
+        piece = left[-1][k].reshape(slots, 1, part, model)
+        result = lax.dynamic_update_slice_in_dim(result, piece, (chip ^ k) * chunks + chunks - 1, axis=1)
     return result.reshape(rows, model)
 
 

time: 129 us -> 129 us (level)
  local copies, waits for them, and re-layouts: 11.3 us -> 12.6 us
    dynamic_update_slice x0 -> x2, local copies, waits for them, and re-layouts: none -> 1.33 us  [body(): lax.dynamic_update_slice_in_dim(result, piece, (chip ^ k) * chunks + chun...]
    pallas_call x3 -> x2, Pallas kernels: 2.8 us -> 2.07 us  [body(): result = collect(*[left[j][k] for k in ways], *([result] if n else []))]
  transfers between devices with their start and end apart: 32 -> 32, of which waited for: 6 -> 6; matrix products, arithmetic and copies ran while one was open for 1% -> 2% of each run, Pallas kernels for 17% -> 17%
where the time goes in v6:
time: 129 us
  starting transfers between devices  72.7 us (56%)
  Pallas kernels  23.8 us (18%)
  waiting for transfers between devices  19.5 us (15%)
  local copies, waits for them, and re-layouts  12.6 us (10%)
    ppermute x28, starting transfers between devices, to_chip(): lax.ppermute(piece, 'blk', [(i, i ^ k * CORES) for i in range(peers)])  72 us
    ppermute x28, waiting for transfers between devices, to_chip(): lax.ppermute(piece, 'blk', [(i, i ^ k * CORES) for i in range(peers)])  19.5 us
    pallas_call x2, Pallas kernels, body(): pieces = rest(x, narrow, partner, *weights)  13.9 us
    unnamed x18, local copies, waits for them, and re-layouts  8.92 us
    pallas_call x2, Pallas kernels, body(): x, narrow = slot_block(x, narrow, partner, *weights)  5.31 us
  transfers between devices with their start and end apart: 32, of which 6 were waited for; matrix products, arithmetic and copies ran while one was open for 2% of the time, Pallas kernels for 17%

profile of v6, /device:TPU:0, one launch (start us, length us, event | category | flops | bytes accessed | tf_op | source)
XLA Modules:
  0.0 128.9 jit_solution(16362492232450283376)
XLA Ops:
  0.0 1.0 constant_dynamic-slice_fusion
  1.0 5.1 %collective-permute-start.19 = (bf16[64,1024]{1,0:T(8,128)(2,1)S(1)}, bf16[64,1024]{1,0:T(8,128)(2,1)S(1)}, u32[]{:S(2)}, u32[]{:S(2)}) collective-permute-start(bf16[64,1024]{1,0:T(8,128)(2,1)S(1)} %bitcast.69), channel_id=1, source_target_pairs={{0,12},{1,13},{2,14},{3,15},{4,8},{5,9},{6,10},{7,11},{8,4},{9,5},... | collective-permute-start | bytes 393224 | tf_op jit(solution)/shard_map/ppermute | solution.py:192
  6.1 1.2 collective-permute-start.20
  7.3 1.3 constant_dynamic-slice_fusion.2
  8.6 0.9 collective-permute-start.17
  9.5 1.9 %collective-permute-start.18 = (bf16[64,1024]{1,0:T(8,128)(2,1)S(1)}, bf16[64,1024]{1,0:T(8,128)(2,1)S(1)}, u32[]{:S(2)}, u32[]{:S(2)}) collective-permute-start(bf16[64,1024]{1,0:T(8,128)(2,1)S(1)} %bitcast.73), channel_id=1, source_target_pairs={{0,10},{1,11},{2,8},{3,9},{4,14},{5,15},{6,12},{7,13},{8,2},{9,3},... | collective-permute-start | bytes 393224 | tf_op jit(solution)/shard_map/ppermute | solution.py:192
  11.4 2.4 %collective-permute-start.16 = (bf16[64,1024]{1,0:T(8,128)(2,1)S(1)}, bf16[64,1024]{1,0:T(8,128)(2,1)S(1)}, u32[]{:S(2)}, u32[]{:S(2)}) collective-permute-start(bf16[64,1024]{1,0:T(8,128)(2,1)S(1)} %bitcast.72), channel_id=1, source_target_pairs={{0,6},{1,7},{2,4},{3,5},{4,2},{5,3},{6,0},{7,1},{8,14},{9,15},{10,... | collective-permute-start | bytes 393224 | tf_op jit(solution)/shard_map/ppermute | solution.py:192
  13.8 7.7 %collective-permute-start.15 = (bf16[64,1024]{1,0:T(8,128)(2,1)S(1)}, bf16[64,1024]{1,0:T(8,128)(2,1)S(1)}, u32[]{:S(2)}, u32[]{:S(2)}) collective-permute-start(bf16[64,1024]{1,0:T(8,128)(2,1)S(1)} %bitcast.71), channel_id=1, source_target_pairs={{0,4},{1,5},{2,6},{3,7},{4,0},{5,1},{6,2},{7,3},{8,12},{9,13},{10,... | collective-permute-start | bytes 393224 | tf_op jit(solution)/shard_map/ppermute | solution.py:192
  21.5 1.5 %collective-permute-start.14 = (bf16[64,1024]{1,0:T(8,128)(2,1)S(1)}, bf16[64,1024]{1,0:T(8,128)(2,1)S(1)}, u32[]{:S(2)}, u32[]{:S(2)}) collective-permute-start(bf16[64,1024]{1,0:T(8,128)(2,1)S(1)} %bitcast.70), channel_id=1, source_target_pairs={{0,2},{1,3},{2,0},{3,1},{4,6},{5,7},{6,4},{7,5},{8,10},{9,11},{10,... | collective-permute-start | bytes 393224 | tf_op jit(solution)/shard_map/ppermute | solution.py:192
  23.0 2.8 %copy-done = bf16[4,3,512,512]{3,2,1,0:T(8,128)(2,1)S(1)} copy-done((bf16[4,3,512,512]{3,2,1,0:T(8,128)(2,1)S(1)}, bf16[4,3,512,512]{3,2,1,0:T(8,128)(2,1)}, u32[]{:S(2)}) %copy-start) | copy-done | bytes 6291480
  25.8 2.2 %copy-done.1 = bf16[4,1024,512]{2,1,0:T(8,128)(2,1)S(1)} copy-done((bf16[4,1024,512]{2,1,0:T(8,128)(2,1)S(1)}, bf16[4,1024,512]{2,1,0:T(8,128)(2,1)}, u32[]{:S(2)}) %copy-start.1) | copy-done | bytes 4194328
  28.0 2.2 %copy-done.2 = bf16[4,512,1024]{2,1,0:T(8,128)(2,1)S(1)} copy-done((bf16[4,512,1024]{2,1,0:T(8,128)(2,1)S(1)}, bf16[4,512,1024]{2,1,0:T(8,128)(2,1)}, u32[]{:S(2)}) %copy-start.2) | copy-done | bytes 4194328
  30.3 0.7 copy-done.4
  30.9 1.2 enter.3
  32.6 3.2 %collective-permute-start.5 = (bf16[64,1024]{1,0:T(8,128)(2,1)S(1)}, bf16[64,1024]{1,0:T(8,128)(2,1)S(1)}, u32[]{:S(2)}, u32[]{:S(2)}) collective-permute-start(bf16[64,1024]{1,0:T(8,128)(2,1)S(1)} %bitcast.65), channel_id=1, source_target_pairs={{0,12},{1,13},{2,14},{3,15},{4,8},{5,9},{6,10},{7,11},{8,4},{9,5},... | collective-permute-start | bytes 393224 | tf_op jit(solution)/shard_map/ppermute | solution.py:192
  35.9 0.6 collective-permute-start.6
  36.5 3.6 %collective-permute-start.4 = (bf16[64,1024]{1,0:T(8,128)(2,1)S(1)}, bf16[64,1024]{1,0:T(8,128)(2,1)S(1)}, u32[]{:S(2)}, u32[]{:S(2)}) collective-permute-start(bf16[64,1024]{1,0:T(8,128)(2,1)S(1)} %bitcast.63), channel_id=1, source_target_pairs={{0,10},{1,11},{2,8},{3,9},{4,14},{5,15},{6,12},{7,13},{8,2},{9,3},... | collective-permute-start | bytes 393224 | tf_op jit(solution)/shard_map/ppermute | solution.py:192
  40.6 11.4 %collective-permute-start.2 = (bf16[64,1024]{1,0:T(8,128)(2,1)S(1)}, bf16[64,1024]{1,0:T(8,128)(2,1)S(1)}, u32[]{:S(2)}, u32[]{:S(2)}) collective-permute-start(bf16[64,1024]{1,0:T(8,128)(2,1)S(1)} %bitcast.61), channel_id=1, source_target_pairs={{0,6},{1,7},{2,4},{3,5},{4,2},{5,3},{6,0},{7,1},{8,14},{9,15},{10,... | collective-permute-start | bytes 393224 | tf_op jit(solution)/shard_map/ppermute | solution.py:192
  51.9 2.8 %collective-permute-start.1 = (bf16[64,1024]{1,0:T(8,128)(2,1)S(1)}, bf16[64,1024]{1,0:T(8,128)(2,1)S(1)}, u32[]{:S(2)}, u32[]{:S(2)}) collective-permute-start(bf16[64,1024]{1,0:T(8,128)(2,1)S(1)} %bitcast.60), channel_id=1, source_target_pairs={{0,4},{1,5},{2,6},{3,7},{4,0},{5,1},{6,2},{7,3},{8,12},{9,13},{10,... | collective-permute-start | bytes 393224 | tf_op jit(solution)/shard_map/ppermute | solution.py:192
  54.8 2.3 %collective-permute-done.4.refs_5_ = bf16[64,1024]{1,0:T(8,128)(2,1)S(1)} collective-permute-done((bf16[64,1024]{1,0:T(8,128)(2,1)S(1)}, bf16[64,1024]{1,0:T(8,128)(2,1)S(1)}, u32[]{:S(2)}, u32[]{:S(2)}) %collective-permute-start.4) | collective-permute-done | bytes 131104 | tf_op jit(solution)/shard_map/ppermute | solution.py:192
  57.1 1.5 %collective-permute-start = (bf16[64,1024]{1,0:T(8,128)(2,1)S(1)}, bf16[64,1024]{1,0:T(8,128)(2,1)S(1)}, u32[]{:S(2)}, u32[]{:S(2)}) collective-permute-start(bf16[64,1024]{1,0:T(8,128)(2,1)S(1)} %bitcast.59), channel_id=1, source_target_pairs={{0,2},{1,3},{2,0},{3,1},{4,6},{5,7},{6,4},{7,5},{8,10},{9,11},{10,... | collective-permute-start | bytes 393224 | tf_op jit(solution)/shard_map/ppermute | solution.py:192
  58.6 1.3 collective-permute-done.3.refs_4_
  59.9 2.0 %collective-permute-done.2.refs_3_ = bf16[64,1024]{1,0:T(8,128)(2,1)S(1)} collective-permute-done((bf16[64,1024]{1,0:T(8,128)(2,1)S(1)}, bf16[64,1024]{1,0:T(8,128)(2,1)S(1)}, u32[]{:S(2)}, u32[]{:S(2)}) %collective-permute-start.2) | collective-permute-done | bytes 131104 | tf_op jit(solution)/shard_map/ppermute | solution.py:192
  61.9 2.2 %collective-permute-done.1.refs_2_ = bf16[64,1024]{1,0:T(8,128)(2,1)S(1)} collective-permute-done((bf16[64,1024]{1,0:T(8,128)(2,1)S(1)}, bf16[64,1024]{1,0:T(8,128)(2,1)S(1)}, u32[]{:S(2)}, u32[]{:S(2)}) %collective-permute-start.1) | collective-permute-done | bytes 131104 | tf_op jit(solution)/shard_map/ppermute | solution.py:192
  64.1 1.3 enter.2
  65.5 0.8 copy-done.3
  66.3 2.7 %slot_block.3 = (bf16[512,1024]{1,0:T(8,128)(2,1)S(1)}, bf16[512,512]{1,0:T(8,128)(2,1)S(1)}) custom-call(bf16[512,1024]{1,0:T(8,128)(2,1)S(1)} %get-tuple-element.39.x_in, bf16[512,512]{1,0:T(8,128)(2,1)S(1)} %get-tuple-element.40.narrow, bf16[512,512]{1,0:T(8,128)(2,1)S(1)} %collective-permute-done.21.partner, f32[4,1024]{1,0:T(4,128)S(1)} %copy-done.4, ...), custom_call_target="tpu_custom_call" | custom-call | flops 1879048192 | bytes 7864320 | tf_op jit(solution)/shard_map/slot_block/pallas_call | solution.py:264
  69.0 2.7 %slot_block.2 = (bf16[512,1024]{1,0:T(8,128)(2,1)S(1)}, bf16[512,512]{1,0:T(8,128)(2,1)S(1)}) custom-call(bf16[512,1024]{1,0:T(8,128)(2,1)S(1)} %get-tuple-element.29.x_in, bf16[512,512]{1,0:T(8,128)(2,1)S(1)} %get-tuple-element.30.narrow, bf16[512,512]{1,0:T(8,128)(2,1)S(1)} %collective-permute-done.7.partner, f32[4,1024]{1,0:T(4,128)S(1)} %copy-done.4, ...), custom_call_target="tpu_custom_call" | custom-call | flops 1879048192 | bytes 7864320 | tf_op jit(solution)/shard_map/slot_block/pallas_call | solution.py:264
  71.7 0.6 collective-permute-start.8
  72.3 7.1 %rest.3 = (bf16[64,1024]{1,0:T(8,128)(2,1)S(1)}, bf16[64,1024]{1,0:T(8,128)(2,1)S(1)}, bf16[64,1024]{1,0:T(8,128)(2,1)S(1)}, bf16[64,1024]{1,0:T(8,128)(2,1)S(1)...) custom-call(bf16[512,1024]{1,0:T(8,128)(2,1)S(1)} %get-tuple-element, ...), custom_call_target="tpu_custom_call" | custom-call | flops 5637144576 | bytes 15204352 | tf_op jit(solution)/shard_map/rest/pallas_call | solution.py:266
  79.3 3.2 %collective-permute-start.23 = (bf16[64,1024]{1,0:T(8,128)(2,1)S(1)}, bf16[64,1024]{1,0:T(8,128)(2,1)S(1)}, u32[]{:S(2)}, u32[]{:S(2)}) collective-permute-start(bf16[64,1024]{1,0:T(8,128)(2,1)S(1)} %get-tuple-element.44), channel_id=1, source_target_pairs={{0,12},{1,13},{2,14},{3,15},{4,8},{5,9},{6,10},{7,11},{8,4},{9,5},... | collective-permute-start | bytes 393224 | tf_op jit(solution)/shard_map/ppermute | solution.py:192
  82.5 1.4 %collective-permute-start.24 = (bf16[64,1024]{1,0:T(8,128)(2,1)S(1)}, bf16[64,1024]{1,0:T(8,128)(2,1)S(1)}, u32[]{:S(2)}, u32[]{:S(2)}) collective-permute-start(bf16[64,1024]{1,0:T(8,128)(2,1)S(1)} %get-tuple-element.45), channel_id=1, source_target_pairs={{0,14},{1,15},{2,12},{3,13},{4,10},{5,11},{6,8},{7,9},{8,6},{9,7},... | collective-permute-start | bytes 393224 | tf_op jit(solution)/shard_map/ppermute | solution.py:192
  83.9 2.3 %collective-permute-start.26 = (bf16[64,1024]{1,0:T(8,128)(2,1)S(1)}, bf16[64,1024]{1,0:T(8,128)(2,1)S(1)}, u32[]{:S(2)}, u32[]{:S(2)}) collective-permute-start(bf16[64,1024]{1,0:T(8,128)(2,1)S(1)} %get-tuple-element.47), channel_id=1, source_target_pairs={{0,6},{1,7},{2,4},{3,5},{4,2},{5,3},{6,0},{7,1},{8,14},{9,15},{10,... | collective-permute-start | bytes 393224 | tf_op jit(solution)/shard_map/ppermute | solution.py:192
  86.2 1.7 %collective-permute-start.27 = (bf16[64,1024]{1,0:T(8,128)(2,1)S(1)}, bf16[64,1024]{1,0:T(8,128)(2,1)S(1)}, u32[]{:S(2)}, u32[]{:S(2)}) collective-permute-start(bf16[64,1024]{1,0:T(8,128)(2,1)S(1)} %get-tuple-element.48), channel_id=1, source_target_pairs={{0,8},{1,9},{2,10},{3,11},{4,12},{5,13},{6,14},{7,15},{8,0},{9,1},... | collective-permute-start | bytes 393224 | tf_op jit(solution)/shard_map/ppermute | solution.py:192
  87.8 6.8 %rest.2 = (bf16[64,1024]{1,0:T(8,128)(2,1)S(1)}, bf16[64,1024]{1,0:T(8,128)(2,1)S(1)}, bf16[64,1024]{1,0:T(8,128)(2,1)S(1)}, bf16[64,1024]{1,0:T(8,128)(2,1)S(1)...) custom-call(bf16[512,1024]{1,0:T(8,128)(2,1)S(1)} %get-tuple-element, ...), custom_call_target="tpu_custom_call" | custom-call | flops 5637144576 | bytes 15204352 | tf_op jit(solution)/shard_map/rest/pallas_call | solution.py:266
  94.7 2.0 %collective-permute-start.28 = (bf16[64,1024]{1,0:T(8,128)(2,1)S(1)}, bf16[64,1024]{1,0:T(8,128)(2,1)S(1)}, u32[]{:S(2)}, u32[]{:S(2)}) collective-permute-start(bf16[64,1024]{1,0:T(8,128)(2,1)S(1)} %get-tuple-element.49), channel_id=1, source_target_pairs={{0,10},{1,11},{2,8},{3,9},{4,14},{5,15},{6,12},{7,13},{8,2},{9,3},... | collective-permute-start | bytes 393224 | tf_op jit(solution)/shard_map/ppermute | solution.py:192
  96.7 0.8 collective-permute-start.29
  97.5 3.1 %collective-permute-start.9 = (bf16[64,1024]{1,0:T(8,128)(2,1)S(1)}, bf16[64,1024]{1,0:T(8,128)(2,1)S(1)}, u32[]{:S(2)}, u32[]{:S(2)}) collective-permute-start(bf16[64,1024]{1,0:T(8,128)(2,1)S(1)} %get-tuple-element.34), channel_id=1, source_target_pairs={{0,12},{1,13},{2,14},{3,15},{4,8},{5,9},{6,10},{7,11},{8,4},{9,5},... | collective-permute-start | bytes 393224 | tf_op jit(solution)/shard_map/ppermute | solution.py:192
  100.6 1.5 %collective-permute-start.10 = (bf16[64,1024]{1,0:T(8,128)(2,1)S(1)}, bf16[64,1024]{1,0:T(8,128)(2,1)S(1)}, u32[]{:S(2)}, u32[]{:S(2)}) collective-permute-start(bf16[64,1024]{1,0:T(8,128)(2,1)S(1)} %get-tuple-element.35), channel_id=1, source_target_pairs={{0,14},{1,15},{2,12},{3,13},{4,10},{5,11},{6,8},{7,9},{8,6},{9,7},... | collective-permute-start | bytes 393224 | tf_op jit(solution)/shard_map/ppermute | solution.py:192
  102.1 8.4 %collective-permute-done.28.refs_6_ = bf16[64,1024]{1,0:T(8,128)(2,1)S(1)} collective-permute-done((bf16[64,1024]{1,0:T(8,128)(2,1)S(1)}, bf16[64,1024]{1,0:T(8,128)(2,1)S(1)}, u32[]{:S(2)}, u32[]{:S(2)}) %collective-permute-start.28) | collective-permute-done | bytes 131104 | tf_op jit(solution)/shard_map/ppermute | solution.py:192
  110.5 1.2 collective-permute-start.13
  111.8 3.4 %collective-permute-start.30 = (bf16[64,1024]{1,0:T(8,128)(2,1)S(1)}, bf16[64,1024]{1,0:T(8,128)(2,1)S(1)}, u32[]{:S(2)}, u32[]{:S(2)}) collective-permute-start(bf16[64,1024]{1,0:T(8,128)(2,1)S(1)} %get-tuple-element.51), channel_id=1, source_target_pairs={{0,8},{1,9},{2,10},{3,11},{4,12},{5,13},{6,14},{7,15},{8,0},{9,1},... | collective-permute-start | bytes 393224 | tf_op jit(solution)/shard_map/ppermute | solution.py:192
  115.2 7.0 %collective-permute-start.31 = (bf16[64,1024]{1,0:T(8,128)(2,1)S(1)}, bf16[64,1024]{1,0:T(8,128)(2,1)S(1)}, u32[]{:S(2)}, u32[]{:S(2)}) collective-permute-start(bf16[64,1024]{1,0:T(8,128)(2,1)S(1)} %get-tuple-element.52), channel_id=1, source_target_pairs={{0,10},{1,11},{2,8},{3,9},{4,14},{5,15},{6,12},{7,13},{8,2},{9,3},... | collective-permute-start | bytes 393224 | tf_op jit(solution)/shard_map/ppermute | solution.py:192
  122.2 1.1 collect.2.refs_6_
  123.3 1.0 collect.3
  124.3 0.7 constant_dynamic-update-slice_fusion.1
  125.0 3.2 %collective-permute-done.31 = bf16[64,1024]{1,0:T(8,128)(2,1)S(1)} collective-permute-done((bf16[64,1024]{1,0:T(8,128)(2,1)S(1)}, bf16[64,1024]{1,0:T(8,128)(2,1)S(1)}, u32[]{:S(2)}, u32[]{:S(2)}) %collective-permute-start.31) | collective-permute-done | bytes 131104 | tf_op jit(solution)/shard_map/ppermute | solution.py:192
  128.2 0.7 constant_dynamic-update-slice_fusion
  (49 shorter events, 1.1 us)
Async XLA Ops:
  1.0 12.8 %collective-permute-start.19 = (bf16[64,1024]{1,0:T(8,128)(2,1)S(1)}, bf16[64,1024]{1,0:T(8,128)(2,1)S(1)}, u32[]{:S(2)}, u32[]{:S(2)}) collective-permute-start(bf16[64,1024]{1,0:T(8,128)(2,1)S(1)} %bitcast.69), channel_id=1, source_target_pairs={{0,12},{1,13},{2,14},{3,15},{4,8},{5,9},{6,10},{7,11},{8,4},{9,5},... | collective-permute-start | bytes 393224 | tf_op jit(solution)/shard_map/ppermute | solution.py:192
  6.1 15.4 %collective-permute-start.20 = (bf16[64,1024]{1,0:T(8,128)(2,1)S(1)}, bf16[64,1024]{1,0:T(8,128)(2,1)S(1)}, u32[]{:S(2)}, u32[]{:S(2)}) collective-permute-start(bf16[64,1024]{1,0:T(8,128)(2,1)S(1)} %bitcast.68), channel_id=1, source_target_pairs={{0,14},{1,15},{2,12},{3,13},{4,10},{5,11},{6,8},{7,9},{8,6},{9,7},... | collective-permute-start | bytes 393224 | tf_op jit(solution)/shard_map/ppermute | solution.py:192
  8.6 21.6 %collective-permute-start.17 = (bf16[64,1024]{1,0:T(8,128)(2,1)S(1)}, bf16[64,1024]{1,0:T(8,128)(2,1)S(1)}, u32[]{:S(2)}, u32[]{:S(2)}) collective-permute-start(bf16[64,1024]{1,0:T(8,128)(2,1)S(1)} %bitcast.74), channel_id=1, source_target_pairs={{0,8},{1,9},{2,10},{3,11},{4,12},{5,13},{6,14},{7,15},{8,0},{9,1},... | collective-permute-start | bytes 393224 | tf_op jit(solution)/shard_map/ppermute | solution.py:192
  9.5 20.8 %collective-permute-start.18 = (bf16[64,1024]{1,0:T(8,128)(2,1)S(1)}, bf16[64,1024]{1,0:T(8,128)(2,1)S(1)}, u32[]{:S(2)}, u32[]{:S(2)}) collective-permute-start(bf16[64,1024]{1,0:T(8,128)(2,1)S(1)} %bitcast.73), channel_id=1, source_target_pairs={{0,10},{1,11},{2,8},{3,9},{4,14},{5,15},{6,12},{7,13},{8,2},{9,3},... | collective-permute-start | bytes 393224 | tf_op jit(solution)/shard_map/ppermute | solution.py:192
  11.4 18.8 %collective-permute-start.16 = (bf16[64,1024]{1,0:T(8,128)(2,1)S(1)}, bf16[64,1024]{1,0:T(8,128)(2,1)S(1)}, u32[]{:S(2)}, u32[]{:S(2)}) collective-permute-start(bf16[64,1024]{1,0:T(8,128)(2,1)S(1)} %bitcast.72), channel_id=1, source_target_pairs={{0,6},{1,7},{2,4},{3,5},{4,2},{5,3},{6,0},{7,1},{8,14},{9,15},{10,... | collective-permute-start | bytes 393224 | tf_op jit(solution)/shard_map/ppermute | solution.py:192
  13.8 16.4 %collective-permute-start.15 = (bf16[64,1024]{1,0:T(8,128)(2,1)S(1)}, bf16[64,1024]{1,0:T(8,128)(2,1)S(1)}, u32[]{:S(2)}, u32[]{:S(2)}) collective-permute-start(bf16[64,1024]{1,0:T(8,128)(2,1)S(1)} %bitcast.71), channel_id=1, source_target_pairs={{0,4},{1,5},{2,6},{3,7},{4,0},{5,1},{6,2},{7,3},{8,12},{9,13},{10,... | collective-permute-start | bytes 393224 | tf_op jit(solution)/shard_map/ppermute | solution.py:192
  21.5 8.7 %collective-permute-start.14 = (bf16[64,1024]{1,0:T(8,128)(2,1)S(1)}, bf16[64,1024]{1,0:T(8,128)(2,1)S(1)}, u32[]{:S(2)}, u32[]{:S(2)}) collective-permute-start(bf16[64,1024]{1,0:T(8,128)(2,1)S(1)} %bitcast.70), channel_id=1, source_target_pairs={{0,2},{1,3},{2,0},{3,1},{4,6},{5,7},{6,4},{7,5},{8,10},{9,11},{10,... | collective-permute-start | bytes 393224 | tf_op jit(solution)/shard_map/ppermute | solution.py:192
  23.0 2.8 %copy-start = (bf16[4,3,512,512]{3,2,1,0:T(8,128)(2,1)S(1)}, bf16[4,3,512,512]{3,2,1,0:T(8,128)(2,1)}, u32[]{:S(2)}) copy-start(bf16[4,3,512,512]{3,2,1,0:T(8,128)(2,1)} %taps.9) | copy-start | bytes 18874372
  25.8 2.2 %copy-start.1 = (bf16[4,1024,512]{2,1,0:T(8,128)(2,1)S(1)}, bf16[4,1024,512]{2,1,0:T(8,128)(2,1)}, u32[]{:S(2)}) copy-start(bf16[4,1024,512]{2,1,0:T(8,128)(2,1)} %proj.9) | copy-start | bytes 12582916
  28.0 2.2 %copy-start.2 = (bf16[4,512,1024]{2,1,0:T(8,128)(2,1)S(1)}, bf16[4,512,1024]{2,1,0:T(8,128)(2,1)}, u32[]{:S(2)}) copy-start(bf16[4,512,1024]{2,1,0:T(8,128)(2,1)} %output.9) | copy-start | bytes 12582916
  30.2 0.7 copy-start.4
  30.2 0.7 copy-start.5
  30.9 1.6 %copy-start.6 = (bf16[1024,1024]{1,0:T(8,128)(2,1)S(1)}, bf16[1024,1024]{1,0:T(8,128)(2,1)}, u32[]{:S(2)}) copy-start(bf16[1024,1024]{1,0:T(8,128)(2,1)} %param.6) | copy-start | bytes 6291460
  30.9 34.5 %slice-start = ((s8[6291456]{0:T(1024)(128)(4,1)}), s8[4194304]{0:T(1024)(128)(4,1)S(1)}, s32[]{:S(2)}) async-start(s8[6291456]{0:T(1024)(128)(4,1)} %bitcast.52), calls=%async_computation | async-start | bytes 8388608
  32.2 33.3 %slice-start.1 = ((s8[6291456]{0:T(1024)(128)(4,1)}), s8[2097152]{0:T(1024)(128)(4,1)S(1)}, s32[]{:S(2)}) async-start(s8[6291456]{0:T(1024)(128)(4,1)} %bitcast.52), calls=%async_computation.1 | async-start | bytes 4194304
  32.2 33.2 %collective-permute-start.21 = (bf16[512,512]{1,0:T(8,128)(2,1)S(1)}, bf16[512,512]{1,0:T(8,128)(2,1)S(1)}, u32[]{:S(2)}, u32[]{:S(2)}) collective-permute-start(bf16[512,512]{1,0:T(8,128)(2,1)S(1)} %get-tuple-element.40.narrow), channel_id=1, source_target_pairs={{0,1},{1,0},{2,3},{3,2},{4,5},{5,4},{6,7},{7,6},{8,9},{9,8},{10,11... | collective-permute-start | bytes 1572872 | tf_op jit(solution)/shard_map/ppermute | solution.py:195
  32.6 7.9 %collective-permute-start.5 = (bf16[64,1024]{1,0:T(8,128)(2,1)S(1)}, bf16[64,1024]{1,0:T(8,128)(2,1)S(1)}, u32[]{:S(2)}, u32[]{:S(2)}) collective-permute-start(bf16[64,1024]{1,0:T(8,128)(2,1)S(1)} %bitcast.65), channel_id=1, source_target_pairs={{0,12},{1,13},{2,14},{3,15},{4,8},{5,9},{6,10},{7,11},{8,4},{9,5},... | collective-permute-start | bytes 393224 | tf_op jit(solution)/shard_map/ppermute | solution.py:192
  35.9 16.1 %collective-permute-start.6 = (bf16[64,1024]{1,0:T(8,128)(2,1)S(1)}, bf16[64,1024]{1,0:T(8,128)(2,1)S(1)}, u32[]{:S(2)}, u32[]{:S(2)}) collective-permute-start(bf16[64,1024]{1,0:T(8,128)(2,1)S(1)} %bitcast.64), channel_id=1, source_target_pairs={{0,14},{1,15},{2,12},{3,13},{4,10},{5,11},{6,8},{7,9},{8,6},{9,7},... | collective-permute-start | bytes 393224 | tf_op jit(solution)/shard_map/ppermute | solution.py:192
  36.5 20.6 %collective-permute-start.4 = (bf16[64,1024]{1,0:T(8,128)(2,1)S(1)}, bf16[64,1024]{1,0:T(8,128)(2,1)S(1)}, u32[]{:S(2)}, u32[]{:S(2)}) collective-permute-start(bf16[64,1024]{1,0:T(8,128)(2,1)S(1)} %bitcast.63), channel_id=1, source_target_pairs={{0,10},{1,11},{2,8},{3,9},{4,14},{5,15},{6,12},{7,13},{8,2},{9,3},... | collective-permute-start | bytes 393224 | tf_op jit(solution)/shard_map/ppermute | solution.py:192
  40.1 19.8 %collective-permute-start.3 = (bf16[64,1024]{1,0:T(8,128)(2,1)S(1)}, bf16[64,1024]{1,0:T(8,128)(2,1)S(1)}, u32[]{:S(2)}, u32[]{:S(2)}) collective-permute-start(bf16[64,1024]{1,0:T(8,128)(2,1)S(1)} %bitcast.62), channel_id=1, source_target_pairs={{0,8},{1,9},{2,10},{3,11},{4,12},{5,13},{6,14},{7,15},{8,0},{9,1},... | collective-permute-start | bytes 393224 | tf_op jit(solution)/shard_map/ppermute | solution.py:192
  40.6 21.3 %collective-permute-start.2 = (bf16[64,1024]{1,0:T(8,128)(2,1)S(1)}, bf16[64,1024]{1,0:T(8,128)(2,1)S(1)}, u32[]{:S(2)}, u32[]{:S(2)}) collective-permute-start(bf16[64,1024]{1,0:T(8,128)(2,1)S(1)} %bitcast.61), channel_id=1, source_target_pairs={{0,6},{1,7},{2,4},{3,5},{4,2},{5,3},{6,0},{7,1},{8,14},{9,15},{10,... | collective-permute-start | bytes 393224 | tf_op jit(solution)/shard_map/ppermute | solution.py:192
  51.9 12.2 %collective-permute-start.1 = (bf16[64,1024]{1,0:T(8,128)(2,1)S(1)}, bf16[64,1024]{1,0:T(8,128)(2,1)S(1)}, u32[]{:S(2)}, u32[]{:S(2)}) collective-permute-start(bf16[64,1024]{1,0:T(8,128)(2,1)S(1)} %bitcast.60), channel_id=1, source_target_pairs={{0,4},{1,5},{2,6},{3,7},{4,0},{5,1},{6,2},{7,3},{8,12},{9,13},{10,... | collective-permute-start | bytes 393224 | tf_op jit(solution)/shard_map/ppermute | solution.py:192
  57.1 7.0 %collective-permute-start = (bf16[64,1024]{1,0:T(8,128)(2,1)S(1)}, bf16[64,1024]{1,0:T(8,128)(2,1)S(1)}, u32[]{:S(2)}, u32[]{:S(2)}) collective-permute-start(bf16[64,1024]{1,0:T(8,128)(2,1)S(1)} %bitcast.59), channel_id=1, source_target_pairs={{0,2},{1,3},{2,0},{3,1},{4,6},{5,7},{6,4},{7,5},{8,10},{9,11},{10,... | collective-permute-start | bytes 393224 | tf_op jit(solution)/shard_map/ppermute | solution.py:192
  64.1 2.2 %copy-start.3 = (bf16[4,512,1024]{2,1,0:T(8,128)(2,1)S(1)}, bf16[4,512,1024]{2,1,0:T(8,128)(2,1)}, u32[]{:S(2)}) copy-start(bf16[4,512,1024]{2,1,0:T(8,128)(2,1)} %output.9) | copy-start | bytes 12582916
  65.4 3.7 %collective-permute-start.7 = (bf16[512,512]{1,0:T(8,128)(2,1)S(1)}, bf16[512,512]{1,0:T(8,128)(2,1)S(1)}, u32[]{:S(2)}, u32[]{:S(2)}) collective-permute-start(bf16[512,512]{1,0:T(8,128)(2,1)S(1)} %get-tuple-element.30.narrow), channel_id=1, source_target_pairs={{0,1},{1,0},{2,3},{3,2},{4,5},{5,4},{6,7},{7,6},{8,9},{9,8},{10,11... | collective-permute-start | bytes 1572872 | tf_op jit(solution)/shard_map/ppermute | solution.py:195
  69.0 3.3 %collective-permute-start.22 = (bf16[512,512]{1,0:T(8,128)(2,1)S(1)}, bf16[512,512]{1,0:T(8,128)(2,1)S(1)}, u32[]{:S(2)}, u32[]{:S(2)}) collective-permute-start(bf16[512,512]{1,0:T(8,128)(2,1)S(1)} %get-tuple-element.42.narrow), channel_id=1, source_target_pairs={{0,1},{1,0},{2,3},{3,2},{4,5},{5,4},{6,7},{7,6},{8,9},{9,8},{10,11... | collective-permute-start | bytes 1572872 | tf_op jit(solution)/shard_map/ppermute | solution.py:195
  71.7 14.5 %collective-permute-start.8 = (bf16[512,512]{1,0:T(8,128)(2,1)S(1)}, bf16[512,512]{1,0:T(8,128)(2,1)S(1)}, u32[]{:S(2)}, u32[]{:S(2)}) collective-permute-start(bf16[512,512]{1,0:T(8,128)(2,1)S(1)} %get-tuple-element.32.narrow), channel_id=1, source_target_pairs={{0,1},{1,0},{2,3},{3,2},{4,5},{5,4},{6,7},{7,6},{8,9},{9,8},{10,11... | collective-permute-start | bytes 1572872 | tf_op jit(solution)/shard_map/ppermute | solution.py:195
  79.3 15.3 %collective-permute-start.23 = (bf16[64,1024]{1,0:T(8,128)(2,1)S(1)}, bf16[64,1024]{1,0:T(8,128)(2,1)S(1)}, u32[]{:S(2)}, u32[]{:S(2)}) collective-permute-start(bf16[64,1024]{1,0:T(8,128)(2,1)S(1)} %get-tuple-element.44), channel_id=1, source_target_pairs={{0,12},{1,13},{2,14},{3,15},{4,8},{5,9},{6,10},{7,11},{8,4},{9,5},... | collective-permute-start | bytes 393224 | tf_op jit(solution)/shard_map/ppermute | solution.py:192
  82.5 14.1 %collective-permute-start.24 = (bf16[64,1024]{1,0:T(8,128)(2,1)S(1)}, bf16[64,1024]{1,0:T(8,128)(2,1)S(1)}, u32[]{:S(2)}, u32[]{:S(2)}) collective-permute-start(bf16[64,1024]{1,0:T(8,128)(2,1)S(1)} %get-tuple-element.45), channel_id=1, source_target_pairs={{0,14},{1,15},{2,12},{3,13},{4,10},{5,11},{6,8},{7,9},{8,6},{9,7},... | collective-permute-start | bytes 393224 | tf_op jit(solution)/shard_map/ppermute | solution.py:192
  83.9 13.6 %collective-permute-start.25 = (bf16[64,1024]{1,0:T(8,128)(2,1)S(1)}, bf16[64,1024]{1,0:T(8,128)(2,1)S(1)}, u32[]{:S(2)}, u32[]{:S(2)}) collective-permute-start(bf16[64,1024]{1,0:T(8,128)(2,1)S(1)} %get-tuple-element.46), channel_id=1, source_target_pairs={{0,4},{1,5},{2,6},{3,7},{4,0},{5,1},{6,2},{7,3},{8,12},{9,13},{10,... | collective-permute-start | bytes 393224 | tf_op jit(solution)/shard_map/ppermute | solution.py:192
  83.9 16.7 %collective-permute-start.26 = (bf16[64,1024]{1,0:T(8,128)(2,1)S(1)}, bf16[64,1024]{1,0:T(8,128)(2,1)S(1)}, u32[]{:S(2)}, u32[]{:S(2)}) collective-permute-start(bf16[64,1024]{1,0:T(8,128)(2,1)S(1)} %get-tuple-element.47), channel_id=1, source_target_pairs={{0,6},{1,7},{2,4},{3,5},{4,2},{5,3},{6,0},{7,1},{8,14},{9,15},{10,... | collective-permute-start | bytes 393224 | tf_op jit(solution)/shard_map/ppermute | solution.py:192
  86.2 15.9 %collective-permute-start.27 = (bf16[64,1024]{1,0:T(8,128)(2,1)S(1)}, bf16[64,1024]{1,0:T(8,128)(2,1)S(1)}, u32[]{:S(2)}, u32[]{:S(2)}) collective-permute-start(bf16[64,1024]{1,0:T(8,128)(2,1)S(1)} %get-tuple-element.48), channel_id=1, source_target_pairs={{0,8},{1,9},{2,10},{3,11},{4,12},{5,13},{6,14},{7,15},{8,0},{9,1},... | collective-permute-start | bytes 393224 | tf_op jit(solution)/shard_map/ppermute | solution.py:192
  94.7 15.8 %collective-permute-start.28 = (bf16[64,1024]{1,0:T(8,128)(2,1)S(1)}, bf16[64,1024]{1,0:T(8,128)(2,1)S(1)}, u32[]{:S(2)}, u32[]{:S(2)}) collective-permute-start(bf16[64,1024]{1,0:T(8,128)(2,1)S(1)} %get-tuple-element.49), channel_id=1, source_target_pairs={{0,10},{1,11},{2,8},{3,9},{4,14},{5,15},{6,12},{7,13},{8,2},{9,3},... | collective-permute-start | bytes 393224 | tf_op jit(solution)/shard_map/ppermute | solution.py:192
  96.7 13.8 %collective-permute-start.29 = (bf16[64,1024]{1,0:T(8,128)(2,1)S(1)}, bf16[64,1024]{1,0:T(8,128)(2,1)S(1)}, u32[]{:S(2)}, u32[]{:S(2)}) collective-permute-start(bf16[64,1024]{1,0:T(8,128)(2,1)S(1)} %get-tuple-element.50), channel_id=1, source_target_pairs={{0,2},{1,3},{2,0},{3,1},{4,6},{5,7},{6,4},{7,5},{8,10},{9,11},{10,... | collective-permute-start | bytes 393224 | tf_op jit(solution)/shard_map/ppermute | solution.py:192
  97.5 14.3 %collective-permute-start.9 = (bf16[64,1024]{1,0:T(8,128)(2,1)S(1)}, bf16[64,1024]{1,0:T(8,128)(2,1)S(1)}, u32[]{:S(2)}, u32[]{:S(2)}) collective-permute-start(bf16[64,1024]{1,0:T(8,128)(2,1)S(1)} %get-tuple-element.34), channel_id=1, source_target_pairs={{0,12},{1,13},{2,14},{3,15},{4,8},{5,9},{6,10},{7,11},{8,4},{9,5},... | collective-permute-start | bytes 393224 | tf_op jit(solution)/shard_map/ppermute | solution.py:192
  100.6 14.6 %collective-permute-start.10 = (bf16[64,1024]{1,0:T(8,128)(2,1)S(1)}, bf16[64,1024]{1,0:T(8,128)(2,1)S(1)}, u32[]{:S(2)}, u32[]{:S(2)}) collective-permute-start(bf16[64,1024]{1,0:T(8,128)(2,1)S(1)} %get-tuple-element.35), channel_id=1, source_target_pairs={{0,14},{1,15},{2,12},{3,13},{4,10},{5,11},{6,8},{7,9},{8,6},{9,7},... | collective-permute-start | bytes 393224 | tf_op jit(solution)/shard_map/ppermute | solution.py:192
  102.1 21.2 %collective-permute-start.11 = (bf16[64,1024]{1,0:T(8,128)(2,1)S(1)}, bf16[64,1024]{1,0:T(8,128)(2,1)S(1)}, u32[]{:S(2)}, u32[]{:S(2)}) collective-permute-start(bf16[64,1024]{1,0:T(8,128)(2,1)S(1)} %get-tuple-element.36), channel_id=1, source_target_pairs={{0,4},{1,5},{2,6},{3,7},{4,0},{5,1},{6,2},{7,3},{8,12},{9,13},{10,... | collective-permute-start | bytes 393224 | tf_op jit(solution)/shard_map/ppermute | solution.py:192
  110.5 12.8 %collective-permute-start.12 = (bf16[64,1024]{1,0:T(8,128)(2,1)S(1)}, bf16[64,1024]{1,0:T(8,128)(2,1)S(1)}, u32[]{:S(2)}, u32[]{:S(2)}) collective-permute-start(bf16[64,1024]{1,0:T(8,128)(2,1)S(1)} %get-tuple-element.37), channel_id=1, source_target_pairs={{0,6},{1,7},{2,4},{3,5},{4,2},{5,3},{6,0},{7,1},{8,14},{9,15},{10,... | collective-permute-start | bytes 393224 | tf_op jit(solution)/shard_map/ppermute | solution.py:192
  110.5 12.8 %collective-permute-start.13 = (bf16[64,1024]{1,0:T(8,128)(2,1)S(1)}, bf16[64,1024]{1,0:T(8,128)(2,1)S(1)}, u32[]{:S(2)}, u32[]{:S(2)}) collective-permute-start(bf16[64,1024]{1,0:T(8,128)(2,1)S(1)} %get-tuple-element.38), channel_id=1, source_target_pairs={{0,2},{1,3},{2,0},{3,1},{4,6},{5,7},{6,4},{7,5},{8,10},{9,11},{10,... | collective-permute-start | bytes 393224 | tf_op jit(solution)/shard_map/ppermute | solution.py:192
  111.8 12.6 %collective-permute-start.30 = (bf16[64,1024]{1,0:T(8,128)(2,1)S(1)}, bf16[64,1024]{1,0:T(8,128)(2,1)S(1)}, u32[]{:S(2)}, u32[]{:S(2)}) collective-permute-start(bf16[64,1024]{1,0:T(8,128)(2,1)S(1)} %get-tuple-element.51), channel_id=1, source_target_pairs={{0,8},{1,9},{2,10},{3,11},{4,12},{5,13},{6,14},{7,15},{8,0},{9,1},... | collective-permute-start | bytes 393224 | tf_op jit(solution)/shard_map/ppermute | solution.py:192
  115.2 13.0 %collective-permute-start.31 = (bf16[64,1024]{1,0:T(8,128)(2,1)S(1)}, bf16[64,1024]{1,0:T(8,128)(2,1)S(1)}, u32[]{:S(2)}, u32[]{:S(2)}) collective-permute-start(bf16[64,1024]{1,0:T(8,128)(2,1)S(1)} %get-tuple-element.52), channel_id=1, source_target_pairs={{0,10},{1,11},{2,8},{3,9},{4,14},{5,15},{6,12},{7,13},{8,2},{9,3},... | collective-permute-start | bytes 393224 | tf_op jit(solution)/shard_map/ppermute | solution.py:192

commit v7 on v6

--- a/solution.py
+++ b/solution.py
@@ -165,9 +165,14 @@
     return list(range(2, half)), far, list(range(1, min(2, chips)))
 
 
+def arrive_order(chips):
+    near, far, next_to = travel_order(chips)
+    return far[:2] + near + far[2:] + next_to
+
+
 def leave_order(chips):
     near, far, next_to = travel_order(chips)
-    return far[:2] + near + far[2:] + next_to
+    return far + near + next_to
 
 
 def chunk_count(chips):
@@ -248,9 +253,7 @@
     for j in range(chunks):
         pieces = {}
         grid = lax.optimization_barrier(grid)
-        for n, k in enumerate([*leave_order(chips), 0]):
-            if j == 0 and n == 2:
-                grid = lax.optimization_barrier(grid)
+        for k in [*arrive_order(chips), 0]:
             piece = lax.dynamic_slice_in_dim(grid, (chip ^ k) * chunks + j, 1, axis=1).reshape(width, model)
             pieces[k] = to_chip(piece, k) if k else piece
         arrived.append([pieces[k] for k in range(chips)])

time: 129 us -> 127 us (0.984)
  waiting for transfers between devices: 19.5 us -> 16.1 us
  starting transfers between devices: 72.7 us -> 75.1 us
    ppermute x28, waiting for transfers between devices: 19.5 us -> 16.1 us  [to_chip(): lax.ppermute(piece, 'blk', [(i, i ^ k * CORES) for i in range(peers)])]
    ppermute x28, starting transfers between devices: 72 us -> 74.4 us  [to_chip(): lax.ppermute(piece, 'blk', [(i, i ^ k * CORES) for i in range(peers)])]
  transfers between devices with their start and end apart: 32 -> 32, of which waited for: 6 -> 9; matrix products, arithmetic and copies ran while one was open for 2% -> 1% of each run, Pallas kernels for 17% -> 18%
where the time goes in v7:
time: 127 us
  starting transfers between devices  75.1 us (59%)
  Pallas kernels  23.8 us (19%)
  waiting for transfers between devices  16.1 us (13%)
  local copies, waits for them, and re-layouts  11.7 us (9%)
    ppermute x28, starting transfers between devices, to_chip(): lax.ppermute(piece, 'blk', [(i, i ^ k * CORES) for i in range(peers)])  74.4 us
    ppermute x28, waiting for transfers between devices, to_chip(): lax.ppermute(piece, 'blk', [(i, i ^ k * CORES) for i in range(peers)])  16.1 us
    pallas_call x2, Pallas kernels, body(): pieces = rest(x, narrow, partner, *weights)  13.9 us
    unnamed x18, local copies, waits for them, and re-layouts  8.91 us
    pallas_call x2, Pallas kernels, body(): x, narrow = slot_block(x, narrow, partner, *weights)  5.3 us
  transfers between devices with their start and end apart: 32, of which 9 were waited for; matrix products, arithmetic and copies ran while one was open for 1% of the time, Pallas kernels for 18%

profile of v7, /device:TPU:0, one launch (start us, length us, event | category | flops | bytes accessed | tf_op | source)
XLA Modules:
  0.0 127.0 jit_solution(6881786882942113241)
XLA Ops:
  0.0 1.4 %constant_dynamic-slice_fusion = (bf16[2,1,32,1024]{3,2,1,0:T(8,128)(2,1)S(1)}, bf16[2,1,32,1024]{3,2,1,0:T(8,128)(2,1)S(1)}, bf16[2,1,32,1024]{3,2,1,0:T(8,128)...) fusion(bf16[2,16,32,1024]{3,2,1,0:T(8,128)(2,1)} %bitcast.56, ...), kind=kLoop, calls=%fused_computation.2 | loop fusion | bytes 2097184 | tf_op jit(solution)/shard_map/dynamic_slice | solution.py:257
  1.4 5.1 %collective-permute-start.19 = (bf16[64,1024]{1,0:T(8,128)(2,1)S(1)}, bf16[64,1024]{1,0:T(8,128)(2,1)S(1)}, u32[]{:S(2)}, u32[]{:S(2)}) collective-permute-start(bf16[64,1024]{1,0:T(8,128)(2,1)S(1)} %bitcast.70), channel_id=1, source_target_pairs={{0,12},{1,13},{2,14},{3,15},{4,8},{5,9},{6,10},{7,11},{8,4},{9,5},... | collective-permute-start | bytes 393224 | tf_op jit(solution)/shard_map/ppermute | solution.py:197
  6.5 1.2 collective-permute-start.20
  7.7 0.7 collective-permute-start.18
  8.4 2.0 %collective-permute-start.17 = (bf16[64,1024]{1,0:T(8,128)(2,1)S(1)}, bf16[64,1024]{1,0:T(8,128)(2,1)S(1)}, u32[]{:S(2)}, u32[]{:S(2)}) collective-permute-start(bf16[64,1024]{1,0:T(8,128)(2,1)S(1)} %bitcast.61), channel_id=1, source_target_pairs={{0,8},{1,9},{2,10},{3,11},{4,12},{5,13},{6,14},{7,15},{8,0},{9,1},... | collective-permute-start | bytes 393224 | tf_op jit(solution)/shard_map/ppermute | solution.py:197
  10.4 2.3 %collective-permute-start.16 = (bf16[64,1024]{1,0:T(8,128)(2,1)S(1)}, bf16[64,1024]{1,0:T(8,128)(2,1)S(1)}, u32[]{:S(2)}, u32[]{:S(2)}) collective-permute-start(bf16[64,1024]{1,0:T(8,128)(2,1)S(1)} %bitcast.60), channel_id=1, source_target_pairs={{0,6},{1,7},{2,4},{3,5},{4,2},{5,3},{6,0},{7,1},{8,14},{9,15},{10,... | collective-permute-start | bytes 393224 | tf_op jit(solution)/shard_map/ppermute | solution.py:197
  12.8 9.1 %collective-permute-start.15 = (bf16[64,1024]{1,0:T(8,128)(2,1)S(1)}, bf16[64,1024]{1,0:T(8,128)(2,1)S(1)}, u32[]{:S(2)}, u32[]{:S(2)}) collective-permute-start(bf16[64,1024]{1,0:T(8,128)(2,1)S(1)} %bitcast.59), channel_id=1, source_target_pairs={{0,4},{1,5},{2,6},{3,7},{4,0},{5,1},{6,2},{7,3},{8,12},{9,13},{10,... | collective-permute-start | bytes 393224 | tf_op jit(solution)/shard_map/ppermute | solution.py:197
  21.9 1.5 %collective-permute-start.14 = (bf16[64,1024]{1,0:T(8,128)(2,1)S(1)}, bf16[64,1024]{1,0:T(8,128)(2,1)S(1)}, u32[]{:S(2)}, u32[]{:S(2)}) collective-permute-start(bf16[64,1024]{1,0:T(8,128)(2,1)S(1)} %bitcast.58), channel_id=1, source_target_pairs={{0,2},{1,3},{2,0},{3,1},{4,6},{5,7},{6,4},{7,5},{8,10},{9,11},{10,... | collective-permute-start | bytes 393224 | tf_op jit(solution)/shard_map/ppermute | solution.py:197
  23.4 2.8 %copy-done = bf16[4,3,512,512]{3,2,1,0:T(8,128)(2,1)S(1)} copy-done((bf16[4,3,512,512]{3,2,1,0:T(8,128)(2,1)S(1)}, bf16[4,3,512,512]{3,2,1,0:T(8,128)(2,1)}, u32[]{:S(2)}) %copy-start) | copy-done | bytes 6291480
  26.2 2.2 %copy-done.1 = bf16[4,1024,512]{2,1,0:T(8,128)(2,1)S(1)} copy-done((bf16[4,1024,512]{2,1,0:T(8,128)(2,1)S(1)}, bf16[4,1024,512]{2,1,0:T(8,128)(2,1)}, u32[]{:S(2)}) %copy-start.1) | copy-done | bytes 4194328
  28.4 2.2 %copy-done.2 = bf16[4,512,1024]{2,1,0:T(8,128)(2,1)S(1)} copy-done((bf16[4,512,1024]{2,1,0:T(8,128)(2,1)S(1)}, bf16[4,512,1024]{2,1,0:T(8,128)(2,1)}, u32[]{:S(2)}) %copy-start.2) | copy-done | bytes 4194328
  30.7 0.7 copy-done.4
  31.3 1.2 enter.3
  33.0 2.7 %collective-permute-start.5 = (bf16[64,1024]{1,0:T(8,128)(2,1)S(1)}, bf16[64,1024]{1,0:T(8,128)(2,1)S(1)}, u32[]{:S(2)}, u32[]{:S(2)}) collective-permute-start(bf16[64,1024]{1,0:T(8,128)(2,1)S(1)} %bitcast.71), channel_id=1, source_target_pairs={{0,12},{1,13},{2,14},{3,15},{4,8},{5,9},{6,10},{7,11},{8,4},{9,5},... | collective-permute-start | bytes 393224 | tf_op jit(solution)/shard_map/ppermute | solution.py:197
  35.8 1.1 collective-permute-start.6
  36.9 3.1 %collective-permute-start.4 = (bf16[64,1024]{1,0:T(8,128)(2,1)S(1)}, bf16[64,1024]{1,0:T(8,128)(2,1)S(1)}, u32[]{:S(2)}, u32[]{:S(2)}) collective-permute-start(bf16[64,1024]{1,0:T(8,128)(2,1)S(1)} %bitcast.67), channel_id=1, source_target_pairs={{0,10},{1,11},{2,8},{3,9},{4,14},{5,15},{6,12},{7,13},{8,2},{9,3},... | collective-permute-start | bytes 393224 | tf_op jit(solution)/shard_map/ppermute | solution.py:197
  40.0 0.8 collective-permute-start.3
  41.1 11.2 %collective-permute-start.2 = (bf16[64,1024]{1,0:T(8,128)(2,1)S(1)}, bf16[64,1024]{1,0:T(8,128)(2,1)S(1)}, u32[]{:S(2)}, u32[]{:S(2)}) collective-permute-start(bf16[64,1024]{1,0:T(8,128)(2,1)S(1)} %bitcast.65), channel_id=1, source_target_pairs={{0,6},{1,7},{2,4},{3,5},{4,2},{5,3},{6,0},{7,1},{8,14},{9,15},{10,... | collective-permute-start | bytes 393224 | tf_op jit(solution)/shard_map/ppermute | solution.py:197
  52.4 2.8 %collective-permute-start.1 = (bf16[64,1024]{1,0:T(8,128)(2,1)S(1)}, bf16[64,1024]{1,0:T(8,128)(2,1)S(1)}, u32[]{:S(2)}, u32[]{:S(2)}) collective-permute-start(bf16[64,1024]{1,0:T(8,128)(2,1)S(1)} %bitcast.64), channel_id=1, source_target_pairs={{0,4},{1,5},{2,6},{3,7},{4,0},{5,1},{6,2},{7,3},{8,12},{9,13},{10,... | collective-permute-start | bytes 393224 | tf_op jit(solution)/shard_map/ppermute | solution.py:197
  55.2 2.3 %collective-permute-done.4.refs_5_ = bf16[64,1024]{1,0:T(8,128)(2,1)S(1)} collective-permute-done((bf16[64,1024]{1,0:T(8,128)(2,1)S(1)}, bf16[64,1024]{1,0:T(8,128)(2,1)S(1)}, u32[]{:S(2)}, u32[]{:S(2)}) %collective-permute-start.4) | collective-permute-done | bytes 131104 | tf_op jit(solution)/shard_map/ppermute | solution.py:197
  57.5 1.5 %collective-permute-start = (bf16[64,1024]{1,0:T(8,128)(2,1)S(1)}, bf16[64,1024]{1,0:T(8,128)(2,1)S(1)}, u32[]{:S(2)}, u32[]{:S(2)}) collective-permute-start(bf16[64,1024]{1,0:T(8,128)(2,1)S(1)} %bitcast.63), channel_id=1, source_target_pairs={{0,2},{1,3},{2,0},{3,1},{4,6},{5,7},{6,4},{7,5},{8,10},{9,11},{10,... | collective-permute-start | bytes 393224 | tf_op jit(solution)/shard_map/ppermute | solution.py:197
  59.0 1.3 %collective-permute-done.3.refs_4_ = bf16[64,1024]{1,0:T(8,128)(2,1)S(1)} collective-permute-done((bf16[64,1024]{1,0:T(8,128)(2,1)S(1)}, bf16[64,1024]{1,0:T(8,128)(2,1)S(1)}, u32[]{:S(2)}, u32[]{:S(2)}) %collective-permute-start.3) | collective-permute-done | bytes 131104 | tf_op jit(solution)/shard_map/ppermute | solution.py:197
  60.3 2.0 %collective-permute-done.2.refs_3_ = bf16[64,1024]{1,0:T(8,128)(2,1)S(1)} collective-permute-done((bf16[64,1024]{1,0:T(8,128)(2,1)S(1)}, bf16[64,1024]{1,0:T(8,128)(2,1)S(1)}, u32[]{:S(2)}, u32[]{:S(2)}) %collective-permute-start.2) | collective-permute-done | bytes 131104 | tf_op jit(solution)/shard_map/ppermute | solution.py:197
  62.3 2.2 %collective-permute-done.1.refs_2_ = bf16[64,1024]{1,0:T(8,128)(2,1)S(1)} collective-permute-done((bf16[64,1024]{1,0:T(8,128)(2,1)S(1)}, bf16[64,1024]{1,0:T(8,128)(2,1)S(1)}, u32[]{:S(2)}, u32[]{:S(2)}) %collective-permute-start.1) | collective-permute-done | bytes 131104 | tf_op jit(solution)/shard_map/ppermute | solution.py:197
  64.5 1.3 enter.2
  65.9 0.8 copy-done.3
  66.7 2.6 %slot_block.3 = (bf16[512,1024]{1,0:T(8,128)(2,1)S(1)}, bf16[512,512]{1,0:T(8,128)(2,1)S(1)}) custom-call(bf16[512,1024]{1,0:T(8,128)(2,1)S(1)} %get-tuple-element.39.x_in, bf16[512,512]{1,0:T(8,128)(2,1)S(1)} %get-tuple-element.40.narrow, bf16[512,512]{1,0:T(8,128)(2,1)S(1)} %collective-permute-done.21.partner, f32[4,1024]{1,0:T(4,128)S(1)} %copy-done.4, ...), custom_call_target="tpu_custom_call" | custom-call | flops 1879048192 | bytes 7864320 | tf_op jit(solution)/shard_map/slot_block/pallas_call | solution.py:267
  69.4 2.7 %slot_block.2 = (bf16[512,1024]{1,0:T(8,128)(2,1)S(1)}, bf16[512,512]{1,0:T(8,128)(2,1)S(1)}) custom-call(bf16[512,1024]{1,0:T(8,128)(2,1)S(1)} %get-tuple-element.29.x_in, bf16[512,512]{1,0:T(8,128)(2,1)S(1)} %get-tuple-element.30.narrow, bf16[512,512]{1,0:T(8,128)(2,1)S(1)} %collective-permute-done.7.partner, f32[4,1024]{1,0:T(4,128)S(1)} %copy-done.4, ...), custom_call_target="tpu_custom_call" | custom-call | flops 1879048192 | bytes 7864320 | tf_op jit(solution)/shard_map/slot_block/pallas_call | solution.py:267
  72.1 0.6 collective-permute-start.8
  72.7 7.1 %rest.3 = (bf16[64,1024]{1,0:T(8,128)(2,1)S(1)}, bf16[64,1024]{1,0:T(8,128)(2,1)S(1)}, bf16[64,1024]{1,0:T(8,128)(2,1)S(1)}, bf16[64,1024]{1,0:T(8,128)(2,1)S(1)...) custom-call(bf16[512,1024]{1,0:T(8,128)(2,1)S(1)} %get-tuple-element, ...), custom_call_target="tpu_custom_call" | custom-call | flops 5637144576 | bytes 15204352 | tf_op jit(solution)/shard_map/rest/pallas_call | solution.py:269
  79.7 2.7 %collective-permute-start.23 = (bf16[64,1024]{1,0:T(8,128)(2,1)S(1)}, bf16[64,1024]{1,0:T(8,128)(2,1)S(1)}, u32[]{:S(2)}, u32[]{:S(2)}) collective-permute-start(bf16[64,1024]{1,0:T(8,128)(2,1)S(1)} %get-tuple-element.44), channel_id=1, source_target_pairs={{0,12},{1,13},{2,14},{3,15},{4,8},{5,9},{6,10},{7,11},{8,4},{9,5},... | collective-permute-start | bytes 393224 | tf_op jit(solution)/shard_map/ppermute | solution.py:197
  82.4 1.8 %collective-permute-start.24 = (bf16[64,1024]{1,0:T(8,128)(2,1)S(1)}, bf16[64,1024]{1,0:T(8,128)(2,1)S(1)}, u32[]{:S(2)}, u32[]{:S(2)}) collective-permute-start(bf16[64,1024]{1,0:T(8,128)(2,1)S(1)} %get-tuple-element.45), channel_id=1, source_target_pairs={{0,14},{1,15},{2,12},{3,13},{4,10},{5,11},{6,8},{7,9},{8,6},{9,7},... | collective-permute-start | bytes 393224 | tf_op jit(solution)/shard_map/ppermute | solution.py:197
  84.3 3.2 %collective-permute-start.26 = (bf16[64,1024]{1,0:T(8,128)(2,1)S(1)}, bf16[64,1024]{1,0:T(8,128)(2,1)S(1)}, u32[]{:S(2)}, u32[]{:S(2)}) collective-permute-start(bf16[64,1024]{1,0:T(8,128)(2,1)S(1)} %get-tuple-element.47), channel_id=1, source_target_pairs={{0,10},{1,11},{2,8},{3,9},{4,14},{5,15},{6,12},{7,13},{8,2},{9,3},... | collective-permute-start | bytes 393224 | tf_op jit(solution)/shard_map/ppermute | solution.py:197
  87.7 6.8 %rest.2 = (bf16[64,1024]{1,0:T(8,128)(2,1)S(1)}, bf16[64,1024]{1,0:T(8,128)(2,1)S(1)}, bf16[64,1024]{1,0:T(8,128)(2,1)S(1)}, bf16[64,1024]{1,0:T(8,128)(2,1)S(1)...) custom-call(bf16[512,1024]{1,0:T(8,128)(2,1)S(1)} %get-tuple-element, ...), custom_call_target="tpu_custom_call" | custom-call | flops 5637144576 | bytes 15204352 | tf_op jit(solution)/shard_map/rest/pallas_call | solution.py:269
  94.6 2.5 %collective-permute-start.28 = (bf16[64,1024]{1,0:T(8,128)(2,1)S(1)}, bf16[64,1024]{1,0:T(8,128)(2,1)S(1)}, u32[]{:S(2)}, u32[]{:S(2)}) collective-permute-start(bf16[64,1024]{1,0:T(8,128)(2,1)S(1)} %get-tuple-element.49), channel_id=1, source_target_pairs={{0,6},{1,7},{2,4},{3,5},{4,2},{5,3},{6,0},{7,1},{8,14},{9,15},{10,... | collective-permute-start | bytes 393224 | tf_op jit(solution)/shard_map/ppermute | solution.py:197
  97.1 0.8 collective-permute-start.29
  97.9 4.2 %collective-permute-done.25.refs_3_ = bf16[64,1024]{1,0:T(8,128)(2,1)S(1)} collective-permute-done((bf16[64,1024]{1,0:T(8,128)(2,1)S(1)}, bf16[64,1024]{1,0:T(8,128)(2,1)S(1)}, u32[]{:S(2)}, u32[]{:S(2)}) %collective-permute-start.25) | collective-permute-done | bytes 131104 | tf_op jit(solution)/shard_map/ppermute | solution.py:197
  102.1 2.7 %collective-permute-start.9 = (bf16[64,1024]{1,0:T(8,128)(2,1)S(1)}, bf16[64,1024]{1,0:T(8,128)(2,1)S(1)}, u32[]{:S(2)}, u32[]{:S(2)}) collective-permute-start(bf16[64,1024]{1,0:T(8,128)(2,1)S(1)} %get-tuple-element.34), channel_id=1, source_target_pairs={{0,12},{1,13},{2,14},{3,15},{4,8},{5,9},{6,10},{7,11},{8,4},{9,5},... | collective-permute-start | bytes 393224 | tf_op jit(solution)/shard_map/ppermute | solution.py:197
  104.7 5.1 %collective-permute-start.10 = (bf16[64,1024]{1,0:T(8,128)(2,1)S(1)}, bf16[64,1024]{1,0:T(8,128)(2,1)S(1)}, u32[]{:S(2)}, u32[]{:S(2)}) collective-permute-start(bf16[64,1024]{1,0:T(8,128)(2,1)S(1)} %get-tuple-element.35), channel_id=1, source_target_pairs={{0,14},{1,15},{2,12},{3,13},{4,10},{5,11},{6,8},{7,9},{8,6},{9,7},... | collective-permute-start | bytes 393224 | tf_op jit(solution)/shard_map/ppermute | solution.py:197
  109.8 2.0 %collective-permute-start.12 = (bf16[64,1024]{1,0:T(8,128)(2,1)S(1)}, bf16[64,1024]{1,0:T(8,128)(2,1)S(1)}, u32[]{:S(2)}, u32[]{:S(2)}) collective-permute-start(bf16[64,1024]{1,0:T(8,128)(2,1)S(1)} %get-tuple-element.37), channel_id=1, source_target_pairs={{0,6},{1,7},{2,4},{3,5},{4,2},{5,3},{6,0},{7,1},{8,14},{9,15},{10,... | collective-permute-start | bytes 393224 | tf_op jit(solution)/shard_map/ppermute | solution.py:197
  111.8 1.5 %collective-permute-start.13 = (bf16[64,1024]{1,0:T(8,128)(2,1)S(1)}, bf16[64,1024]{1,0:T(8,128)(2,1)S(1)}, u32[]{:S(2)}, u32[]{:S(2)}) collective-permute-start(bf16[64,1024]{1,0:T(8,128)(2,1)S(1)} %get-tuple-element.38), channel_id=1, source_target_pairs={{0,2},{1,3},{2,0},{3,1},{4,6},{5,7},{6,4},{7,5},{8,10},{9,11},{10,... | collective-permute-start | bytes 393224 | tf_op jit(solution)/shard_map/ppermute | solution.py:197
  114.1 6.3 %collective-permute-start.31 = (bf16[64,1024]{1,0:T(8,128)(2,1)S(1)}, bf16[64,1024]{1,0:T(8,128)(2,1)S(1)}, u32[]{:S(2)}, u32[]{:S(2)}) collective-permute-start(bf16[64,1024]{1,0:T(8,128)(2,1)S(1)} %get-tuple-element.52), channel_id=1, source_target_pairs={{0,10},{1,11},{2,8},{3,9},{4,14},{5,15},{6,12},{7,13},{8,2},{9,3},... | collective-permute-start | bytes 393224 | tf_op jit(solution)/shard_map/ppermute | solution.py:197
  120.4 1.1 collect.2.refs_6_
  121.5 1.0 collect.3
  122.5 2.3 %collective-permute-done.30 = bf16[64,1024]{1,0:T(8,128)(2,1)S(1)} collective-permute-done((bf16[64,1024]{1,0:T(8,128)(2,1)S(1)}, bf16[64,1024]{1,0:T(8,128)(2,1)S(1)}, u32[]{:S(2)}, u32[]{:S(2)}) %collective-permute-start.30) | collective-permute-done | bytes 131104 | tf_op jit(solution)/shard_map/ppermute | solution.py:197
  124.8 0.7 constant_dynamic-update-slice_fusion.1
  125.5 0.9 collective-permute-done.31
  126.3 0.7 constant_dynamic-update-slice_fusion
  (48 shorter events, 2.2 us)
Async XLA Ops:
  1.4 11.4 %collective-permute-start.19 = (bf16[64,1024]{1,0:T(8,128)(2,1)S(1)}, bf16[64,1024]{1,0:T(8,128)(2,1)S(1)}, u32[]{:S(2)}, u32[]{:S(2)}) collective-permute-start(bf16[64,1024]{1,0:T(8,128)(2,1)S(1)} %bitcast.70), channel_id=1, source_target_pairs={{0,12},{1,13},{2,14},{3,15},{4,8},{5,9},{6,10},{7,11},{8,4},{9,5},... | collective-permute-start | bytes 393224 | tf_op jit(solution)/shard_map/ppermute | solution.py:197
  6.5 15.4 %collective-permute-start.20 = (bf16[64,1024]{1,0:T(8,128)(2,1)S(1)}, bf16[64,1024]{1,0:T(8,128)(2,1)S(1)}, u32[]{:S(2)}, u32[]{:S(2)}) collective-permute-start(bf16[64,1024]{1,0:T(8,128)(2,1)S(1)} %bitcast.68), channel_id=1, source_target_pairs={{0,14},{1,15},{2,12},{3,13},{4,10},{5,11},{6,8},{7,9},{8,6},{9,7},... | collective-permute-start | bytes 393224 | tf_op jit(solution)/shard_map/ppermute | solution.py:197
  7.7 22.9 %collective-permute-start.18 = (bf16[64,1024]{1,0:T(8,128)(2,1)S(1)}, bf16[64,1024]{1,0:T(8,128)(2,1)S(1)}, u32[]{:S(2)}, u32[]{:S(2)}) collective-permute-start(bf16[64,1024]{1,0:T(8,128)(2,1)S(1)} %bitcast.62), channel_id=1, source_target_pairs={{0,10},{1,11},{2,8},{3,9},{4,14},{5,15},{6,12},{7,13},{8,2},{9,3},... | collective-permute-start | bytes 393224 | tf_op jit(solution)/shard_map/ppermute | solution.py:197
  8.4 22.2 %collective-permute-start.17 = (bf16[64,1024]{1,0:T(8,128)(2,1)S(1)}, bf16[64,1024]{1,0:T(8,128)(2,1)S(1)}, u32[]{:S(2)}, u32[]{:S(2)}) collective-permute-start(bf16[64,1024]{1,0:T(8,128)(2,1)S(1)} %bitcast.61), channel_id=1, source_target_pairs={{0,8},{1,9},{2,10},{3,11},{4,12},{5,13},{6,14},{7,15},{8,0},{9,1},... | collective-permute-start | bytes 393224 | tf_op jit(solution)/shard_map/ppermute | solution.py:197
  10.4 20.2 %collective-permute-start.16 = (bf16[64,1024]{1,0:T(8,128)(2,1)S(1)}, bf16[64,1024]{1,0:T(8,128)(2,1)S(1)}, u32[]{:S(2)}, u32[]{:S(2)}) collective-permute-start(bf16[64,1024]{1,0:T(8,128)(2,1)S(1)} %bitcast.60), channel_id=1, source_target_pairs={{0,6},{1,7},{2,4},{3,5},{4,2},{5,3},{6,0},{7,1},{8,14},{9,15},{10,... | collective-permute-start | bytes 393224 | tf_op jit(solution)/shard_map/ppermute | solution.py:197
  12.8 17.9 %collective-permute-start.15 = (bf16[64,1024]{1,0:T(8,128)(2,1)S(1)}, bf16[64,1024]{1,0:T(8,128)(2,1)S(1)}, u32[]{:S(2)}, u32[]{:S(2)}) collective-permute-start(bf16[64,1024]{1,0:T(8,128)(2,1)S(1)} %bitcast.59), channel_id=1, source_target_pairs={{0,4},{1,5},{2,6},{3,7},{4,0},{5,1},{6,2},{7,3},{8,12},{9,13},{10,... | collective-permute-start | bytes 393224 | tf_op jit(solution)/shard_map/ppermute | solution.py:197
  21.9 8.7 %collective-permute-start.14 = (bf16[64,1024]{1,0:T(8,128)(2,1)S(1)}, bf16[64,1024]{1,0:T(8,128)(2,1)S(1)}, u32[]{:S(2)}, u32[]{:S(2)}) collective-permute-start(bf16[64,1024]{1,0:T(8,128)(2,1)S(1)} %bitcast.58), channel_id=1, source_target_pairs={{0,2},{1,3},{2,0},{3,1},{4,6},{5,7},{6,4},{7,5},{8,10},{9,11},{10,... | collective-permute-start | bytes 393224 | tf_op jit(solution)/shard_map/ppermute | solution.py:197
  23.4 2.8 %copy-start = (bf16[4,3,512,512]{3,2,1,0:T(8,128)(2,1)S(1)}, bf16[4,3,512,512]{3,2,1,0:T(8,128)(2,1)}, u32[]{:S(2)}) copy-start(bf16[4,3,512,512]{3,2,1,0:T(8,128)(2,1)} %taps.9) | copy-start | bytes 18874372
  26.2 2.2 %copy-start.1 = (bf16[4,1024,512]{2,1,0:T(8,128)(2,1)S(1)}, bf16[4,1024,512]{2,1,0:T(8,128)(2,1)}, u32[]{:S(2)}) copy-start(bf16[4,1024,512]{2,1,0:T(8,128)(2,1)} %proj.9) | copy-start | bytes 12582916
  28.4 2.2 %copy-start.2 = (bf16[4,512,1024]{2,1,0:T(8,128)(2,1)S(1)}, bf16[4,512,1024]{2,1,0:T(8,128)(2,1)}, u32[]{:S(2)}) copy-start(bf16[4,512,1024]{2,1,0:T(8,128)(2,1)} %output.9) | copy-start | bytes 12582916
  30.6 0.7 copy-start.4
  30.6 0.7 copy-start.5
  31.3 1.6 %copy-start.6 = (bf16[1024,1024]{1,0:T(8,128)(2,1)S(1)}, bf16[1024,1024]{1,0:T(8,128)(2,1)}, u32[]{:S(2)}) copy-start(bf16[1024,1024]{1,0:T(8,128)(2,1)} %param.6) | copy-start | bytes 6291460
  31.3 34.5 %slice-start = ((s8[6291456]{0:T(1024)(128)(4,1)}), s8[4194304]{0:T(1024)(128)(4,1)S(1)}, s32[]{:S(2)}) async-start(s8[6291456]{0:T(1024)(128)(4,1)} %bitcast.52), calls=%async_computation | async-start | bytes 8388608
  32.6 33.3 %slice-start.1 = ((s8[6291456]{0:T(1024)(128)(4,1)}), s8[2097152]{0:T(1024)(128)(4,1)S(1)}, s32[]{:S(2)}) async-start(s8[6291456]{0:T(1024)(128)(4,1)} %bitcast.52), calls=%async_computation.1 | async-start | bytes 4194304
  32.6 33.2 %collective-permute-start.21 = (bf16[512,512]{1,0:T(8,128)(2,1)S(1)}, bf16[512,512]{1,0:T(8,128)(2,1)S(1)}, u32[]{:S(2)}, u32[]{:S(2)}) collective-permute-start(bf16[512,512]{1,0:T(8,128)(2,1)S(1)} %get-tuple-element.40.narrow), channel_id=1, source_target_pairs={{0,1},{1,0},{2,3},{3,2},{4,5},{5,4},{6,7},{7,6},{8,9},{9,8},{10,11... | collective-permute-start | bytes 1572872 | tf_op jit(solution)/shard_map/ppermute | solution.py:200
  33.0 8.1 %collective-permute-start.5 = (bf16[64,1024]{1,0:T(8,128)(2,1)S(1)}, bf16[64,1024]{1,0:T(8,128)(2,1)S(1)}, u32[]{:S(2)}, u32[]{:S(2)}) collective-permute-start(bf16[64,1024]{1,0:T(8,128)(2,1)S(1)} %bitcast.71), channel_id=1, source_target_pairs={{0,12},{1,13},{2,14},{3,15},{4,8},{5,9},{6,10},{7,11},{8,4},{9,5},... | collective-permute-start | bytes 393224 | tf_op jit(solution)/shard_map/ppermute | solution.py:197
  35.8 16.6 %collective-permute-start.6 = (bf16[64,1024]{1,0:T(8,128)(2,1)S(1)}, bf16[64,1024]{1,0:T(8,128)(2,1)S(1)}, u32[]{:S(2)}, u32[]{:S(2)}) collective-permute-start(bf16[64,1024]{1,0:T(8,128)(2,1)S(1)} %bitcast.69), channel_id=1, source_target_pairs={{0,14},{1,15},{2,12},{3,13},{4,10},{5,11},{6,8},{7,9},{8,6},{9,7},... | collective-permute-start | bytes 393224 | tf_op jit(solution)/shard_map/ppermute | solution.py:197
  36.9 20.6 %collective-permute-start.4 = (bf16[64,1024]{1,0:T(8,128)(2,1)S(1)}, bf16[64,1024]{1,0:T(8,128)(2,1)S(1)}, u32[]{:S(2)}, u32[]{:S(2)}) collective-permute-start(bf16[64,1024]{1,0:T(8,128)(2,1)S(1)} %bitcast.67), channel_id=1, source_target_pairs={{0,10},{1,11},{2,8},{3,9},{4,14},{5,15},{6,12},{7,13},{8,2},{9,3},... | collective-permute-start | bytes 393224 | tf_op jit(solution)/shard_map/ppermute | solution.py:197
  40.0 20.3 %collective-permute-start.3 = (bf16[64,1024]{1,0:T(8,128)(2,1)S(1)}, bf16[64,1024]{1,0:T(8,128)(2,1)S(1)}, u32[]{:S(2)}, u32[]{:S(2)}) collective-permute-start(bf16[64,1024]{1,0:T(8,128)(2,1)S(1)} %bitcast.66), channel_id=1, source_target_pairs={{0,8},{1,9},{2,10},{3,11},{4,12},{5,13},{6,14},{7,15},{8,0},{9,1},... | collective-permute-start | bytes 393224 | tf_op jit(solution)/shard_map/ppermute | solution.py:197
  41.1 21.2 %collective-permute-start.2 = (bf16[64,1024]{1,0:T(8,128)(2,1)S(1)}, bf16[64,1024]{1,0:T(8,128)(2,1)S(1)}, u32[]{:S(2)}, u32[]{:S(2)}) collective-permute-start(bf16[64,1024]{1,0:T(8,128)(2,1)S(1)} %bitcast.65), channel_id=1, source_target_pairs={{0,6},{1,7},{2,4},{3,5},{4,2},{5,3},{6,0},{7,1},{8,14},{9,15},{10,... | collective-permute-start | bytes 393224 | tf_op jit(solution)/shard_map/ppermute | solution.py:197
  52.4 12.1 %collective-permute-start.1 = (bf16[64,1024]{1,0:T(8,128)(2,1)S(1)}, bf16[64,1024]{1,0:T(8,128)(2,1)S(1)}, u32[]{:S(2)}, u32[]{:S(2)}) collective-permute-start(bf16[64,1024]{1,0:T(8,128)(2,1)S(1)} %bitcast.64), channel_id=1, source_target_pairs={{0,4},{1,5},{2,6},{3,7},{4,0},{5,1},{6,2},{7,3},{8,12},{9,13},{10,... | collective-permute-start | bytes 393224 | tf_op jit(solution)/shard_map/ppermute | solution.py:197
  57.5 7.0 %collective-permute-start = (bf16[64,1024]{1,0:T(8,128)(2,1)S(1)}, bf16[64,1024]{1,0:T(8,128)(2,1)S(1)}, u32[]{:S(2)}, u32[]{:S(2)}) collective-permute-start(bf16[64,1024]{1,0:T(8,128)(2,1)S(1)} %bitcast.63), channel_id=1, source_target_pairs={{0,2},{1,3},{2,0},{3,1},{4,6},{5,7},{6,4},{7,5},{8,10},{9,11},{10,... | collective-permute-start | bytes 393224 | tf_op jit(solution)/shard_map/ppermute | solution.py:197
  64.5 2.2 %copy-start.3 = (bf16[4,512,1024]{2,1,0:T(8,128)(2,1)S(1)}, bf16[4,512,1024]{2,1,0:T(8,128)(2,1)}, u32[]{:S(2)}) copy-start(bf16[4,512,1024]{2,1,0:T(8,128)(2,1)} %output.9) | copy-start | bytes 12582916
  65.8 3.7 %collective-permute-start.7 = (bf16[512,512]{1,0:T(8,128)(2,1)S(1)}, bf16[512,512]{1,0:T(8,128)(2,1)S(1)}, u32[]{:S(2)}, u32[]{:S(2)}) collective-permute-start(bf16[512,512]{1,0:T(8,128)(2,1)S(1)} %get-tuple-element.30.narrow), channel_id=1, source_target_pairs={{0,1},{1,0},{2,3},{3,2},{4,5},{5,4},{6,7},{7,6},{8,9},{9,8},{10,11... | collective-permute-start | bytes 1572872 | tf_op jit(solution)/shard_map/ppermute | solution.py:200
  69.3 3.3 %collective-permute-start.22 = (bf16[512,512]{1,0:T(8,128)(2,1)S(1)}, bf16[512,512]{1,0:T(8,128)(2,1)S(1)}, u32[]{:S(2)}, u32[]{:S(2)}) collective-permute-start(bf16[512,512]{1,0:T(8,128)(2,1)S(1)} %get-tuple-element.42.narrow), channel_id=1, source_target_pairs={{0,1},{1,0},{2,3},{3,2},{4,5},{5,4},{6,7},{7,6},{8,9},{9,8},{10,11... | collective-permute-start | bytes 1572872 | tf_op jit(solution)/shard_map/ppermute | solution.py:200
  72.1 15.3 %collective-permute-start.8 = (bf16[512,512]{1,0:T(8,128)(2,1)S(1)}, bf16[512,512]{1,0:T(8,128)(2,1)S(1)}, u32[]{:S(2)}, u32[]{:S(2)}) collective-permute-start(bf16[512,512]{1,0:T(8,128)(2,1)S(1)} %get-tuple-element.32.narrow), channel_id=1, source_target_pairs={{0,1},{1,0},{2,3},{3,2},{4,5},{5,4},{6,7},{7,6},{8,9},{9,8},{10,11... | collective-permute-start | bytes 1572872 | tf_op jit(solution)/shard_map/ppermute | solution.py:200
  79.7 14.9 %collective-permute-start.23 = (bf16[64,1024]{1,0:T(8,128)(2,1)S(1)}, bf16[64,1024]{1,0:T(8,128)(2,1)S(1)}, u32[]{:S(2)}, u32[]{:S(2)}) collective-permute-start(bf16[64,1024]{1,0:T(8,128)(2,1)S(1)} %get-tuple-element.44), channel_id=1, source_target_pairs={{0,12},{1,13},{2,14},{3,15},{4,8},{5,9},{6,10},{7,11},{8,4},{9,5},... | collective-permute-start | bytes 393224 | tf_op jit(solution)/shard_map/ppermute | solution.py:197
  82.4 14.6 %collective-permute-start.24 = (bf16[64,1024]{1,0:T(8,128)(2,1)S(1)}, bf16[64,1024]{1,0:T(8,128)(2,1)S(1)}, u32[]{:S(2)}, u32[]{:S(2)}) collective-permute-start(bf16[64,1024]{1,0:T(8,128)(2,1)S(1)} %get-tuple-element.45), channel_id=1, source_target_pairs={{0,14},{1,15},{2,12},{3,13},{4,10},{5,11},{6,8},{7,9},{8,6},{9,7},... | collective-permute-start | bytes 393224 | tf_op jit(solution)/shard_map/ppermute | solution.py:197
  84.3 17.8 %collective-permute-start.25 = (bf16[64,1024]{1,0:T(8,128)(2,1)S(1)}, bf16[64,1024]{1,0:T(8,128)(2,1)S(1)}, u32[]{:S(2)}, u32[]{:S(2)}) collective-permute-start(bf16[64,1024]{1,0:T(8,128)(2,1)S(1)} %get-tuple-element.46), channel_id=1, source_target_pairs={{0,8},{1,9},{2,10},{3,11},{4,12},{5,13},{6,14},{7,15},{8,0},{9,1},... | collective-permute-start | bytes 393224 | tf_op jit(solution)/shard_map/ppermute | solution.py:197
  84.3 20.5 %collective-permute-start.26 = (bf16[64,1024]{1,0:T(8,128)(2,1)S(1)}, bf16[64,1024]{1,0:T(8,128)(2,1)S(1)}, u32[]{:S(2)}, u32[]{:S(2)}) collective-permute-start(bf16[64,1024]{1,0:T(8,128)(2,1)S(1)} %get-tuple-element.47), channel_id=1, source_target_pairs={{0,10},{1,11},{2,8},{3,9},{4,14},{5,15},{6,12},{7,13},{8,2},{9,3},... | collective-permute-start | bytes 393224 | tf_op jit(solution)/shard_map/ppermute | solution.py:197
  87.4 22.4 %collective-permute-start.27 = (bf16[64,1024]{1,0:T(8,128)(2,1)S(1)}, bf16[64,1024]{1,0:T(8,128)(2,1)S(1)}, u32[]{:S(2)}, u32[]{:S(2)}) collective-permute-start(bf16[64,1024]{1,0:T(8,128)(2,1)S(1)} %get-tuple-element.48), channel_id=1, source_target_pairs={{0,4},{1,5},{2,6},{3,7},{4,0},{5,1},{6,2},{7,3},{8,12},{9,13},{10,... | collective-permute-start | bytes 393224 | tf_op jit(solution)/shard_map/ppermute | solution.py:197
  94.6 15.2 %collective-permute-start.28 = (bf16[64,1024]{1,0:T(8,128)(2,1)S(1)}, bf16[64,1024]{1,0:T(8,128)(2,1)S(1)}, u32[]{:S(2)}, u32[]{:S(2)}) collective-permute-start(bf16[64,1024]{1,0:T(8,128)(2,1)S(1)} %get-tuple-element.49), channel_id=1, source_target_pairs={{0,6},{1,7},{2,4},{3,5},{4,2},{5,3},{6,0},{7,1},{8,14},{9,15},{10,... | collective-permute-start | bytes 393224 | tf_op jit(solution)/shard_map/ppermute | solution.py:197
  97.1 14.7 %collective-permute-start.29 = (bf16[64,1024]{1,0:T(8,128)(2,1)S(1)}, bf16[64,1024]{1,0:T(8,128)(2,1)S(1)}, u32[]{:S(2)}, u32[]{:S(2)}) collective-permute-start(bf16[64,1024]{1,0:T(8,128)(2,1)S(1)} %get-tuple-element.50), channel_id=1, source_target_pairs={{0,2},{1,3},{2,0},{3,1},{4,6},{5,7},{6,4},{7,5},{8,10},{9,11},{10,... | collective-permute-start | bytes 393224 | tf_op jit(solution)/shard_map/ppermute | solution.py:197
  102.1 11.2 %collective-permute-start.9 = (bf16[64,1024]{1,0:T(8,128)(2,1)S(1)}, bf16[64,1024]{1,0:T(8,128)(2,1)S(1)}, u32[]{:S(2)}, u32[]{:S(2)}) collective-permute-start(bf16[64,1024]{1,0:T(8,128)(2,1)S(1)} %get-tuple-element.34), channel_id=1, source_target_pairs={{0,12},{1,13},{2,14},{3,15},{4,8},{5,9},{6,10},{7,11},{8,4},{9,5},... | collective-permute-start | bytes 393224 | tf_op jit(solution)/shard_map/ppermute | solution.py:197
  104.7 9.4 %collective-permute-start.10 = (bf16[64,1024]{1,0:T(8,128)(2,1)S(1)}, bf16[64,1024]{1,0:T(8,128)(2,1)S(1)}, u32[]{:S(2)}, u32[]{:S(2)}) collective-permute-start(bf16[64,1024]{1,0:T(8,128)(2,1)S(1)} %get-tuple-element.35), channel_id=1, source_target_pairs={{0,14},{1,15},{2,12},{3,13},{4,10},{5,11},{6,8},{7,9},{8,6},{9,7},... | collective-permute-start | bytes 393224 | tf_op jit(solution)/shard_map/ppermute | solution.py:197
  109.8 11.7 %collective-permute-start.11 = (bf16[64,1024]{1,0:T(8,128)(2,1)S(1)}, bf16[64,1024]{1,0:T(8,128)(2,1)S(1)}, u32[]{:S(2)}, u32[]{:S(2)}) collective-permute-start(bf16[64,1024]{1,0:T(8,128)(2,1)S(1)} %get-tuple-element.36), channel_id=1, source_target_pairs={{0,4},{1,5},{2,6},{3,7},{4,0},{5,1},{6,2},{7,3},{8,12},{9,13},{10,... | collective-permute-start | bytes 393224 | tf_op jit(solution)/shard_map/ppermute | solution.py:197
  109.8 11.7 %collective-permute-start.12 = (bf16[64,1024]{1,0:T(8,128)(2,1)S(1)}, bf16[64,1024]{1,0:T(8,128)(2,1)S(1)}, u32[]{:S(2)}, u32[]{:S(2)}) collective-permute-start(bf16[64,1024]{1,0:T(8,128)(2,1)S(1)} %get-tuple-element.37), channel_id=1, source_target_pairs={{0,6},{1,7},{2,4},{3,5},{4,2},{5,3},{6,0},{7,1},{8,14},{9,15},{10,... | collective-permute-start | bytes 393224 | tf_op jit(solution)/shard_map/ppermute | solution.py:197
  111.8 9.7 %collective-permute-start.13 = (bf16[64,1024]{1,0:T(8,128)(2,1)S(1)}, bf16[64,1024]{1,0:T(8,128)(2,1)S(1)}, u32[]{:S(2)}, u32[]{:S(2)}) collective-permute-start(bf16[64,1024]{1,0:T(8,128)(2,1)S(1)} %get-tuple-element.38), channel_id=1, source_target_pairs={{0,2},{1,3},{2,0},{3,1},{4,6},{5,7},{6,4},{7,5},{8,10},{9,11},{10,... | collective-permute-start | bytes 393224 | tf_op jit(solution)/shard_map/ppermute | solution.py:197
  113.3 11.5 %collective-permute-start.30 = (bf16[64,1024]{1,0:T(8,128)(2,1)S(1)}, bf16[64,1024]{1,0:T(8,128)(2,1)S(1)}, u32[]{:S(2)}, u32[]{:S(2)}) collective-permute-start(bf16[64,1024]{1,0:T(8,128)(2,1)S(1)} %get-tuple-element.51), channel_id=1, source_target_pairs={{0,8},{1,9},{2,10},{3,11},{4,12},{5,13},{6,14},{7,15},{8,0},{9,1},... | collective-permute-start | bytes 393224 | tf_op jit(solution)/shard_map/ppermute | solution.py:197
  114.1 12.2 %collective-permute-start.31 = (bf16[64,1024]{1,0:T(8,128)(2,1)S(1)}, bf16[64,1024]{1,0:T(8,128)(2,1)S(1)}, u32[]{:S(2)}, u32[]{:S(2)}) collective-permute-start(bf16[64,1024]{1,0:T(8,128)(2,1)S(1)} %get-tuple-element.52), channel_id=1, source_target_pairs={{0,10},{1,11},{2,8},{3,9},{4,14},{5,15},{6,12},{7,13},{8,2},{9,3},... | collective-permute-start | bytes 393224 | tf_op jit(solution)/shard_map/ppermute | solution.py:197
